TPU v7x, 32 devices: a whole 2x2x4 slice. The times are simulated.
32 devices in a mesh: dp: 8 (over y, x, core), head: 4 (over z).
Axes of the slice: x: 2, y: 2, z: 4, core: 2. Of those that a mesh axis runs over, the one named last changes fastest.
Arguments:
- series: float32 [512, 512], P(('dp', 'head')), may hold values from -15 to 15
- observed: int32 [512, 512], P(('dp', 'head')), may hold values from 0 to 1, as said below
- item_split: int32 [512], P('dp'), may hold values 0 or 1
- recon_cot: float32 [512, 512], P(('dp', 'head')), may hold values from -6 to 6
- gain_attn: bfloat16 [512], replicated, may hold values from 0.099609375 to 1.8984375
- gain_ff: bfloat16 [512], replicated, may hold values from 0.099609375 to 1.8984375
- gain_final: bfloat16 [512], replicated, may hold values from 0.099609375 to 1.8984375
- patch_weight: bfloat16 [8, 512], replicated, may hold values from -2 to 2
- patch_bias: bfloat16 [512], replicated, may hold values from -4 to 4
- query_weight: bfloat16 [512, 512], P(None, 'head'), may hold values from -0.125 to 0.125
- key_weight: bfloat16 [512, 512], P(None, 'head'), may hold values from -0.125 to 0.125
- value_weight: bfloat16 [512, 512], P(None, 'head'), may hold values from -0.25 to 0.25
- out_weight: bfloat16 [512, 512], P('head'), may hold values from -0.75 to 0.75
- bias_table: bfloat16 [32, 8], P(None, 'head'), may hold values from -4 to 4
- gate_weight: bfloat16 [512, 1024], P(None, 'head'), may hold values from -1 to 1
- up_weight: bfloat16 [512, 1024], P(None, 'head'), may hold values from -1 to 1
- down_weight: bfloat16 [1024, 512], P('head'), may hold values from -2 to 2
- head_weight: bfloat16 [512, 8], replicated, may hold values from -1 to 1
- head_bias: bfloat16 [8], replicated, may hold values from -4 to 4
Outputs:
- rebuilt: float32 [512, 512], P(('dp', 'head'))
- series_grad: float32 [512, 512], P(('dp', 'head'))
- gain_attn_grad: float32 [512], replicated
- gain_ff_grad: float32 [512], replicated
- gain_final_grad: float32 [512], replicated
- patch_weight_grad: float32 [8, 512], replicated
- patch_bias_grad: float32 [512], replicated
- query_grad: float32 [512, 512], P(None, 'head')
- key_grad: float32 [512, 512], P(None, 'head')
- value_grad: float32 [512, 512], P(None, 'head')
- out_grad: float32 [512, 512], P('head')
- table_grad: float32 [32, 8], P(None, 'head')
- gate_grad: float32 [512, 1024], P(None, 'head')
- up_grad: float32 [512, 1024], P(None, 'head')
- down_grad: float32 [1024, 512], P('head')
- head_weight_grad: float32 [512, 8], replicated
- head_bias_grad: float32 [8], replicated
Inputs may be any that keep to these rules, and one draw needn't show every extreme that they name: 1 marks an observed value; the first step of every block of 32 steps that starts at a multiple of 32 is observed. `item_split`: 1 marks a row that packs two items of half of 64 patches, 0 a row of one item.
All inputs are finite; a program needn't handle non-finite values. No bound on the sum of `item_split` on one device may be relied on, other than what follows from the above.
Results may differ from a plain program's by a relative error of at most 0.025.
Values may be sent and summed in bfloat16 or wider, within the bound.
A program may use at most 128 MiB of HBM per device.

v0:
```python
import math

import jax
import jax.numpy as jnp
import numpy as np
from jax import lax
from jax.sharding import PartitionSpec as P

HEAD_DIM = 64
BUCKETS = 32
MAX_DIST = 128


def bucket_onehot(length, buckets, far_reach):
    half_count = buckets // 2
    exact_count = half_count // 2
    onehot_table = np.zeros((length, length, buckets), np.float32)
    for row_pos in range(length):
        for col_pos in range(length):
            offset = col_pos - row_pos
            distance = abs(offset)
            bucket_id = half_count if offset > 0 else 0
            if distance < exact_count:
                bucket_id += distance
            else:
                bucket_id += min(
                    half_count - 1,
                    exact_count
                    + int(
                        math.log(distance / exact_count)
                        / math.log(far_reach / exact_count)
                        * (half_count - exact_count)
                    ),
                )
            onehot_table[row_pos, col_pos, bucket_id] = 1.0
    return onehot_table


def norm_scale(values):
    return lax.rsqrt(jnp.mean(values * values, axis=-1, keepdims=True) + 1e-06)


def norm_back(grad_out, unit_rows, row_scale, gain_vec):
    d_unit = grad_out * gain_vec
    gain_grad = jnp.sum(grad_out * unit_rows, axis=0)
    spread = jnp.mean(d_unit * unit_rows, axis=-1, keepdims=True)
    return (row_scale * (d_unit - unit_rows * spread), gain_grad)


def gelu_tanh(values):
    return jax.nn.gelu(values, approximate=True)


def item_combine(sums, split_col):
    return split_col * sums + (1.0 - split_col) * jnp.sum(sums, axis=-1, keepdims=True)


def same_items(split_rows, length):
    positions = jnp.arange(length, dtype=jnp.int32) // (length // 2)
    item_ids = split_rows[:, None] * positions[None, :]
    return (item_ids[:, :, None] == item_ids[:, None, :])[:, None]


def score_rows(query_rows, key_rows, offsets):
    return (
        jnp.einsum("rihd,rjhd->rhij", query_rows, key_rows, preferred_element_type=jnp.float32)
        + offsets[None]
    )


def attend_forward(rows_in, qkv_weight, table_here, onehot, same_item):
    tokens = rows_in.shape[0]
    length = onehot.shape[0]
    columns = qkv_weight.shape[1] // 3
    head_shape = (tokens // length, length, columns // HEAD_DIM, HEAD_DIM)
    projected = jnp.dot(rows_in, qkv_weight, preferred_element_type=jnp.float32).astype(
        jnp.bfloat16
    )
    query_rows = projected[:, :columns].reshape(head_shape)
    key_rows = projected[:, columns : 2 * columns].reshape(head_shape)
    value_rows = projected[:, 2 * columns :].reshape(head_shape)
    offsets = jnp.einsum(
        "ijb,bh->hij", onehot, table_here.astype(jnp.float32), precision=lax.Precision.HIGHEST
    )
    scores = score_rows(query_rows, key_rows, offsets)
    masked = jnp.where(same_item, scores, -1e30)
    row_top = jnp.max(masked, axis=-1, keepdims=True)
    raised = jnp.where(same_item, jnp.exp(masked - row_top), 0.0)
    totals = jnp.sum(raised, axis=-1, keepdims=True)
    prob_low = (raised / totals).astype(jnp.bfloat16)
    context = jnp.einsum(
        "rhij,rjhd->rihd", prob_low, value_rows, preferred_element_type=jnp.float32
    )
    context = context.reshape(tokens, columns).astype(jnp.bfloat16)
    return (context, (query_rows, key_rows, value_rows, offsets, row_top + jnp.log(totals)))


def attend_backward(d_context, attn_kept, same_item, onehot_low, rows_in):
    query_rows, key_rows, value_rows, offsets, log_total = attn_kept
    tokens = rows_in.shape[0]
    d_heads = d_context.reshape(query_rows.shape)
    scores = score_rows(query_rows, key_rows, offsets)
    probs = jnp.where(same_item, jnp.exp(jnp.where(same_item, scores, -1e30) - log_total), 0.0)
    d_values = jnp.einsum(
        "rhij,rihd->rjhd", probs.astype(jnp.bfloat16), d_heads, preferred_element_type=jnp.float32
    ).astype(jnp.bfloat16)
    d_probs = jnp.einsum("rihd,rjhd->rhij", d_heads, value_rows, preferred_element_type=jnp.float32)
    d_scores = (probs * (d_probs - jnp.sum(probs * d_probs, axis=-1, keepdims=True))).astype(
        jnp.bfloat16
    )
    table_grad = jnp.einsum(
        "rhij,ijb->bh", d_scores, onehot_low, preferred_element_type=jnp.float32
    )
    d_queries = jnp.einsum(
        "rhij,rjhd->rihd", d_scores, key_rows, preferred_element_type=jnp.float32
    ).astype(jnp.bfloat16)
    d_keys = jnp.einsum(
        "rhij,rihd->rjhd", d_scores, query_rows, preferred_element_type=jnp.float32
    ).astype(jnp.bfloat16)
    d_qkv = jnp.concatenate(
        [d_queries.reshape(tokens, -1), d_keys.reshape(tokens, -1), d_values.reshape(tokens, -1)],
        axis=1,
    )
    qkv_grad = jnp.einsum("td,tc->dc", rows_in, d_qkv, preferred_element_type=jnp.float32)
    return (d_qkv, qkv_grad, table_grad)


def feed_forward(rows_in, gate_up_weight):
    gate_up = jnp.dot(rows_in, gate_up_weight, preferred_element_type=jnp.float32)
    width = gate_up_weight.shape[1] // 2
    gate_proj = gate_up[:, :width]
    up_proj = gate_up[:, width:]
    act_value, act_pull = jax.vjp(gelu_tanh, gate_proj)
    inner_act = (act_value * up_proj).astype(jnp.bfloat16)
    return (inner_act, (up_proj, act_value, act_pull))


def feed_back(d_rows, inner_act, ff_kept, rows_in, down_here):
    up_proj, act_value, act_pull = ff_kept
    down_grad = jnp.einsum("tf,td->fd", inner_act, d_rows, preferred_element_type=jnp.float32)
    d_inner = jnp.einsum("td,fd->tf", d_rows, down_here, preferred_element_type=jnp.float32)
    d_gate = act_pull(d_inner * up_proj)[0].astype(jnp.bfloat16)
    d_up = (d_inner * act_value).astype(jnp.bfloat16)
    d_gate_up = jnp.concatenate([d_gate, d_up], axis=1)
    gate_up_grad = jnp.einsum("td,tf->df", rows_in, d_gate_up, preferred_element_type=jnp.float32)
    return (d_gate_up, gate_up_grad, down_grad)


def local(
    series,
    observed,
    item_split,
    recon_cot,
    gain_attn,
    gain_ff,
    gain_final,
    patch_weight,
    patch_bias,
    query_weight,
    key_weight,
    value_weight,
    out_weight,
    bias_table,
    gate_weight,
    up_weight,
    down_weight,
    head_weight,
    head_bias,
):
    rows_here, length = series.shape
    patch_len = patch_weight.shape[0]
    row_patches = length // patch_len
    half_len = length // 2
    local_split = lax.dynamic_slice_in_dim(
        item_split, lax.axis_index("head") * rows_here, rows_here, 0
    )
    split_col = local_split.astype(jnp.float32)[:, None]
    halves = series.reshape(rows_here, 2, half_len)
    obs_mask = observed.astype(jnp.float32).reshape(rows_here, 2, half_len)
    counts = item_combine(jnp.sum(obs_mask, axis=-1), split_col)
    item_mean = item_combine(jnp.sum(obs_mask * halves, axis=-1), split_col) / counts
    centred = halves - item_mean[..., None]
    item_var = item_combine(jnp.sum(obs_mask * centred * centred, axis=-1), split_col) / counts
    item_std = jnp.sqrt(item_var + 1e-05)
    normed = obs_mask * centred / item_std[..., None]
    patches = normed.reshape(-1, patch_len).astype(jnp.bfloat16)
    embedded = jnp.dot(
        patches, patch_weight, preferred_element_type=jnp.float32
    ) + patch_bias.astype(jnp.float32)
    attn_scale = norm_scale(embedded)
    attn_unit = embedded * attn_scale
    attn_in = (attn_unit * gain_attn.astype(jnp.float32)).astype(jnp.bfloat16)
    onehot = jnp.asarray(bucket_onehot(row_patches, BUCKETS, MAX_DIST))
    qkv_weight = jnp.concatenate([query_weight, key_weight, value_weight], axis=1)
    gate_up_weight = jnp.concatenate([gate_weight, up_weight], axis=1)
    table_here, out_here, down_here = (bias_table, out_weight, down_weight)
    same_item = same_items(item_split, row_patches)
    attn_rows = lax.all_gather(attn_in, "head", axis=0, tiled=True)
    context, attn_kept = attend_forward(attn_rows, qkv_weight, table_here, onehot, same_item)
    attn_out = lax.psum_scatter(
        jnp.dot(context, out_here, preferred_element_type=jnp.float32).astype(jnp.bfloat16),
        "head",
        scatter_dimension=0,
        tiled=True,
    ).astype(jnp.float32)
    hidden_mid = embedded + attn_out
    ff_scale = norm_scale(hidden_mid)
    ff_unit = hidden_mid * ff_scale
    ff_in = (ff_unit * gain_ff.astype(jnp.float32)).astype(jnp.bfloat16)
    ff_rows = lax.all_gather(ff_in, "head", axis=0, tiled=True)
    inner_act, ff_kept = feed_forward(ff_rows, gate_up_weight)
    ff_out = lax.psum_scatter(
        jnp.dot(inner_act, down_here, preferred_element_type=jnp.float32).astype(jnp.bfloat16),
        "head",
        scatter_dimension=0,
        tiled=True,
    ).astype(jnp.float32)
    hidden_end = hidden_mid + ff_out
    final_scale = norm_scale(hidden_end)
    final_unit = hidden_end * final_scale
    final_in = (final_unit * gain_final.astype(jnp.float32)).astype(jnp.bfloat16)
    output = jnp.dot(final_in, head_weight, preferred_element_type=jnp.float32) + head_bias.astype(
        jnp.float32
    )
    output_items = output.reshape(rows_here, 2, half_len)
    rebuilt = (output_items * item_std[..., None] + item_mean[..., None]).reshape(rows_here, length)
    cot_items = recon_cot.reshape(rows_here, 2, half_len)
    d_output = (cot_items * item_std[..., None]).reshape(-1, patch_len).astype(jnp.bfloat16)
    head_weight_grad = jnp.einsum(
        "td,tp->dp", final_in, d_output, preferred_element_type=jnp.float32
    )
    head_bias_grad = jnp.sum(d_output.astype(jnp.float32), axis=0)
    d_final = jnp.einsum("tp,dp->td", d_output, head_weight, preferred_element_type=jnp.float32)
    d_hidden_end, gain_final_grad = norm_back(
        d_final, final_unit, final_scale, gain_final.astype(jnp.float32)
    )
    ff_grad_low = d_hidden_end.astype(jnp.bfloat16)
    d_ff_rows = lax.all_gather(ff_grad_low, "head", axis=0, tiled=True)
    d_gate_up, gate_up_grad, down_grad = feed_back(
        d_ff_rows, inner_act, ff_kept, ff_rows, down_here
    )
    d_ff_in = lax.psum_scatter(
        jnp.einsum(
            "tf,df->td", d_gate_up, gate_up_weight, preferred_element_type=jnp.float32
        ).astype(jnp.bfloat16),
        "head",
        scatter_dimension=0,
        tiled=True,
    ).astype(jnp.float32)
    d_mid_norm, gain_ff_grad = norm_back(d_ff_in, ff_unit, ff_scale, gain_ff.astype(jnp.float32))
    d_hidden_mid = d_hidden_end + d_mid_norm
    attn_grad_low = d_hidden_mid.astype(jnp.bfloat16)
    d_attn_rows = lax.all_gather(attn_grad_low, "head", axis=0, tiled=True)
    out_grad = jnp.einsum("tc,td->cd", context, d_attn_rows, preferred_element_type=jnp.float32)
    d_context = jnp.einsum(
        "td,cd->tc", d_attn_rows, out_here, preferred_element_type=jnp.float32
    ).astype(jnp.bfloat16)
    d_qkv, qkv_grad, table_grad = attend_backward(
        d_context, attn_kept, same_item, onehot.astype(jnp.bfloat16), attn_rows
    )
    d_attn_in = lax.psum_scatter(
        jnp.einsum("tc,dc->td", d_qkv, qkv_weight, preferred_element_type=jnp.float32).astype(
            jnp.bfloat16
        ),
        "head",
        scatter_dimension=0,
        tiled=True,
    ).astype(jnp.float32)
    d_embed_norm, gain_attn_grad = norm_back(
        d_attn_in, attn_unit, attn_scale, gain_attn.astype(jnp.float32)
    )
    d_embedded = (d_hidden_mid + d_embed_norm).astype(jnp.bfloat16)
    patch_weight_grad = jnp.einsum(
        "tp,td->pd", patches, d_embedded, preferred_element_type=jnp.float32
    )
    patch_bias_grad = jnp.sum(d_embedded.astype(jnp.float32), axis=0)
    d_normed = jnp.einsum(
        "td,pd->tp", d_embedded, patch_weight, preferred_element_type=jnp.float32
    ).reshape(rows_here, 2, half_len)
    std_col = item_std[..., None]
    std_grad = (
        jnp.sum(cot_items * output_items, axis=-1) - jnp.sum(d_normed * normed, axis=-1) / item_std
    )
    var_weight = item_combine(std_grad / (2.0 * item_std) / counts, split_col)
    d_centred = d_normed * obs_mask / std_col + 2.0 * obs_mask * centred * var_weight[..., None]
    mean_grad = jnp.sum(cot_items, axis=-1) - jnp.sum(d_centred, axis=-1)
    mean_weight = item_combine(mean_grad / counts, split_col)
    series_grad = (d_centred + obs_mask * mean_weight[..., None]).reshape(rows_here, length)
    columns = qkv_grad.shape[1] // 3
    query_grad = qkv_grad[:, :columns]
    key_grad = qkv_grad[:, columns : 2 * columns]
    value_grad = qkv_grad[:, 2 * columns :]
    ff_columns = gate_up_grad.shape[1] // 2
    gate_grad = gate_up_grad[:, :ff_columns]
    up_grad = gate_up_grad[:, ff_columns:]
    query_grad, key_grad, value_grad, out_grad, table_grad, gate_grad, up_grad, down_grad = (
        lax.psum(
            (query_grad, key_grad, value_grad, out_grad, table_grad, gate_grad, up_grad, down_grad),
            "dp",
        )
    )
    (
        gain_attn_grad,
        gain_ff_grad,
        gain_final_grad,
        patch_weight_grad,
        patch_bias_grad,
        head_weight_grad,
        head_bias_grad,
    ) = lax.psum(
        (
            gain_attn_grad,
            gain_ff_grad,
            gain_final_grad,
            patch_weight_grad,
            patch_bias_grad,
            head_weight_grad,
            head_bias_grad,
        ),
        ("dp", "head"),
    )
    return (
        rebuilt,
        series_grad,
        gain_attn_grad,
        gain_ff_grad,
        gain_final_grad,
        patch_weight_grad,
        patch_bias_grad,
        query_grad,
        key_grad,
        value_grad,
        out_grad,
        table_grad,
        gate_grad,
        up_grad,
        down_grad,
        head_weight_grad,
        head_bias_grad,
    )


def solution(mesh):
    placed = (
        P(("dp", "head"), None),
        P(("dp", "head"), None),
        P("dp"),
        P(("dp", "head"), None),
        P(),
        P(),
        P(),
        P(),
        P(),
        P(None, "head"),
        P(None, "head"),
        P(None, "head"),
        P("head", None),
        P(None, "head"),
        P(None, "head"),
        P(None, "head"),
        P("head", None),
        P(),
        P(),
    )
    return jax.shard_map(
        local,
        mesh=mesh,
        in_specs=placed,
        out_specs=(
            P(("dp", "head"), None),
            P(("dp", "head"), None),
            P(),
            P(),
            P(),
            P(),
            P(),
            P(None, "head"),
            P(None, "head"),
            P(None, "head"),
            P("head", None),
            P(None, "head"),
            P(None, "head"),
            P(None, "head"),
            P("head", None),
            P(),
            P(),
        ),
        check_vma=False,
    )
```

profile of v0, /device:TPU:0, one launch (start us, length us, event | category | flops | bytes accessed | tf_op | source)
XLA Modules:
  0.0 882.6 jit_solution(1440008322378606804)
XLA Ops:
  24.2 81.8 %all-gather.5.cloned.1.call-done = bf16[4096,512]{0,1:T(8,128)(2,1)} async-done(((bf16[1024,512]{0,1:T(8,128)(2,1)}), bf16[4096,512]{0,1:T(8,128)(2,1)}) %all-gather.5.cloned.1.call-update) | async-done | bytes 4194320 | tf_op jit(solution)/shard_map/all_gather | solution.py:198
  106.1 4.6 convolution_convert_fusion.4
  115.8 4.8 copy.96
  120.6 5.3 reshape.517
  125.9 6.1 copy.99
  143.2 4.3 convolution_convert_fusion
  148.2 74.8 %reduce-scatter.5.cloned.1.call-done = bf16[1024,512]{0,1:T(8,128)(2,1)} async-done(((bf16[4096,512]{0,1:T(8,128)(2,1)}), bf16[1024,512]{0,1:T(8,128)(2,1)}) %reduce-scatter.5.cloned.1.call-update) | async-done | bytes 1048592 | tf_op jit(solution)/shard_map/reduce_scatter | solution.py:200
  226.8 81.3 %all-gather.7.cloned.1.call-done = bf16[4096,512]{0,1:T(8,128)(2,1)} async-done(((bf16[1024,512]{0,1:T(8,128)(2,1)}), bf16[4096,512]{0,1:T(8,128)(2,1)}) %all-gather.7.cloned.1.call-update) | async-done | bytes 4194320 | tf_op jit(solution)/shard_map/all_gather | solution.py:210
  308.1 4.7 fusion.57
  312.8 3.3 copy-done.4
  323.5 74.2 %reduce-scatter.7.cloned.1.call-done = bf16[1024,512]{0,1:T(8,128)(2,1)} async-done(((bf16[4096,512]{0,1:T(8,128)(2,1)}), bf16[1024,512]{0,1:T(8,128)(2,1)}) %reduce-scatter.7.cloned.1.call-update) | async-done | bytes 1048592 | tf_op jit(solution)/shard_map/reduce_scatter | solution.py:212
  404.7 81.4 %all-gather.9.cloned.1.call-done = bf16[4096,512]{0,1:T(8,128)(2,1)} async-done(((bf16[1024,512]{0,1:T(8,128)(2,1)}), bf16[4096,512]{0,1:T(8,128)(2,1)}) %all-gather.9.cloned.1.call-update) | async-done | bytes 4194320 | tf_op jit(solution)/shard_map/all_gather | solution.py:238
  486.1 8.4 fusion.6
  496.5 4.3 convolution_convert_fusion.3
  500.9 75.4 %reduce-scatter.9.cloned.1.call-done = bf16[1024,512]{0,1:T(8,128)(2,1)} async-done(((bf16[4096,512]{0,1:T(8,128)(2,1)}), bf16[1024,512]{0,1:T(8,128)(2,1)}) %reduce-scatter.9.cloned.1.call-update) | async-done | bytes 1048592 | tf_op jit(solution)/shard_map/reduce_scatter | solution.py:242
  579.0 4.0 fusion.52
  583.2 81.3 %all-gather.11.cloned.1.call-done = bf16[4096,512]{0,1:T(8,128)(2,1)} async-done(((bf16[1024,512]{0,1:T(8,128)(2,1)}), bf16[4096,512]{0,1:T(8,128)(2,1)}) %all-gather.11.cloned.1.call-update) | async-done | bytes 4194320 | tf_op jit(solution)/shard_map/all_gather | solution.py:253
  664.5 4.5 convolution_convert_fusion.5
  669.0 4.0 reshape.521
  673.0 3.7 copy.102
  676.7 4.4 convert_bitcast_fusion
  692.6 3.5 reshape.524
  696.1 4.2 copy.98
  700.4 4.1 reshape.522
  707.2 3.4 reshape.523
  712.6 4.3 convolution_convert_fusion.1
  719.0 5.8 fusion.9
  731.5 14.2 %psum.114 = f32[32,2]{0,1:T(2,128)} all-reduce(f32[32,2]{0,1:T(2,128)S(1)} %convolution_bitcast_fusion.1), channel_id=1, replica_groups=mesh['dp'=8,'head'=4] {'dp'}, use_global_device_ids=true, to_apply=%region_39.40 | all-reduce | flops 64 | bytes 512 | tf_op jit(solution)/shard_map/psum | solution.py:297
  745.7 5.6 fusion.60
  754.5 37.9 %reduce-scatter.11.cloned.1.call-done = bf16[1024,512]{0,1:T(8,128)(2,1)} async-done(((bf16[4096,512]{0,1:T(8,128)(2,1)}), bf16[1024,512]{0,1:T(8,128)(2,1)}) %reduce-scatter.11.cloned.1.call-update) | async-done | bytes 1048592 | tf_op jit(solution)/shard_map/reduce_scatter | solution.py:261
  799.7 42.2 %all-reduce = (f32[512]{0:T(512)}, f32[512]{0:T(512)}, f32[512]{0:T(512)}, f32[8,512]{1,0:T(8,128)}, f32[512]{0:T(512)}, /*index=5*/f32[512,8]{0,1:T(8,128)}, f32[8]{0:T(128)}) all-reduce(f32[512]{0:T(512)S(1)} %copy-done.88, f32[512]{0:T(512)S(1)} %copy-done.87, ...), channel_id=1, replica_groups=mesh['dp'=8,'head'=4] {'dp','head'}, use_global_device_ids=true, to_apply=%region_26.27 | all-reduce | flops 10248 | bytes 81984 | tf_op jit(solution)/shard_map/psum | solution.py:310
  842.6 23.0 %all-reduce.4.cloned.1.call-done = (f32[512,128]{1,0:T(8,128)}, f32[512,128]{1,0:T(8,128)}, f32[512,128]{1,0:T(8,128)}, f32[128,512]{1,0:T(8,128)}, f32[512,256]...) async-done(((f32[512,128]{1,0:T(8,128)}, f32[512,128]{1,0:T(8,128)}, f32[512,128]{1,0:T(8,128)}, f32[128,512]{1,0:T(8,128)}, f32[512,256]{1,0:T(8,128)}, ...) | async-done | bytes 2621456 | tf_op jit(solution)/shard_map/psum | solution.py:297
  (326 shorter events, 102.2 us)
Async XLA Ops:
  7.2 311.8 %copy-start = (bf16[256,512]{1,0:T(8,128)(2,1)S(1)}, bf16[256,512]{1,0:T(8,128)(2,1)}, u32[]{:S(2)}) copy-start(bf16[256,512]{1,0:T(8,128)(2,1)} %param.36) | copy-start | bytes 786436
  7.2 98.9 %all-gather.5.cloned.1.call-start = ((), (), s32[]{:S(2)}) async-start(), calls=%async_computation.4 | async-start | bytes 5242880 | tf_op jit(solution)/shard_map/all_gather | solution.py:198
  9.8 9.5 %copy-start.76 = (bf16[8,512]{1,0:T(8,128)(2,1)S(1)}, bf16[8,512]{1,0:T(8,128)(2,1)}, u32[]{:S(2)}) copy-start(bf16[8,512]{1,0:T(8,128)(2,1)} %param.27) | copy-start | bytes 24580
  22.5 200.5 %reduce-scatter.5.cloned.1.call-start = ((), (), s32[]{:S(2)}) async-start(), calls=%async_computation.5 | async-start | bytes 5242880 | tf_op jit(solution)/shard_map/reduce_scatter | solution.py:200
  23.4 87.2 %copy-start.70 = (bf16[512,384]{1,0:T(8,128)(2,1)}, bf16[512,384]{1,0:T(8,128)(2,1)S(1)}, u32[]{:S(2)}) copy-start(bf16[512,384]{1,0:T(8,128)(2,1)S(1)} %constant_dynamic-update-slice_fusion) | copy-start | bytes 1179652
  24.2 112.5 %copy-start.19 = (pred[64,64,64]{1,2,0:T(8,128)(4,1)}, pred[64,64,64]{1,2,0:T(8,128)(4,1)S(1)}, u32[]{:S(2)}) copy-start(pred[64,64,64]{1,2,0:T(8,128)(4,1)S(1)} %broadcast_compare_fusion) | copy-start | bytes 786436
  120.6 11.4 %copy-start.8 = (bf16[64,64,2,64]{1,3,2,0:T(8,128)(2,1)}, bf16[64,64,2,64]{1,3,2,0:T(8,128)(2,1)S(1)}, u32[]{:S(2)}) copy-start(bf16[64,64,2,64]{1,3,2,0:T(8,128)(2,1)S(1)} %copy.96) | copy-start | bytes 3145732
  147.5 75.5 %copy-start.62 = (f32[512]{0:T(512)S(1)}, f32[512]{0:T(512)}, u32[]{:S(2)}) copy-start(f32[512]{0:T(512)} %copy-done.61) | copy-start | bytes 6148
  147.5 160.6 %all-gather.7.cloned.1.call-start = ((), (), s32[]{:S(2)}) async-start(), calls=%async_computation.6 | async-start | bytes 5242880 | tf_op jit(solution)/shard_map/all_gather | solution.py:210
  148.2 78.5 %copy-start.79 = (f32[512]{0:T(512)}, f32[512]{0:T(512)S(1)}, u32[]{:S(2)}) copy-start(f32[512]{0:T(512)S(1)} %convert_element_type.149) | copy-start | bytes 6148
  226.7 171.0 %reduce-scatter.7.cloned.1.call-start = ((), (), s32[]{:S(2)}) async-start(), calls=%async_computation.7 | async-start | bytes 5242880 | tf_op jit(solution)/shard_map/reduce_scatter | solution.py:212
  226.8 86.0 %copy-start.31 = (bf16[512,512]{1,0:T(8,128)(2,1)}, bf16[512,512]{1,0:T(8,128)(2,1)S(1)}, u32[]{:S(2)}) copy-start(bf16[512,512]{1,0:T(8,128)(2,1)S(1)} %constant_dynamic-update-slice_fusion.3) | copy-start | bytes 1572868
  322.3 163.8 %all-gather.9.cloned.1.call-start = ((), (), s32[]{:S(2)}) async-start(), calls=%async_computation.8 | async-start | bytes 5242880 | tf_op jit(solution)/shard_map/all_gather | solution.py:238
  404.7 171.6 %reduce-scatter.9.cloned.1.call-start = ((), (), s32[]{:S(2)}) async-start(), calls=%async_computation.9 | async-start | bytes 5242880 | tf_op jit(solution)/shard_map/reduce_scatter | solution.py:242
  486.1 10.4 %copy-start.32 = (bf16[512,512]{1,0:T(8,128)(2,1)S(1)}, bf16[512,512]{1,0:T(8,128)(2,1)}, u32[]{:S(2)}) copy-start(bf16[512,512]{1,0:T(8,128)(2,1)} %copy-done.31) | copy-start | bytes 1572868
  500.8 75.5 %copy-start.67 = (f32[1024]{0:T(1024)S(1)}, f32[1024]{0:T(1024)}, u32[]{:S(2)}) copy-start(f32[1024]{0:T(1024)} %copy-done.66) | copy-start | bytes 12292
  500.8 75.5 %copy-start.80 = (f32[512]{0:T(512)S(1)}, f32[512]{0:T(512)}, u32[]{:S(2)}) copy-start(f32[512]{0:T(512)} %copy-done.79) | copy-start | bytes 6148
  500.8 163.7 %all-gather.11.cloned.1.call-start = ((), (), s32[]{:S(2)}) async-start(), calls=%async_computation.10 | async-start | bytes 5242880 | tf_op jit(solution)/shard_map/all_gather | solution.py:253
  579.0 85.5 %copy-start.37 = (bf16[128,512]{1,0:T(8,128)(2,1)S(1)}, bf16[128,512]{1,0:T(8,128)(2,1)}, u32[]{:S(2)}) copy-start(bf16[128,512]{1,0:T(8,128)(2,1)} %param.32) | copy-start | bytes 393220
  583.1 209.4 %reduce-scatter.11.cloned.1.call-start = ((), (), s32[]{:S(2)}) async-start(), calls=%async_computation.11 | async-start | bytes 5242880 | tf_op jit(solution)/shard_map/reduce_scatter | solution.py:261
  717.0 148.5 %all-reduce.4.cloned.1.call-start = ((), (), s32[]{:S(2)}) async-start(), calls=%async_computation.12 | async-start | bytes 5242880 | tf_op jit(solution)/shard_map/psum | solution.py:297
  752.2 40.2 %copy-start.3 = (f32[1024,512]{0,1:T(8,128)S(1)}, f32[1024,512]{0,1:T(8,128)}, u32[]{:S(2)}) copy-start(f32[1024,512]{0,1:T(8,128)} %copy-done.2) | copy-start | bytes 6291460
  752.2 40.2 %copy-start.63 = (f32[512]{0:T(512)S(1)}, f32[512]{0:T(512)}, u32[]{:S(2)}) copy-start(f32[512]{0:T(512)} %copy-done.61) | copy-start | bytes 6148
  752.3 40.2 %copy-start.65 = (f32[1024]{0:T(1024)S(1)}, f32[1024]{0:T(1024)}, u32[]{:S(2)}) copy-start(f32[1024]{0:T(1024)} %copy-done.64) | copy-start | bytes 12292
  752.3 40.2 %copy-start.74 = (f32[512]{0:T(512)S(1)}, f32[512]{0:T(512)}, u32[]{:S(2)}) copy-start(f32[512]{0:T(512)} %copy-done.73) | copy-start | bytes 6148
  796.9 45.0 %copy-start.34 = (f32[16,512]{1,0:T(8,128)S(1)}, f32[16,512]{1,0:T(8,128)}, u32[]{:S(2)}) copy-start(f32[16,512]{1,0:T(8,128)} %param.20) | copy-start | bytes 98308
  796.9 45.0 %copy-start.38 = (s32[16,512]{1,0:T(8,128)S(1)}, s32[16,512]{1,0:T(8,128)}, u32[]{:S(2)}) copy-start(s32[16,512]{1,0:T(8,128)} %param.21) | copy-start | bytes 98308
  796.9 45.0 %copy-start.43 = (f32[2,8,2,256]{3,1,2,0:T(8,128)S(1)}, f32[2,8,2,256]{3,1,2,0:T(8,128)}, u32[]{:S(2)}) copy-start(f32[2,8,2,256]{3,1,2,0:T(8,128)} %copy-done.42) | copy-start | bytes 98308
  796.9 45.0 %copy-start.53 = (f32[16,512]{1,0:T(8,128)S(1)}, f32[16,512]{1,0:T(8,128)}, u32[]{:S(2)}) copy-start(f32[16,512]{1,0:T(8,128)} %reshape.519) | copy-start | bytes 98308
  797.0 45.0 %copy-start.56 = (f32[2,8,2,256]{3,1,2,0:T(8,128)S(1)}, f32[2,8,2,256]{3,1,2,0:T(8,128)}, u32[]{:S(2)}) copy-start(f32[2,8,2,256]{3,1,2,0:T(8,128)} %copy.122) | copy-start | bytes 98308
  799.2 76.5 %copy-start.1 = (bf16[256,512]{1,0:T(8,128)(2,1)S(1)}, bf16[256,512]{1,0:T(8,128)(2,1)}, u32[]{:S(2)}) copy-start(bf16[256,512]{1,0:T(8,128)(2,1)} %param.36) | copy-start | bytes 786436
  865.5 9.4 %copy-start.39 = (f32[256,512]{1,0:T(8,128)S(1)}, f32[256,512]{1,0:T(8,128)}, u32[]{:S(2)}) copy-start(f32[256,512]{1,0:T(8,128)} %get-tuple-element.95) | copy-start | bytes 1572868
  (77 other events, 236.2 us)
Sparse Core Ops, SparseCore 0:
  22.6 83.4 all-gather.4
  147.6 75.2 reduce-scatter.4
  226.8 81.2 all-gather.6
  322.4 75.2 reduce-scatter.6
  404.8 81.2 all-gather.8
  501.0 75.2 reduce-scatter.8
  583.2 81.2 all-gather.10
  717.1 75.2 reduce-scatter.10
  797.7 67.7 all-reduce.3
where the time goes:
time: 887 us; the launch traced here: 883 us
  waiting for transfers between devices  611 us (69%)
  local copies, waits for them, and re-layouts  90.6 us (10%)
  matrix products  74.1 us (8%)
  blocking collectives  56.4 us (6%)
  other arithmetic  34.3 us (4%)
  between operations  15.4 us (2%)
    all_gather x1, waiting for transfers between devices, local(): attn_rows = lax.all_gather(attn_in, 'head', axis=0, tiled=True)  81.8 us
    all_gather x1, waiting for transfers between devices, local(): d_ff_rows = lax.all_gather(ff_grad_low, 'head', axis=0, tiled=True)  81.4 us
    all_gather x1, waiting for transfers between devices, local(): d_attn_rows = lax.all_gather(attn_grad_low, 'head', axis=0, tiled=True)  81.3 us
    all_gather x1, waiting for transfers between devices, local(): ff_rows = lax.all_gather(ff_in, 'head', axis=0, tiled=True)  81.3 us
    reduce_scatter x1, waiting for transfers between devices, local(): lax.psum_scatter(jnp.einsum('tf,df->td', d_gate_up, gate_up_weight, prefe...  75.4 us
    reduce_scatter x1, waiting for transfers between devices, local(): lax.psum_scatter(jnp.dot(context, out_here, preferred_element_type=jnp.fl...  74.8 us
    reduce_scatter x1, waiting for transfers between devices, local(): lax.psum_scatter(jnp.dot(inner_act, down_here, preferred_element_type=jnp...  74.2 us
    psum x1, blocking collectives, local(): lax.psum((gain_attn_grad, gain_ff_grad, gain_final_grad, patch_weight_gra...  42.2 us
  transfers between devices with their start and end apart: 9, of which 9 were waited for; matrix products, arithmetic and copies ran while one was open for 4% of the time, Pallas kernels for 0%

commit v1 on v0

--- a/solution.py
+++ b/solution.py
@@ -191,30 +191,38 @@
     attn_unit = embedded * attn_scale
     attn_in = (attn_unit * gain_attn.astype(jnp.float32)).astype(jnp.bfloat16)
     onehot = jnp.asarray(bucket_onehot(row_patches, BUCKETS, MAX_DIST))
-    qkv_weight = jnp.concatenate([query_weight, key_weight, value_weight], axis=1)
-    gate_up_weight = jnp.concatenate([gate_weight, up_weight], axis=1)
-    table_here, out_here, down_here = (bias_table, out_weight, down_weight)
-    same_item = same_items(item_split, row_patches)
-    attn_rows = lax.all_gather(attn_in, "head", axis=0, tiled=True)
+    columns_here = query_weight.shape[1]
+    ff_here = gate_weight.shape[1]
+    heads_here = bias_table.shape[1]
+    mixed = jnp.concatenate(
+        [query_weight, key_weight, value_weight, gate_weight, up_weight], axis=1
+    )
+    mixed_all = lax.all_gather(mixed, "head", axis=0)
+    rest_all = lax.all_gather(jnp.concatenate([out_weight, down_weight], axis=0), "head", axis=0)
+    table_here = lax.all_gather(bias_table, "head", axis=1, tiled=True)
+
+    def side(start, width):
+        return jnp.moveaxis(mixed_all[:, :, start : start + width], 0, 1).reshape(
+            mixed_all.shape[1], -1
+        )
+
+    qkv_weight = jnp.concatenate([side(i * columns_here, columns_here) for i in range(3)], axis=1)
+    gate_up_weight = jnp.concatenate(
+        [side(3 * columns_here + i * ff_here, ff_here) for i in range(2)], axis=1
+    )
+    out_here = rest_all[:, :columns_here].reshape(-1, rest_all.shape[2])
+    down_here = rest_all[:, columns_here:].reshape(-1, rest_all.shape[2])
+    same_item = same_items(local_split, row_patches)
+    attn_rows = attn_in
     context, attn_kept = attend_forward(attn_rows, qkv_weight, table_here, onehot, same_item)
-    attn_out = lax.psum_scatter(
-        jnp.dot(context, out_here, preferred_element_type=jnp.float32).astype(jnp.bfloat16),
-        "head",
-        scatter_dimension=0,
-        tiled=True,
-    ).astype(jnp.float32)
+    attn_out = jnp.dot(context, out_here, preferred_element_type=jnp.float32)
     hidden_mid = embedded + attn_out
     ff_scale = norm_scale(hidden_mid)
     ff_unit = hidden_mid * ff_scale
     ff_in = (ff_unit * gain_ff.astype(jnp.float32)).astype(jnp.bfloat16)
-    ff_rows = lax.all_gather(ff_in, "head", axis=0, tiled=True)
+    ff_rows = ff_in
     inner_act, ff_kept = feed_forward(ff_rows, gate_up_weight)
-    ff_out = lax.psum_scatter(
-        jnp.dot(inner_act, down_here, preferred_element_type=jnp.float32).astype(jnp.bfloat16),
-        "head",
-        scatter_dimension=0,
-        tiled=True,
-    ).astype(jnp.float32)
+    ff_out = jnp.dot(inner_act, down_here, preferred_element_type=jnp.float32)
     hidden_end = hidden_mid + ff_out
     final_scale = norm_scale(hidden_end)
     final_unit = hidden_end * final_scale
@@ -235,22 +243,17 @@
         d_final, final_unit, final_scale, gain_final.astype(jnp.float32)
     )
     ff_grad_low = d_hidden_end.astype(jnp.bfloat16)
-    d_ff_rows = lax.all_gather(ff_grad_low, "head", axis=0, tiled=True)
+    d_ff_rows = ff_grad_low
     d_gate_up, gate_up_grad, down_grad = feed_back(
         d_ff_rows, inner_act, ff_kept, ff_rows, down_here
     )
-    d_ff_in = lax.psum_scatter(
-        jnp.einsum(
-            "tf,df->td", d_gate_up, gate_up_weight, preferred_element_type=jnp.float32
-        ).astype(jnp.bfloat16),
-        "head",
-        scatter_dimension=0,
-        tiled=True,
-    ).astype(jnp.float32)
+    d_ff_in = jnp.einsum(
+        "tf,df->td", d_gate_up, gate_up_weight, preferred_element_type=jnp.float32
+    )
     d_mid_norm, gain_ff_grad = norm_back(d_ff_in, ff_unit, ff_scale, gain_ff.astype(jnp.float32))
     d_hidden_mid = d_hidden_end + d_mid_norm
     attn_grad_low = d_hidden_mid.astype(jnp.bfloat16)
-    d_attn_rows = lax.all_gather(attn_grad_low, "head", axis=0, tiled=True)
+    d_attn_rows = attn_grad_low
     out_grad = jnp.einsum("tc,td->cd", context, d_attn_rows, preferred_element_type=jnp.float32)
     d_context = jnp.einsum(
         "td,cd->tc", d_attn_rows, out_here, preferred_element_type=jnp.float32
@@ -258,14 +261,7 @@
     d_qkv, qkv_grad, table_grad = attend_backward(
         d_context, attn_kept, same_item, onehot.astype(jnp.bfloat16), attn_rows
     )
-    d_attn_in = lax.psum_scatter(
-        jnp.einsum("tc,dc->td", d_qkv, qkv_weight, preferred_element_type=jnp.float32).astype(
-            jnp.bfloat16
-        ),
-        "head",
-        scatter_dimension=0,
-        tiled=True,
-    ).astype(jnp.float32)
+    d_attn_in = jnp.einsum("tc,dc->td", d_qkv, qkv_weight, preferred_element_type=jnp.float32)
     d_embed_norm, gain_attn_grad = norm_back(
         d_attn_in, attn_unit, attn_scale, gain_attn.astype(jnp.float32)
     )
@@ -293,13 +289,38 @@
     ff_columns = gate_up_grad.shape[1] // 2
     gate_grad = gate_up_grad[:, :ff_columns]
     up_grad = gate_up_grad[:, ff_columns:]
-    query_grad, key_grad, value_grad, out_grad, table_grad, gate_grad, up_grad, down_grad = (
-        lax.psum(
-            (query_grad, key_grad, value_grad, out_grad, table_grad, gate_grad, up_grad, down_grad),
-            "dp",
-        )
-    )
+    def by_head(grad, width):
+        return jnp.moveaxis(grad.reshape(grad.shape[0], -1, width), 1, 0)
+
+    mixed_grad = jnp.concatenate(
+        [by_head(g, columns_here) for g in (query_grad, key_grad, value_grad)]
+        + [by_head(g, ff_here) for g in (gate_grad, up_grad)],
+        axis=2,
+    )
+    rest_grad = jnp.concatenate(
+        [
+            out_grad.reshape(-1, columns_here, out_grad.shape[1]),
+            down_grad.reshape(-1, ff_here, down_grad.shape[1]),
+        ],
+        axis=1,
+    )
+    mixed_grad = lax.psum_scatter(
+        mixed_grad.astype(jnp.bfloat16), "head", scatter_dimension=0, tiled=True
+    )[0].astype(jnp.float32)
+    rest_grad = lax.psum_scatter(
+        rest_grad.astype(jnp.bfloat16), "head", scatter_dimension=0, tiled=True
+    )[0].astype(jnp.float32)
+    mixed_grad, rest_grad = lax.psum((mixed_grad, rest_grad), "dp")
+    query_grad, key_grad, value_grad = (
+        mixed_grad[:, i * columns_here : (i + 1) * columns_here] for i in range(3)
+    )
+    gate_grad, up_grad = (
+        mixed_grad[:, 3 * columns_here + i * ff_here : 3 * columns_here + (i + 1) * ff_here]
+        for i in range(2)
+    )
+    out_grad, down_grad = (rest_grad[:columns_here], rest_grad[columns_here:])
     (
+        table_grad,
         gain_attn_grad,
         gain_ff_grad,
         gain_final_grad,
@@ -309,6 +330,7 @@
         head_bias_grad,
     ) = lax.psum(
         (
+            table_grad,
             gain_attn_grad,
             gain_ff_grad,
             gain_final_grad,
@@ -318,6 +340,9 @@
             head_bias_grad,
         ),
         ("dp", "head"),
+    )
+    table_grad = lax.dynamic_slice_in_dim(
+        table_grad, lax.axis_index("head") * heads_here, heads_here, 1
     )
     return (
         rebuilt,

time: 887 us -> 428 us (0.48)
  waiting for transfers between devices: 611 us -> 151 us
  local copies, waits for them, and re-layouts: 90.6 us -> 115 us
  matrix products: 74.1 us -> 59.7 us
    all_gather x4 -> x2, waiting for transfers between devices: 326 us -> 84.5 us  [the longest x1 68.4 us: local(): mixed_all = lax.all_gather(mixed, 'head', axis=0)]
    reduce_scatter x4 -> x2, waiting for transfers between devices: 262 us -> 49.4 us  [the longest x1 49.4 us: local(): lax.psum_scatter(mixed_grad.astype(jnp.bfloat16), 'head', scatter_dimensi...]
    transpose x0 -> x7, local copies, waits for them, and re-layouts: none -> 15.4 us  [side(): jnp.moveaxis(mixed_all[:, :, start:start + width], 0, 1)]
    psum x2 -> x1, blocking collectives: 56.4 us -> 42.2 us  [local(): lax.psum((table_grad, gain_attn_grad, gain_ff_grad, gain_final_grad, patc...]
    unnamed x216 -> x195, local copies, waits for them, and re-layouts: 28.1 us -> 15.3 us
    all_gather x0 -> x1, blocking collectives: none -> 12.7 us  [local(): table_here = lax.all_gather(bias_table, 'head', axis=1, tiled=True)]
    slice x1 -> x6, local copies, waits for them, and re-layouts: 0.89 us -> 10.9 us  [the longest x2 3.67 us: local(): out_grad, down_grad = (rest_grad[:columns_here], rest_grad[columns_here:])]
    reduce_sum x4 -> x0, other arithmetic: 9.42 us -> none  [the longest x2 5.45 us: norm_back(): gain_grad = jnp.sum(grad_out * unit_rows, axis=0)]
  transfers between devices with their start and end apart: 9 -> 5, of which waited for: 9 -> 4; matrix products, arithmetic and copies ran while one was open for 4% -> 19% of each run, Pallas kernels for 0% -> 0%
where the time goes in v1:
time: 428 us; the launch traced here: 422 us
  waiting for transfers between devices  151 us (35%)
  local copies, waits for them, and re-layouts  115 us (27%)
  matrix products  59.7 us (14%)
  blocking collectives  54.9 us (13%)
  other arithmetic  25.9 us (6%)
  between operations  15.3 us (4%)
    all_gather x1, waiting for transfers between devices, local(): mixed_all = lax.all_gather(mixed, 'head', axis=0)  68.4 us
    reduce_scatter x1, waiting for transfers between devices, local(): lax.psum_scatter(mixed_grad.astype(jnp.bfloat16), 'head', scatter_dimensi...  49.4 us
    psum x1, blocking collectives, local(): lax.psum((table_grad, gain_attn_grad, gain_ff_grad, gain_final_grad, patc...  42.2 us
    psum x1, waiting for transfers between devices, local(): mixed_grad, rest_grad = lax.psum((mixed_grad, rest_grad), 'dp')  17 us
    all_gather x1, waiting for transfers between devices, local(): lax.all_gather(jnp.concatenate([out_weight, down_weight], axis=0), 'head'...  16.1 us
    transpose x7, local copies, waits for them, and re-layouts, side(): jnp.moveaxis(mixed_all[:, :, start:start + width], 0, 1)  15.4 us
    unnamed x195, local copies, waits for them, and re-layouts  15.3 us
    all_gather x1, blocking collectives, local(): table_here = lax.all_gather(bias_table, 'head', axis=1, tiled=True)  12.7 us
  transfers between devices with their start and end apart: 5, of which 4 were waited for; matrix products, arithmetic and copies ran while one was open for 19% of the time, Pallas kernels for 0%

profile of v1, /device:TPU:0, one launch (start us, length us, event | category | flops | bytes accessed | tf_op | source)
XLA Modules:
  0.0 422.5 jit_solution(615533440905014412)
XLA Ops:
  16.6 12.7 %all-gather.2 = bf16[4,2,32]{2,1,0:T(2,128)(2,1)S(1)} all-gather(bf16[1,2,32]{2,1,0:T(2,128)(2,1)S(1)} %bitcast.180), channel_id=1, replica_groups=mesh['dp'=8,'head'=4] {'head'}, dimensions={0}, use_global_device_ids=true | all-gather | bytes 640 | tf_op jit(solution)/shard_map/all_gather | solution.py:202
  34.0 16.1 %all-gather.8.cloned.1.call-done = bf16[1536,512]{1,0:T(8,128)(2,1)} async-done(((bf16[384,512]{1,0:T(8,128)(2,1)}), bf16[1536,512]{1,0:T(8,128)(2,1)}) %all-gather.8.cloned.1.call-update) | async-done | bytes 1572880 | tf_op jit(solution)/shard_map/all_gather | solution.py:201
  54.2 68.4 %all-gather.6.cloned.1.call-done = bf16[2048,896]{1,0:T(8,128)(2,1)} async-done(((bf16[512,896]{1,0:T(8,128)(2,1)}), bf16[2048,896]{1,0:T(8,128)(2,1)}) %all-gather.6.cloned.1.call-update) | async-done | bytes 3670032 | tf_op jit(solution)/shard_map/all_gather | solution.py:200
  122.6 2.6 slice_bitcast_fusion.7
  125.2 2.6 slice_bitcast_fusion.1
  127.8 2.8 copy.153
  138.1 3.5 convolution_convert_fusion
  143.1 3.9 reshape.571
  147.0 3.9 reshape.573
  150.9 4.1 copy.163
  157.1 4.1 copy.166
  161.2 3.5 fusion.8
  167.9 2.8 convert_bitcast_fusion.3
  170.7 4.1 copy.152
  174.8 3.4 convert_element_type.138
  180.6 2.6 fusion.19
  187.9 4.4 %fusion.6 = (bf16[1024,1024]{1,0:T(8,128)(2,1)S(1)}, bf16[1024,1024]{1,0:T(8,128)(2,1)S(1)}) fusion(f32[1024,2048]{1,0:T(8,128)S(1)} %fusion.19, bf16[1024,512]{1,0:T(8,128)(2,1)S(1)} %bitcast.163, f32[1024,512]{0,1:T(8,128)S(1)} %get-tuple-element.61), kind=kOutput, calls=%fused_computation.8 | convolution fusion | flops 1099431936 | bytes 15728640 | tf_op jit(solution)/shard_map/td,fd->tf/dot_general | solution.py:141
  194.7 3.3 multiply_reduce_fusion.2
  200.8 3.9 reshape.580
  204.7 4.4 %copy.169 = bf16[16,64,8,64]{1,3,2,0:T(8,128)(2,1)} copy(bf16[16,64,8,64]{3,2,1,0:T(8,128)(2,1)} %reshape.580) | data formatting | bytes 2097152 | tf_op jit(solution)/shard_map/reshape | solution.py:101
  209.1 5.8 %convert_bitcast_fusion = bf16[16,64,8,64]{1,3,2,0:T(8,128)(2,1)} fusion(bf16[16,64,8,64]{1,3,2,0:T(8,128)(2,1)} %copy.169, f32[16,8,64,64]{2,3,1,0:T(8,128)} %copy-done.1, f32[16,8,64]{2,1,0:T(8,128)} %log_add_fusion, f32[8,64,64]{1,2,0:T(8,128)S(1)} %copy.149, pred[16,64,64]{1,2,0:T(8,128)(4,1)S(1)} %broadcast_compare_fusion), kind=kOutput, calls=%fused_computation.33 | convolution fusion | flops 70254592 | bytes 4423680 | tf_op jit(solution)/shard_map/rhij,rihd->rjhd/dot_general | solution.py:104
  229.2 4.6 %copy.165 = bf16[16,64,8,64]{3,2,1,0:T(8,128)(2,1)} copy(bf16[16,64,8,64]{1,3,2,0:T(8,128)(2,1)} %convert_bitcast_fusion.2) | data formatting | bytes 2097152 | tf_op jit(solution)/shard_map/convert_element_type | solution.py:116
  233.8 4.1 reshape.581
  237.9 4.1 copy.168
  242.0 4.1 reshape.582
  249.6 4.1 copy.171
  253.7 4.1 reshape.583
  260.4 4.0 convolution_convert_fusion.2
  276.4 6.4 %multiply_reduce_fusion.3 = (f32[512]{0:T(512)}, f32[1024]{0:T(1024)S(1)}, f32[1024,512]{0,1:T(8,128)S(1)}) fusion(f32[1024,512]{0,1:T(8,128)} %copy-done.3, f32[1024]{0:T(1024)S(1)} %copy-done.68, f32[512]{0:T(512)S(1)} %copy-done.62, f32[512]{0:T(512)S(1)} %copy-done.73, bf16[1024,1536]{1,0:T(8,128)(2,1)} %constant_dynamic-update-slice_fusion.5, ...), kind=kOutput, calls=%fused_computation.30 | convolution fusion | flops 1618999808 | bytes 8927232 | tf_op jit(solution)/shard_map/tc,dc->td/dot_general | solution.py:264
  290.1 49.4 %reduce-scatter.3.cloned.1.call-done = bf16[1,512,896]{2,1,0:T(8,128)(2,1)} async-done(((bf16[4,512,896]{2,1,0:T(8,128)(2,1)}), bf16[1,512,896]{2,1,0:T(8,128)(2,1)}) %reduce-scatter.3.cloned.1.call-update) | async-done | bytes 917520 | tf_op jit(solution)/shard_map/reduce_scatter | solution.py:307
  348.5 42.2 %all-reduce = (f32[512]{0:T(512)}, f32[512]{0:T(512)}, f32[512]{0:T(512)}, f32[8,512]{1,0:T(8,128)}, f32[512]{0:T(512)}, /*index=5*/f32[32,8]{0,1:T(8,128)S(1)}, f32[512,8]{0,1:T(8,128)}, f32[8]{0:T(128)}) all-reduce(f32[512]{0:T(512)S(1)} %copy-done.77, f32[512]{0:T(512)S(1)} %copy-done.76, ...), channel_id=1, replica_groups=mesh['dp'=8,'head'=4] {'dp','head'}, use_global_device_ids=true, to_apply=%region_22.23 | all-reduce | flops 10504 | bytes 84032 | tf_op jit(solution)/shard_map/psum | solution.py:331
  392.0 17.0 %all-reduce.4.cloned.1.call-done = (f32[512,896]{1,0:T(8,128)}, f32[384,512]{1,0:T(8,128)}) async-done(((f32[512,896]{1,0:T(8,128)}, f32[384,512]{1,0:T(8,128)}), (f32[512,896]{1,0:T(8,128)}, f32[384,512]{1,0:T(8,128)})) %all-reduce.4.cloned.1.call-update) | async-done | bytes 2621456 | tf_op jit(solution)/shard_map/psum | solution.py:313
  (305 shorter events, 100.4 us)
Async XLA Ops:
  7.2 178.8 %copy-start = (bf16[512,8]{0,1:T(8,128)(2,1)S(1)}, bf16[512,8]{0,1:T(8,128)(2,1)}, u32[]{:S(2)}) copy-start(bf16[512,8]{0,1:T(8,128)(2,1)} %param.37) | copy-start | bytes 24580
  7.2 42.8 %all-gather.8.cloned.1.call-start = ((), (), s32[]{:S(2)}) async-start(), calls=%async_computation.5 | async-start | bytes 1966080 | tf_op jit(solution)/shard_map/all_gather | solution.py:201
  9.2 113.5 %all-gather.6.cloned.1.call-start = ((), (), s32[]{:S(2)}) async-start(), calls=%async_computation.4 | async-start | bytes 4587520 | tf_op jit(solution)/shard_map/all_gather | solution.py:200
  12.1 17.2 %copy-start.28 = (f32[64,64,32]{1,2,0:T(8,128)S(1)}, f32[64,64,32]{1,2,0:T(8,128)}, u32[]{:S(2)}) copy-start(f32[64,64,32]{1,2,0:T(8,128)} %constant.67.clone) | copy-start | bytes 1572868
  13.1 275.0 %reduce-scatter.5.cloned.1.call-start = ((), (), s32[]{:S(2)}) async-start(), calls=%async_computation.3 | async-start | bytes 1966080 | tf_op jit(solution)/shard_map/reduce_scatter | solution.py:310
  13.2 17.5 %copy-start.32 = (f32[16,2,256]{2,1,0:T(2,128)}, f32[16,2,256]{2,1,0:T(2,128)S(1)}, u32[]{:S(2)}) copy-start(f32[16,2,256]{2,1,0:T(2,128)S(1)} %reshape.566) | copy-start | bytes 98308
  13.6 17.2 %copy-start.54 = (f32[16,512]{1,0:T(8,128)S(1)}, f32[16,512]{1,0:T(8,128)}, u32[]{:S(2)}) copy-start(f32[16,512]{1,0:T(8,128)} %param.23) | copy-start | bytes 98308
  13.6 17.4 %copy-start.34 = (f32[16,2,256]{2,1,0:T(2,128)}, f32[16,2,256]{2,1,0:T(2,128)S(1)}, u32[]{:S(2)}) copy-start(f32[16,2,256]{2,1,0:T(2,128)S(1)} %reshape.567) | copy-start | bytes 98308
  14.0 18.5 %copy-start.61 = (f32[512]{0:T(512)}, f32[512]{0:T(512)S(1)}, u32[]{:S(2)}) copy-start(f32[512]{0:T(512)S(1)} %convert_element_type.131) | copy-start | bytes 6148
  15.8 16.7 %copy-start.65 = (f32[16]{0:T(128)}, f32[16]{0:T(128)S(1)}, u32[]{:S(2)}) copy-start(f32[16]{0:T(128)S(1)} %get-tuple-element.49) | copy-start | bytes 196
  15.8 17.9 %copy-start.74 = (s32[16]{0:T(128)}, s32[16]{0:T(128)S(1)}, u32[]{:S(2)}) copy-start(s32[16]{0:T(128)S(1)} %get-tuple-element.50) | copy-start | bytes 196
  16.0 16.4 %copy-start.48 = (f32[16,2]{1,0:T(8,128)}, f32[16,2]{1,0:T(8,128)S(1)}, u32[]{:S(2)}) copy-start(f32[16,2]{1,0:T(8,128)S(1)} %get-tuple-element.27) | copy-start | bytes 388
  16.1 16.4 %copy-start.69 = (f32[16]{0:T(128)}, f32[16]{0:T(128)S(1)}, u32[]{:S(2)}) copy-start(f32[16]{0:T(128)S(1)} %get-tuple-element.77) | copy-start | bytes 196
  16.6 15.9 %copy-start.39 = (f32[2,8,2,256]{3,1,2,0:T(8,128)}, f32[2,8,2,256]{3,1,2,0:T(8,128)S(1)}, u32[]{:S(2)}) copy-start(f32[2,8,2,256]{3,1,2,0:T(8,128)S(1)} %copy.205) | copy-start | bytes 98308
  32.5 21.7 %copy-start.20 = (bf16[1024,8]{1,0:T(8,128)(2,1)}, bf16[1024,8]{1,0:T(8,128)(2,1)S(1)}, u32[]{:S(2)}) copy-start(bf16[1024,8]{1,0:T(8,128)(2,1)S(1)} %get-tuple-element.73) | copy-start | bytes 49156
  33.0 145.1 %copy-start.3 = (f32[1024,512]{0,1:T(8,128)}, f32[1024,512]{0,1:T(8,128)S(1)}, u32[]{:S(2)}) copy-start(f32[1024,512]{0,1:T(8,128)S(1)} %get-tuple-element.79) | copy-start | bytes 6291460
  180.5 17.5 %copy-start.8 = (f32[1024,512]{0,1:T(8,128)}, f32[1024,512]{0,1:T(8,128)S(1)}, u32[]{:S(2)}) copy-start(f32[1024,512]{0,1:T(8,128)S(1)} %get-tuple-element.83) | copy-start | bytes 6291460
  180.5 17.5 %copy-start.50 = (f32[1024]{0:T(1024)}, f32[1024]{0:T(1024)S(1)}, u32[]{:S(2)}) copy-start(f32[1024]{0:T(1024)S(1)} %add_rsqrt_fusion.1) | copy-start | bytes 12292
  229.2 110.3 %reduce-scatter.3.cloned.1.call-start = ((), (), s32[]{:S(2)}) async-start(), calls=%async_computation.2 | async-start | bytes 4587520 | tf_op jit(solution)/shard_map/reduce_scatter | solution.py:307
  253.7 6.6 %copy-start.62 = (f32[512]{0:T(512)S(1)}, f32[512]{0:T(512)}, u32[]{:S(2)}) copy-start(f32[512]{0:T(512)} %copy-done.61) | copy-start | bytes 6148
  253.7 6.6 %copy-start.68 = (f32[1024]{0:T(1024)S(1)}, f32[1024]{0:T(1024)}, u32[]{:S(2)}) copy-start(f32[1024]{0:T(1024)} %add_rsqrt_fusion.2) | copy-start | bytes 12292
  253.7 6.6 %copy-start.73 = (f32[512]{0:T(512)S(1)}, f32[512]{0:T(512)}, u32[]{:S(2)}) copy-start(f32[512]{0:T(512)} %convert_element_type.132) | copy-start | bytes 6148
  260.4 7.1 %copy-start.89 = (bf16[1024,1024]{1,0:T(8,128)(2,1)S(1)}, bf16[1024,1024]{1,0:T(8,128)(2,1)}, u32[]{:S(2)}) copy-start(bf16[1024,1024]{1,0:T(8,128)(2,1)} %copy-done.88) | copy-start | bytes 6291460
  272.4 136.7 %all-reduce.4.cloned.1.call-start = ((), (), s32[]{:S(2)}) async-start(), calls=%async_computation.6 | async-start | bytes 5242880 | tf_op jit(solution)/shard_map/psum | solution.py:313
  286.6 55.5 %copy-start.57 = (f32[16,2]{1,0:T(8,128)}, f32[16,2]{1,0:T(8,128)S(1)}, u32[]{:S(2)}) copy-start(f32[16,2]{1,0:T(8,128)S(1)} %multiply_add_fusion.4) | copy-start | bytes 388
  290.1 53.3 %copy-start.14 = (f32[1024,8]{1,0:T(8,128)S(1)}, f32[1024,8]{1,0:T(8,128)}, u32[]{:S(2)}) copy-start(f32[1024,8]{1,0:T(8,128)} %copy.156) | copy-start | bytes 98308
  344.3 47.0 %copy-start.31 = (f32[16,512]{1,0:T(8,128)S(1)}, f32[16,512]{1,0:T(8,128)}, u32[]{:S(2)}) copy-start(f32[16,512]{1,0:T(8,128)} %param.20) | copy-start | bytes 98308
  344.3 47.0 %copy-start.38 = (s32[16,512]{1,0:T(8,128)S(1)}, s32[16,512]{1,0:T(8,128)}, u32[]{:S(2)}) copy-start(s32[16,512]{1,0:T(8,128)} %param.21) | copy-start | bytes 98308
  344.3 47.0 %copy-start.40 = (f32[2,8,2,256]{3,1,2,0:T(8,128)S(1)}, f32[2,8,2,256]{3,1,2,0:T(8,128)}, u32[]{:S(2)}) copy-start(f32[2,8,2,256]{3,1,2,0:T(8,128)} %copy-done.39) | copy-start | bytes 98308
  344.3 47.0 %copy-start.52 = (f32[16,512]{1,0:T(8,128)S(1)}, f32[16,512]{1,0:T(8,128)}, u32[]{:S(2)}) copy-start(f32[16,512]{1,0:T(8,128)} %reshape.578) | copy-start | bytes 98308
  345.3 46.1 %copy-start.53 = (f32[16,512]{1,0:T(8,128)S(1)}, f32[16,512]{1,0:T(8,128)}, u32[]{:S(2)}) copy-start(f32[16,512]{1,0:T(8,128)} %reshape.584) | copy-start | bytes 98308
  345.3 46.1 %copy-start.56 = (f32[2,8,2,256]{3,1,2,0:T(8,128)S(1)}, f32[2,8,2,256]{3,1,2,0:T(8,128)}, u32[]{:S(2)}) copy-start(f32[2,8,2,256]{3,1,2,0:T(8,128)} %copy.206) | copy-start | bytes 98308
  (63 other events, 201.6 us)
Sparse Core Ops, SparseCore 0:
  10.2 39.7 all-gather.7
  51.6 70.9 all-gather.5
  229.3 33.8 reduce-scatter.4
  272.5 66.9 reduce-scatter.2
  342.7 66.2 all-reduce.3

commit v2 on v0

v2 whole, which is shorter than its diff:
```python
import functools
import math

import jax
import jax.numpy as jnp
from jax import lax
from jax.experimental import pallas as pl
from jax.experimental.pallas import tpu as pltpu
from jax.sharding import PartitionSpec as P

F32 = jnp.float32
BF16 = jnp.bfloat16
EPS = 1e-06
TILE = 256
MAX_DIST = 128


def bucket_cuts(buckets, length):
    half_count = buckets // 2
    exact_count = half_count // 2
    ids = []
    for distance in range(length):
        if distance < exact_count:
            ids.append(distance)
        else:
            ids.append(
                min(
                    half_count - 1,
                    exact_count
                    + int(
                        math.log(distance / exact_count)
                        / math.log(MAX_DIST / exact_count)
                        * (half_count - exact_count)
                    ),
                )
            )
    cuts = []
    for distance in range(1, length):
        cuts += [distance] * (ids[distance] - ids[distance - 1])
    return cuts, ids[-1]


def nt(left, right):
    return lax.dot_general(left, right, (((1,), (1,)), ((), ())), preferred_element_type=F32)


def nn(left, right):
    return jnp.dot(left, right, preferred_element_type=F32)


def tn(left, right):
    return lax.dot_general(left, right, (((0,), (0,)), ((), ())), preferred_element_type=F32)


def iota(shape, dim):
    return lax.broadcasted_iota(jnp.int32, shape, dim)


def fold8(values):
    return jnp.sum(values.reshape(values.shape[0] // 8, 8, values.shape[1]), axis=0)


def row_scale(values):
    return lax.rsqrt(jnp.mean(values * values, axis=-1, keepdims=True) + EPS)


def norm_back(grad_out, unit_rows, scale, gain_row):
    d_unit = grad_out * gain_row
    spread = jnp.mean(d_unit * unit_rows, axis=-1, keepdims=True)
    return scale * (d_unit - unit_rows * spread), fold8(grad_out * unit_rows)


class Layer:
    def __init__(self, **refs):
        self.__dict__.update(refs)

    def prepare(self, head_index):
        rows, steps = self.series.shape
        half = steps // 2
        length = self.pm.shape[0]
        patch = steps // length
        split_row = self.split[...].astype(F32)
        pick = iota((rows, split_row.shape[1]), 1) == (
            iota((rows, split_row.shape[1]), 0) + head_index * rows
        )
        split_col = jnp.sum(jnp.where(pick, split_row, 0.0), axis=1, keepdims=True)
        self.splitb[...] = jnp.broadcast_to(split_col, self.splitb.shape)
        obs = self.observed[...].astype(F32)
        series = self.series[...]
        low_half = iota((rows, steps), 1) < half

        def halves(values):
            return [
                jnp.sum(values[:, :half], axis=1, keepdims=True),
                jnp.sum(values[:, half:], axis=1, keepdims=True),
            ]

        def combine(sums):
            both = sums[0] + sums[1]
            return [split_col * one + (1.0 - split_col) * both for one in sums]

        def spread(pair):
            return jnp.where(low_half, pair[0], pair[1])

        self.halves, self.combine, self.spread = halves, combine, spread
        self.counts = combine(halves(obs))
        item_mean = [a / b for a, b in zip(combine(halves(obs * series)), self.counts)]
        centred = series - spread(item_mean)
        item_var = [a / b for a, b in zip(combine(halves(obs * centred * centred)), self.counts)]
        self.std = [jnp.sqrt(v + 1e-05) for v in item_var]
        std_full = spread(self.std)
        self.std_full, self.mean_full = std_full, spread(item_mean)
        normed = obs * centred / std_full
        self.normed[...] = normed
        self.normed_low[...] = normed.astype(BF16).astype(F32)
        self.dout_low[...] = (self.cot[...] * std_full).astype(BF16).astype(F32)
        self.pm[...] = (iota(self.pm.shape, 1) // patch == iota(self.pm.shape, 0)).astype(F32)
        fold = (iota(self.fold.shape, 1) % patch == iota(self.fold.shape, 0)).astype(BF16)
        self.fold[...] = fold
        pw = self.patch_w[...].astype(F32)
        self.ptile[...] = jnp.broadcast_to(
            pw[None], (self.ptile.shape[0] // patch, patch, pw.shape[1])
        ).reshape(self.ptile.shape).astype(BF16)
        self.htile[...] = nn(self.head_w[...], fold[:patch]).astype(BF16)
        hb = jnp.broadcast_to(self.head_b[...], (16, patch))
        self.hbias = nn(hb, fold[:patch])[0:1]

    def spread_rows(self, source, tile):
        rows_tile = TILE // self.pm.shape[0]
        mask = self.pm[...]
        pieces = [
            (source[pl.ds(tile * rows_tile + r, 1), :] * mask).astype(BF16)
            for r in range(rows_tile)
        ]
        return jnp.concatenate(pieces, axis=0)

    def gather_rows(self, target, tile, values, extra=None):
        length = self.pm.shape[0]
        mask = self.pm[...]
        for r in range(TILE // length):
            part = jnp.sum(values[r * length : (r + 1) * length] * mask, axis=0, keepdims=True)
            if extra is not None:
                part = part + extra
            target[pl.ds(tile * (TILE // length) + r, 1), :] = part

    def embed(self, tile):
        at = pl.ds(pl.multiple_of(tile * TILE, TILE), TILE)
        spread = self.spread_rows(self.normed_low, tile)
        self.p8t[:, at] = nt(self.fold[...], spread).astype(BF16)
        embedded = nn(spread, self.ptile[...]) + self.patch_b[...].astype(F32)
        self.embedded[at, :] = embedded
        scale = row_scale(embedded)
        self.s_attn[at, :] = scale
        self.attn_in[at, :] = (embedded * scale * self.gain_attn[...].astype(F32)).astype(BF16)

    def buckets(self):
        length = self.pm.shape[0]
        lanes = 2 * length
        key = iota((length, lanes), 0)
        query = iota((length, lanes), 1) % length
        offset = key - query
        distance = jnp.abs(offset)
        table = self.tab.shape[1]
        cuts, top = bucket_cuts(table, length)
        ids = jnp.where(offset > 0, table // 2, 0)
        for cut in cuts:
            ids = ids + (distance >= cut).astype(jnp.int32)
        used = list(range(top + 1)) + list(range(table // 2, table // 2 + top + 1))
        return ids, used

    def own_table(self):
        table = self.table[...].astype(F32)
        lane = iota((table.shape[0], 128), 1)
        self.tab[0] = jnp.where(lane < 64, table[:, 0:1], table[:, 1:2])

    def offsets(self, slot):
        ids, used = self.buckets()
        total = jnp.zeros(ids.shape, F32)
        for b in used:
            total = jnp.where(ids == b, self.tab[slot, b : b + 1, :], total)
        self.bias[slot] = total

    def head_masks(self):
        lane = iota((1, 128), 1)
        return (lane < 64).astype(BF16), (lane >= 64).astype(BF16)

    def attend(self, slot, tile):
        at = pl.ds(pl.multiple_of(tile * TILE, TILE), TILE)
        wide = pl.ds(pl.multiple_of(slot * 384, 128), 384)
        length = self.pm.shape[0]
        even, odd = self.head_masks()
        projected = nn(self.attn_in[at, :], self.wq[:, wide]).astype(BF16)
        self.qkv[at, wide] = projected
        bias = self.bias[slot]
        block = (
            iota(bias.shape, 0) // (length // 2) != (iota(bias.shape, 1) % length) // (length // 2)
        ).astype(F32) * -1e30
        contexts = []
        for r in range(TILE // length):
            rows = slice(r * length, (r + 1) * length)
            query, key, value = (projected[rows, i * 128 : (i + 1) * 128] for i in range(3))
            both = jnp.concatenate([query * even, query * odd], axis=0)
            split = self.splitb[pl.ds(tile * (TILE // length) + r, 1), :]
            scores = nt(key, both) + (bias + split * block)
            top = jnp.max(scores, axis=0, keepdims=True)
            raised = jnp.exp(scores - top)
            probs = raised * (1.0 / jnp.sum(raised, axis=0, keepdims=True))
            self.probs[slot, pl.ds(pl.multiple_of(tile * TILE + r * length, length), length), :] = (
                probs
            )
            mixed = tn(probs.astype(BF16), value)
            contexts.append(
                jnp.where(iota((1, 128), 1) < 64, mixed[:length], mixed[length:]).astype(BF16)
            )
        self.ctx[at, pl.ds(pl.multiple_of(slot * 128, 128), 128)] = jnp.concatenate(
            contexts, axis=0
        )

    def middle(self, tile):
        at = pl.ds(pl.multiple_of(tile * TILE, TILE), TILE)
        hidden_mid = self.embedded[at, :] + nt(self.ctx[at, :], self.wo[...])
        ff_scale = row_scale(hidden_mid)
        ff_unit = hidden_mid * ff_scale
        gain_ff = self.gain_ff[...].astype(F32)
        ff_in = (ff_unit * gain_ff).astype(BF16)
        self.ff_in[at, :] = ff_in
        slots = self.slots
        ff_out = None
        keep = []
        for s in range(slots):
            w = self.wg.shape[1] // slots
            gu = nn(ff_in, self.wg[:, s * w : (s + 1) * w])
            gate, up = gu[:, : w // 2], gu[:, w // 2 :]
            c = math.sqrt(2.0 / math.pi)
            square = gate * gate
            t = jnp.tanh(gate * (c + (c * 0.044715) * square))
            plus = 0.5 * (1.0 + t)
            act = gate * plus
            slope = plus + (0.5 * gate) * (1.0 - t * t) * (c + (3.0 * c * 0.044715) * square)
            inner = (act * up).astype(BF16)
            cols = slice(s * (w // 2), (s + 1) * (w // 2))
            self.inner[at, cols] = inner
            self.act[:, cols] = act.astype(BF16)
            self.slope[:, cols] = (up * slope).astype(BF16)
        ff_out = nt(self.inner[at, :], self.wd[...])
        hidden_end = hidden_mid + ff_out
        final_scale = row_scale(hidden_end)
        final_unit = hidden_end * final_scale
        gain_final = self.gain_final[...].astype(F32)
        final_in = (final_unit * gain_final).astype(BF16)
        self.final_in[at, :] = final_in
        self.gather_rows(self.output, tile, nn(final_in, self.htile[...]), self.hbias)
        d_spread = self.spread_rows(self.dout_low, tile)
        self.d8t[:, at] = nt(self.fold[...], d_spread).astype(BF16)
        d_final = nt(d_spread, self.htile[...])
        d_end, gain_part = norm_back(d_final, final_unit, final_scale, gain_final)
        self.g_final[...] += gain_part
        d_low = d_end.astype(BF16)
        self.d_end_low[at, :] = d_low
        d_in = None
        for s in range(slots):
            w = self.wg.shape[1] // slots
            cols = slice(s * (w // 2), (s + 1) * (w // 2))
            d_inner = nn(d_low, self.wd[:, cols])
            d_gate = (d_inner * self.slope[:, cols].astype(F32)).astype(BF16)
            d_up = (d_inner * self.act[:, cols].astype(F32)).astype(BF16)
            self.dgu[at, s * w : s * w + w // 2] = d_gate
            self.dgu[at, s * w + w // 2 : (s + 1) * w] = d_up
        d_in = nt(self.dgu[at, :], self.wg[...])
        d_norm, gain_part = norm_back(d_in, ff_unit, ff_scale, gain_ff)
        self.g_ff[...] += gain_part
        d_mid = d_end + d_norm
        self.d_mid[at, :] = d_mid
        d_mid_low = d_mid.astype(BF16)
        self.d_mid_low[at, :] = d_mid_low
        self.d_ctx[at, :] = nn(d_mid_low, self.wo[...]).astype(BF16)

    def attend_back(self, slot, tile):
        length = self.pm.shape[0]
        even, odd = self.head_masks()
        total = jnp.zeros((length, 128), F32)
        for r in range(TILE // length):
            rows = pl.ds(pl.multiple_of(tile * TILE + r * length, length), length)

            def part(i):
                return self.qkv[rows, pl.ds(pl.multiple_of(slot * 384 + i * 128, 128), 128)]

            query, key, value = part(0), part(1), part(2)
            d_ctx = self.d_ctx[rows, pl.ds(pl.multiple_of(slot * 128, 128), 128)]
            query_both = jnp.concatenate([query * even, query * odd], axis=0)
            d_both = jnp.concatenate([d_ctx * even, d_ctx * odd], axis=0)
            probs = self.probs[slot, rows, :]
            d_probs = nt(value, d_both)
            d_value = nn(probs.astype(BF16), d_both)
            dots = jnp.sum(probs * d_probs, axis=0, keepdims=True)
            d_scores = (probs * (d_probs - dots)).astype(BF16)
            total = total + d_scores.astype(F32)
            d_key = nn(d_scores, query_both)
            mixed = tn(d_scores, key)
            d_query = jnp.where(iota((1, 128), 1) < 64, mixed[:length], mixed[length:])
            for i, grad in enumerate((d_query, d_key, d_value)):
                self.dqkv[rows, pl.ds(pl.multiple_of(slot * 384 + i * 128, 128), 128)] = (
                    grad.astype(BF16)
                )
        self.dsum[slot] += total

    def embed_back(self, tile):
        at = pl.ds(pl.multiple_of(tile * TILE, TILE), TILE)
        d_in = nt(self.dqkv[at, :], self.wq[...])
        scale = self.s_attn[at, :]
        d_norm, gain_part = norm_back(
            d_in, self.embedded[at, :] * scale, scale, self.gain_attn[...].astype(F32)
        )
        self.g_attn[...] += gain_part
        d_embedded = (self.d_mid[at, :] + d_norm).astype(BF16)
        self.d_emb[at, :] = d_embedded
        self.g_bias[...] += fold8(d_embedded.astype(F32))
        self.gather_rows(self.d_normed, tile, nt(d_embedded, self.ptile[...]))

    def finish(self):
        obs = self.observed[...].astype(F32)
        cot = self.cot[...]
        output = self.output[...]
        std_full, mean_full = self.std_full, self.mean_full
        self.rebuilt[...] = output * std_full + mean_full
        d_normed = self.d_normed[...]
        std_grad = [
            a - b / c
            for a, b, c in zip(
                self.halves(cot * output), self.halves(d_normed * self.normed[...]), self.std
            )
        ]
        var_weight = self.combine(
            [g / (2.0 * s) / n for g, s, n in zip(std_grad, self.std, self.counts)]
        )
        centred = self.series[...] - mean_full
        d_centred = d_normed * obs / std_full + 2.0 * obs * centred * self.spread(var_weight)
        mean_grad = [a - b for a, b in zip(self.halves(cot), self.halves(d_centred))]
        mean_weight = self.combine([g / n for g, n in zip(mean_grad, self.counts)])
        self.series_grad[...] = d_centred + obs * self.spread(mean_weight)

    def small_grads(self, head_index):
        small = self.small
        heads = self.slots
        zero = jnp.zeros((4, self.embedded.shape[1]), F32)
        small[0:8, :] = jnp.concatenate(
            [jnp.sum(r[...], axis=0, keepdims=True) for r in (self.g_attn, self.g_ff, self.g_final, self.g_bias)]
            + [zero],
            axis=0,
        )
        small[8:16, :] = nn(self.p8t[...], self.d_emb[...])[0:8]
        small[16:24, :] = nn(self.d8t[...], self.final_in[...])[0:8]
        lane = iota((8, 128), 1)
        groups = self.tab.shape[1] // 8
        pieces = [jnp.zeros((8, 128), F32) for _ in range(groups)]
        pieces[0] = jnp.where(
            lane == 2 * heads, jnp.sum(self.d8t[0:8, :].astype(F32), axis=1, keepdims=True), 0.0
        )
        ids, used = self.buckets()
        for s in range(self.slots):
            dsum = self.dsum[s]
            owner = lax.rem(head_index + s, heads)
            for b in range(self.tab.shape[1]):
                if b in used:
                    self.tgr[b : b + 1, :] = jnp.sum(
                        jnp.where(ids == b, dsum, 0.0), axis=0, keepdims=True
                    )
                else:
                    self.tgr[b : b + 1, :] = jnp.zeros((1, 128), F32)
            for g in range(groups):
                rows = self.tgr[8 * g : 8 * g + 8, :]
                for which in range(2):
                    inside = (lane < 64) if which == 0 else (lane >= 64)
                    column = jnp.sum(jnp.where(inside, rows, 0.0), axis=1, keepdims=True)
                    pieces[g] = pieces[g] + jnp.where(lane == 2 * owner + which, column, 0.0)
        small[24:32, :] = jnp.concatenate(pieces, axis=1)

    def small_out(self, head_index):
        small = self.small
        for row, out in enumerate((self.o_attn, self.o_ff, self.o_final, self.o_pb)):
            out[...] = small[row : row + 1, :]
        self.o_pw[...] = small[8:16, :]
        patch = self.o_pw.shape[0]
        block = jnp.concatenate(
            [small[16:24, :], jnp.zeros((120, small.shape[1]), F32)], axis=0
        )
        self.o_hw[...] = block.T[:, :patch]
        lane = iota((8, 128), 1)
        column = jnp.sum(
            jnp.where(lane == 2 * self.slots, small[24:32, 0:128], 0.0), axis=1, keepdims=True
        )
        self.o_hb[...] = jnp.sum(jnp.where(lane == iota((8, 128), 0), column, 0.0), axis=0, keepdims=True)[
            :, :patch
        ]
        for g in range(self.tab.shape[1] // 8):
            piece = small[24:32, g * 128 : (g + 1) * 128]
            columns = [
                jnp.sum(
                    jnp.where(lane == 2 * head_index + which, piece, 0.0), axis=1, keepdims=True
                )
                for which in range(2)
            ]
            self.o_table[8 * g : 8 * g + 8, :] = jnp.where(
                iota((8, 2), 1) == 0, columns[0], columns[1]
            )

    def clear(self):
        for ref in (self.g_attn, self.g_ff, self.g_final, self.g_bias):
            ref[...] = jnp.zeros(ref.shape, F32)
        self.dsum[...] = jnp.zeros(self.dsum.shape, F32)


MESH = pl.DeviceIdType.MESH


class Net:
    def __init__(self, groups, heads, send_sems, recv_sems):
        self.dp, self.head = lax.axis_index("dp"), lax.axis_index("head")
        self.bits = groups.bit_length() - 1
        self.heads = heads
        self.send_sems, self.recv_sems = send_sems, recv_sems
        self.used = 0
        self.sent = []

    def bit(self, which):
        return (self.dp // (1 << which)) % 2

    def across(self, which):
        step = 1 << which
        return (self.dp + (1 - 2 * self.bit(which)) * step, self.head)

    def beside(self, hops):
        return (self.dp, (self.head + hops) % self.heads)

    def beside_bit(self, which):
        step = 1 << which
        mine = (self.head // step) % 2
        return (self.dp, self.head + (1 - 2 * mine) * step)

    def greet_start(self):
        barrier = pltpu.get_barrier_semaphore()
        partners = [self.across(b) for b in range(self.bits)]
        partners += [self.beside(t) for t in range(1, self.heads)]
        for partner in partners:
            pl.semaphore_signal(barrier, inc=1, device_id=partner, device_id_type=MESH)

    def greet_end(self):
        pl.semaphore_wait(pltpu.get_barrier_semaphore(), self.bits + self.heads - 1)

    def claim(self):
        self.used += 1
        return self.used - 1

    def copy(self, index, src, dst, device):
        return pltpu.make_async_remote_copy(
            src_ref=src,
            dst_ref=dst,
            send_sem=self.send_sems.at[index],
            recv_sem=self.recv_sems.at[index],
            device_id=device,
            device_id_type=MESH,
        )

    def send(self, index, src, dst, device):
        copy = self.copy(index, src, dst, device)
        copy.start()
        self.sent.append(copy)

    def arrived(self, index, dst, device):
        self.copy(index, dst, dst, device).wait_recv()

    def drain(self):
        for copy in self.sent:
            copy.wait_send()
        self.sent = []


def rows_at(start, count, unit):
    return pl.ds(pl.multiple_of(start, unit), count)


class Gather:
    ORDERS = ((1, 2, 0), (2, 1, 0))

    def __init__(self, net, ref):
        self.net, self.ref = net, ref
        self.heads = net.heads
        self.width = ref.shape[1] // self.heads
        self.unit = ref.shape[0] // 16
        self.ids = [[net.claim() for _ in range(net.heads - 1 + 3)] for _ in range(2)]

    def block(self, half):
        bits = [self.net.bit(b) for b in self.ORDERS[half]]
        return bits[0] + 2 * bits[1] + 4 * bits[2]

    def span(self, half, level, mine=True):
        size = 1 << level
        first = self.block(half) // size
        if not mine:
            first = first + 1 - 2 * (first % 2)
        return rows_at((half * 8 + first * size) * self.unit, size * self.unit, self.unit)

    def start(self):
        net, width = self.net, self.width
        for half in range(2):
            rows = self.span(half, 0)
            for t in range(1, self.heads):
                slot = self.heads - t
                net.send(
                    self.ids[half][t - 1],
                    self.ref.at[rows, 0:width],
                    self.ref.at[rows, slot * width : (slot + 1) * width],
                    net.beside(t),
                )

    def step(self, level):
        net, width = self.net, self.width
        others = pl.ds(width, (self.heads - 1) * width)
        for half in range(2):
            if level == 0:
                for t in range(1, self.heads):
                    slot = self.heads - t
                    net.arrived(
                        self.ids[half][t - 1],
                        self.ref.at[self.span(half, 0), slot * width : (slot + 1) * width],
                        net.beside(t),
                    )
            else:
                net.arrived(
                    self.ids[half][self.heads - 2 + level],
                    self.ref.at[self.span(half, level - 1, mine=False), others],
                    net.across(self.ORDERS[half][level - 1]),
                )
            if level < 3:
                rows = self.span(half, level)
                net.send(
                    self.ids[half][self.heads - 1 + level],
                    self.ref.at[rows, others],
                    self.ref.at[rows, others],
                    net.across(self.ORDERS[half][level]),
                )


class Reduce:
    ORDERS = ((1, 2), (2, 1))

    def __init__(self, net, refs, columns, width):
        self.net = net
        self.heads = net.heads
        self.width = width
        self.columns = columns
        (
            self.own, self.snd0, self.rcv0, self.snd1, self.rcv1,
            self.snd2, self.rcv2, self.sndz, self.rcvz, self.fin,
        ) = refs
        self.ids = {}

    def id(self, name):
        if name not in self.ids:
            self.ids[name] = self.net.claim()
        return self.ids[name]

    def slots(self, s):
        first = self.columns.start + s * self.width
        return slice(first, first + self.width)

    @property
    def fin_columns(self):
        first = self.columns.start // self.heads
        return slice(first, first + self.width)

    def produce(self, left_t, right, block=512):
        net = self.net
        count = self.own.shape[0]
        core = net.bit(0)
        wide = self.columns.stop - self.columns.start
        for c in range(0, wide, block):
            cols = slice(self.columns.start + c, self.columns.start + c + block)
            self.snd0[:, cols] = nn(
                left_t[rows_at((1 - core) * count, count, count), :], right[:, c : c + block]
            ).astype(BF16)
        net.send(
            self.id("r0"), self.snd0.at[:, self.columns], self.rcv0.at[:, self.columns], net.across(0)
        )
        for c in range(0, wide, block):
            cols = slice(self.columns.start + c, self.columns.start + c + block)
            self.own[:, cols] = nn(
                left_t[rows_at(core * count, count, count), :], right[:, c : c + block]
            )

    def halving(self, level):
        net, cols = self.net, self.columns
        source = (self.rcv0, self.rcv1, self.rcv2)[level]
        count = self.own.shape[0] // 2 >> level
        if level == 0:
            net.arrived(self.id("r0"), self.rcv0.at[:, cols], net.across(0))
        for half in range(2):
            first = half * count
            if level > 0:
                net.arrived(
                    self.id(f"r{level}{half}"),
                    source.at[first : first + count, cols],
                    net.across(self.ORDERS[half][level - 1]),
                )
            at = self.kept(half, level)
            if level < 2:
                bit = net.bit(self.ORDERS[half][level])
                away = (1 - bit) * (count // 2)
                send, target = ((self.snd1, self.rcv1), (self.snd2, self.rcv2))[level]
                place = slice(half * (count // 2), (half + 1) * (count // 2))
                send[place, cols] = (
                    self.own[rows_at(at + away, count // 2, 32), cols]
                    + source[rows_at(first + away, count // 2, 32), cols].astype(F32)
                ).astype(BF16)
                net.send(
                    self.id(f"r{level + 1}{half}"),
                    send.at[place, cols],
                    target.at[place, cols],
                    net.across(self.ORDERS[half][level]),
                )
        for half in range(2):
            at = self.kept(half, level)
            first = half * count
            if level < 2:
                bit = net.bit(self.ORDERS[half][level])
                stay = bit * (count // 2)
                rows = rows_at(at + stay, count // 2, 32)
                self.own[rows, cols] = self.own[rows, cols] + source[
                    rows_at(first + stay, count // 2, 32), cols
                ].astype(F32)
            else:
                rows = rows_at(at, count, 32)
                total = self.own[rows, cols] + source[first : first + count, cols].astype(F32)
                self.own[rows, cols] = total
                if net.bits <= 3:
                    self.sndz[first : first + count, cols] = total.astype(BF16)

    def kept(self, half, level):
        count = self.own.shape[0] // 2
        start = half * count
        for step in range(level):
            count = count // 2
            start = start + self.net.bit(self.ORDERS[half][step]) * count
        return start

    def groups(self):
        net, cols = self.net, self.columns
        count = self.sndz.shape[0] // 2
        for bit in range(3, net.bits):
            inbox = self.extra.at[bit - 3]
            key = f"g{bit}"
            for half in range(2):
                rows = rows_at(self.kept(half, 2), count, 32)
                self.sndz[half * count : (half + 1) * count, cols] = self.own[rows, cols].astype(
                    BF16
                )
            copy = net.copy(
                self.id(key), self.sndz.at[:, cols], inbox.at[:, cols], net.across(bit)
            )
            copy.start()
            copy.wait()
            for half in range(2):
                rows = rows_at(self.kept(half, 2), count, 32)
                place = slice(half * count, (half + 1) * count)
                self.own[rows, cols] = self.sndz[place, cols].astype(F32) + inbox[
                    place, cols
                ].astype(F32)
        if net.bits > 3:
            for half in range(2):
                rows = rows_at(self.kept(half, 2), count, 32)
                self.sndz[half * count : (half + 1) * count, cols] = self.own[rows, cols].astype(
                    BF16
                )

    def owners(self):
        net = self.net
        for s in range(1, self.heads):
            net.send(
                self.id(f"z{s}"),
                self.sndz.at[:, self.slots(s)],
                self.rcvz.at[s - 1, :, self.fin_columns],
                net.beside(s),
            )

    def place(self, half, level, mine=True):
        net = self.net
        quarter = self.fin.shape[0] // 4
        count = quarter // 4
        start = net.bit(0) * 2 * quarter + half * quarter
        order = self.ORDERS[half]
        if level == 0:
            inner = net.bit(order[1]) if mine else 1 - net.bit(order[1])
            start = start + net.bit(order[0]) * 2 * count + inner * count
            return rows_at(start, count, count)
        outer = net.bit(order[0]) if mine else 1 - net.bit(order[0])
        return rows_at(start + outer * 2 * count, 2 * count, count)

    def owned(self):
        net = self.net
        fin = self.fin_columns
        count = self.sndz.shape[0] // 2
        for s in range(1, self.heads):
            net.arrived(self.id(f"z{s}"), self.rcvz.at[s - 1, :, fin], net.beside(s))
        for half in range(2):
            part = slice(half * count, (half + 1) * count)
            total = self.own[rows_at(self.kept(half, 2), count, 32), self.slots(0)]
            for s in range(1, self.heads):
                total = total + self.rcvz[s - 1, part, fin].astype(F32)
            rows = self.place(half, 0)
            self.fin[rows, fin] = total.astype(BF16)
            net.send(
                self.id(f"f0{half}"),
                self.fin.at[rows, fin],
                self.fin.at[rows, fin],
                net.across(self.ORDERS[half][1]),
            )

    def spread(self, level):
        net, fin = self.net, self.fin_columns
        if level < 2:
            for half in range(2):
                net.arrived(
                    self.id(f"f{level}{half}"),
                    self.fin.at[self.place(half, level, mine=False), fin],
                    net.across(self.ORDERS[half][1 - level]),
                )
                if level == 0:
                    rows = self.place(half, 1)
                    net.send(
                        self.id(f"f1{half}"),
                        self.fin.at[rows, fin],
                        self.fin.at[rows, fin],
                        net.across(self.ORDERS[half][0]),
                    )
        half_rows = self.fin.shape[0] // 2
        core = net.bit(0)
        if level == 1:
            rows = rows_at(core * half_rows, half_rows, half_rows)
            net.send(
                self.id("f2"), self.fin.at[rows, fin], self.fin.at[rows, fin], net.across(0)
            )
        if level == 2:
            rows = rows_at((1 - core) * half_rows, half_rows, half_rows)
            net.arrived(self.id("f2"), self.fin.at[rows, fin], net.across(0))

    def steps(self):
        return [
            lambda: self.halving(0),
            lambda: self.halving(1),
            lambda: (self.halving(2), self.groups(), self.owners()),
            self.owned,
            lambda: self.spread(0),
            lambda: self.spread(1),
            lambda: self.spread(2),
        ]


class Total:
    def __init__(self, net, slabs, inbox):
        self.net, self.slabs, self.inbox = net, slabs, inbox
        self.partners = [net.across(b) for b in range(net.bits)]
        self.partners += [net.beside_bit(b) for b in range(net.heads.bit_length() - 1)]
        self.ids = [net.claim() for _ in self.partners]

    def start(self, level):
        self.net.send(
            self.ids[level], self.slabs.at[level], self.inbox.at[level], self.partners[level]
        )

    def step(self, level):
        self.net.arrived(self.ids[level], self.inbox.at[level], self.partners[level])
        self.slabs[level + 1] = self.slabs[level] + self.inbox[level]
        if level + 1 < len(self.partners):
            self.start(level + 1)


def loop(count, body):
    def once(i, carry):
        body(i)
        return carry

    lax.fori_loop(0, count, once, 0)


INPUTS = (
    "series", "observed", "split", "cot", "gain_attn", "gain_ff", "gain_final", "patch_w", "patch_b", "wq_in", "wk_in", "wv_in", "wo_in", "table", "wg_in", "wu_in", "wd_in", "head_w", "head_b",
)
OUTPUTS = (
    "rebuilt", "series_grad", "o_attn", "o_ff", "o_final", "o_pw", "o_pb", "o_q", "o_k", "o_v", "o_o", "o_table", "o_g", "o_u", "o_d", "o_hw", "o_hb",
)
SHARED = (
    "own", "snd0", "rcv0", "snd1", "rcv1", "snd2", "rcv2", "sndz", "rcvz", "fin",
)


def layer_kernel(groups, heads, names, *refs):
    named = dict(zip(names, refs))
    dgu = named["dgu"]
    wq, wo, wg, wd = (named[k] for k in ("wq", "wo", "wg", "wd"))
    named["dqkv"] = dgu.at[:, 0 : wq.shape[1]]
    named["d_emb"] = named["ff_in"]
    named["fin"] = wg.at[:, 0 : named["rcvz"].shape[2]]
    layer = Layer(slots=heads, **named)
    tiles = layer.embedded.shape[0] // TILE
    net = Net(groups, heads, named["send_sems"], named["recv_sems"])
    net.greet_start()
    part = layer.wq_in.shape[1]
    for i, ref in enumerate((layer.wq_in, layer.wk_in, layer.wv_in)):
        wq[:, i * part : (i + 1) * part] = ref[...]
    wo[:, 0 : layer.wo_in.shape[0]] = layer.wo_in[...].T
    part = layer.wg_in.shape[1]
    for i, ref in enumerate((layer.wg_in, layer.wu_in)):
        wg[:, i * part : (i + 1) * part] = ref[...]
    wd[:, 0 : layer.wd_in.shape[0]] = layer.wd_in[...].T
    layer.own_table()
    net.greet_end()
    gather_q, gather_o, gather_g, gather_d = (Gather(net, ref) for ref in (wq, wo, wg, wd))
    table_ids = [net.claim() for _ in range(heads - 1)]
    gather_q.start()
    for t in range(1, heads):
        net.send(table_ids[t - 1], layer.tab.at[0], layer.tab.at[heads - t], net.beside(t))
    gather_o.start()
    gather_g.start()
    gather_d.start()
    layer.clear()
    layer.prepare(net.head)
    loop(tiles, layer.embed)
    layer.offsets(0)
    gather_q.step(0)
    loop(tiles // 2, lambda t: layer.attend(0, t))
    gather_o.step(0)
    gather_q.step(1)
    loop(tiles // 2, lambda t: layer.attend(0, t + tiles // 2))
    gather_g.step(0)
    gather_o.step(1)
    gather_q.step(2)
    for t in range(1, heads):
        net.arrived(table_ids[t - 1], layer.tab.at[heads - t], net.beside(t))
    loop(heads - 1, lambda s: layer.offsets(s + 1))
    gather_d.step(0)
    gather_g.step(1)
    gather_q.step(3)
    loop(tiles, lambda t: layer.attend(1, t))
    gather_o.step(2)
    gather_d.step(1)
    gather_g.step(2)
    loop(tiles, lambda t: layer.attend(2, t))
    gather_o.step(3)
    gather_d.step(2)
    gather_g.step(3)
    loop(tiles, lambda t: layer.attend(3, t))
    gather_d.step(3)
    net.drain()
    loop(tiles, layer.middle)
    shared = [named[k] for k in SHARED]
    bounds = {}
    first = 0
    for key, ref in zip("qogd", (wq, wo, wg, wd)):
        bounds[key] = slice(first, first + ref.shape[1])
        first += ref.shape[1]
    reduce = {
        key: Reduce(net, shared, bounds[key], ref.shape[1] // heads)
        for key, ref in zip("qogd", (wq, wo, wg, wd))
    }
    for one in reduce.values():
        one.extra = named.get("extra")
    left, right = layer.left_t, layer.right_t
    left[...] = layer.ff_in[...].T
    reduce["g"].produce(left, dgu)
    right[...] = layer.d_end_low[...].T
    reduce["d"].produce(right, layer.inner)
    left[...] = layer.d_mid_low[...].T
    reduce["o"].produce(left, layer.ctx)
    right[...] = layer.attn_in[...].T
    pending = []
    steps = {key: reduce[key].steps() for key in "god"}
    for level in range(7):
        pending += [steps[key][level] for key in "gdo"]

    def advance(count):
        for _ in range(min(count, len(pending))):
            pending.pop(0)()

    for s in range(heads):
        advance(2)
        loop(tiles // 2, lambda t: layer.attend_back(s, t))
        advance(3)
        loop(tiles // 2, lambda t: layer.attend_back(s, t + tiles // 2))
    reduce["q"].produce(right, named["dqkv"])
    advance(1)
    loop(tiles, layer.embed_back)
    last = reduce["q"].steps()
    last[0]()
    layer.small = named["slabs"].at[0]
    layer.small_grads(net.head)
    total = Total(net, named["slabs"], named["inbox"])
    total.start(0)
    last[1]()
    layer.finish()
    total.step(0)
    last[2]()
    advance(len(pending))
    levels = len(total.partners)
    total.step(1)
    last[3]()
    total.step(2)
    last[4]()
    total.step(3)
    last[5]()
    fin = named["fin"]
    ff = layer.o_g.shape[1]
    layer.o_o[...] = fin[:, 3 * 128 : 4 * 128].astype(F32).T
    layer.o_g[...] = fin[:, 512 : 512 + ff].astype(F32)
    layer.o_u[...] = fin[:, 512 + ff : 512 + 2 * ff].astype(F32)
    layer.o_d[...] = fin[:, 512 + 2 * ff :].astype(F32).T
    for level in range(4, levels):
        total.step(level)
    layer.small = named["slabs"].at[levels]
    layer.small_out(net.head)
    last[6]()
    for i, out in enumerate((layer.o_q, layer.o_k, layer.o_v)):
        out[...] = fin[:, i * 128 : (i + 1) * 128].astype(F32)
    net.drain()


def layer_call(groups, heads, args):
    series = args[0]
    rows, steps = series.shape
    patch, width = args[7].shape
    length = steps // patch
    tokens = rows * length
    part = args[9].shape[1]
    ff = args[14].shape[1]
    table_rows, table_heads = args[13].shape
    total = heads * (4 * part + 3 * ff)
    bits = groups.bit_length() - 1
    levels = bits + heads.bit_length() - 1
    scratch = dict(
        pm=((length, steps), F32), fold=((16, steps), BF16), ptile=((steps, width), BF16),
        htile=((width, steps), BF16), splitb=((rows, 128), F32), normed=((rows, steps), F32),
        normed_low=((rows, steps), F32), dout_low=((rows, steps), F32), output=((rows, steps), F32),
        d_normed=((rows, steps), F32), p8t=((16, tokens), BF16), d8t=((16, tokens), BF16),
        embedded=((tokens, width), F32), s_attn=((tokens, 1), F32), attn_in=((tokens, width), BF16),
        qkv=((tokens, heads * 3 * part), BF16), tab=((heads, table_rows, 128), F32),
        bias=((heads, length, 128), F32), probs=((heads, tokens, 128), F32),
        ctx=((tokens, heads * part), BF16), ff_in=((tokens, width), BF16),
        inner=((tokens, heads * ff), BF16), act=((TILE, heads * ff), BF16),
        slope=((TILE, heads * ff), BF16), final_in=((tokens, width), BF16),
        d_end_low=((tokens, width), BF16), dgu=((tokens, heads * 2 * ff), BF16),
        d_mid=((tokens, width), F32), d_mid_low=((tokens, width), BF16),
        d_ctx=((tokens, heads * part), BF16), dsum=((heads, length, 128), F32),
        g_attn=((8, width), F32), g_ff=((8, width), F32),
        g_final=((8, width), F32), g_bias=((8, width), F32), tgr=((table_rows, 128), F32),
        left_t=((width, tokens), BF16), right_t=((width, tokens), BF16),
        wq=((width, heads * 3 * part), BF16), wo=((width, heads * part), BF16),
        wg=((width, heads * 2 * ff), BF16), wd=((width, heads * ff), BF16),
        own=((width // 2, total), F32), snd0=((width // 2, total), BF16),
        rcv0=((width // 2, total), BF16), snd1=((width // 4, total), BF16),
        rcv1=((width // 4, total), BF16), snd2=((width // 8, total), BF16),
        rcv2=((width // 8, total), BF16), sndz=((width // 8, total), BF16),
        rcvz=((heads - 1, width // 8, total // heads), BF16),
        slabs=((levels + 1, 32, width), F32), inbox=((levels, 32, width), F32),
    )
    if bits > 3:
        scratch["extra"] = ((bits - 3, width // 8, total), BF16)
    copies = 4 * 2 * (heads - 1 + 3) + heads - 1 + 4 * (10 + heads - 1 + 2 * (bits - 3)) + levels
    outs = [
        (rows, steps), (rows, steps), (1, width), (1, width), (1, width), (patch, width), (1, width),
        (width, part), (width, part), (width, part), (part, width), (table_rows, table_heads),
        (width, ff), (width, ff), (ff, width), (width, patch), (1, patch),
    ]
    names = list(INPUTS + OUTPUTS) + list(scratch) + ["send_sems", "recv_sems"]
    vmem = pl.BlockSpec(memory_space=pltpu.VMEM)
    return pl.pallas_call(
        functools.partial(layer_kernel, groups, heads, names),
        out_shape=[jax.ShapeDtypeStruct(shape, F32) for shape in outs],
        in_specs=[vmem] * len(INPUTS),
        out_specs=[vmem] * len(OUTPUTS),
        scratch_shapes=[pltpu.VMEM(*v) for v in scratch.values()]
        + [pltpu.SemaphoreType.DMA((copies,)), pltpu.SemaphoreType.DMA((copies,))],
        compiler_params=pltpu.CompilerParams(
            collective_id=0, has_side_effects=True, vmem_limit_bytes=61 * 1024 * 1024
        ),
    )(*args)


def solution(mesh):
    groups, heads = mesh.shape["dp"], mesh.shape["head"]

    def local(*args):
        args = list(args)
        for i in (2, 4, 5, 6, 8, 18):
            args[i] = args[i].reshape(1, -1)
        outs = list(layer_call(groups, heads, args))
        for i in (2, 3, 4, 6, 16):
            outs[i] = outs[i].reshape(-1)
        return tuple(outs)

    both = P(("dp", "head"), None)
    by_column, by_row = P(None, "head"), P("head", None)
    return jax.shard_map(
        local,
        mesh=mesh,
        in_specs=(both, both, P("dp"), both) + (P(),) * 5 + (by_column,) * 3
        + (by_row, by_column, by_column, by_column, by_row, P(), P()),
        out_specs=(both, both) + (P(),) * 5 + (by_column,) * 3
        + (by_row, by_column, by_column, by_column, by_row, P(), P()),
        check_vma=False,
    )
```

time: 887 us -> 149 us (0.17)
  waiting for transfers between devices: 611 us -> 0 us
  Pallas kernels: 0 us -> 128 us
  matrix products: 74.1 us -> 0 us
  local copies, waits for them, and re-layouts: 90.6 us -> 19.6 us
  blocking collectives: 56.4 us -> 0 us
  other arithmetic: 34.3 us -> 0 us
  between operations: 15.4 us -> 0.71 us
    all_gather x4 -> x0, waiting for transfers between devices: 326 us -> none  [the longest x1 81.8 us: local(): attn_rows = lax.all_gather(attn_in, 'head', axis=0, tiled=True)]
    reduce_scatter x4 -> x0, waiting for transfers between devices: 262 us -> none  [the longest x1 75.4 us: local(): lax.psum_scatter(jnp.einsum('tf,df->td', d_gate_up, gate_up_weight, prefe...]
    pallas_call x0 -> x1, Pallas kernels: none -> 128 us  [layer_call(): pl.pallas_call(functools.partial(layer_kernel, groups, heads, names), out...]
    dot_general x26 -> x0, matrix products: 74.1 us -> none  [the longest x1 8.43 us: feed_back(): jnp.einsum('td,fd->tf', d_rows, down_here, preferred_element_type=jnp.flo...]
    psum x2 -> x0, blocking collectives: 56.4 us -> none  [the longest x1 42.2 us: local(): lax.psum((gain_attn_grad, gain_ff_grad, gain_final_grad, patch_weight_gra...]
    reshape x20 -> x4, local copies, waits for them, and re-layouts: 44.8 us -> 2.32 us  [local(): args[i] = args[i].reshape(1, -1)]
    psum x1 -> x0, waiting for transfers between devices: 23 us -> none  [local(): lax.psum((query_grad, key_grad, value_grad, out_grad, table_grad, gate_gr...]
    reduce_sum x16 -> x0, other arithmetic: 19.4 us -> none  [the longest x2 5.45 us: norm_back(): gain_grad = jnp.sum(grad_out * unit_rows, axis=0)]
  transfers between devices with their start and end apart: 9 -> 0, of which waited for: 9 -> 0; matrix products, arithmetic and copies ran while one was open for 4% -> 0% of each run, Pallas kernels for 0% -> 0%
where the time goes in v2:
time: 149 us; the launch traced here: 148 us
  Pallas kernels  128 us (86%)
  local copies, waits for them, and re-layouts  19.6 us (13%)
    pallas_call x1, Pallas kernels, layer_call(): pl.pallas_call(functools.partial(layer_kernel, groups, heads, names), out...  128 us
    unnamed x61, local copies, waits for them, and re-layouts  17.2 us

profile of v2, /device:TPU:0, one launch (start us, length us, event | category | flops | bytes accessed | tf_op | source)
XLA Modules:
  0.0 148.2 jit_solution(6247582579842095856)
XLA Ops:
  0.7 0.7 copy-done.15
  1.3 0.6 reshape.68.refs_4_
  1.9 0.1 copy-done.16
  2.0 0.6 reshape.69.refs_5_
  2.6 0.1 copy-done.17
  2.7 0.6 reshape.70.refs_6_
  3.3 0.6 reshape.71.refs_8_
  3.9 0.7 copy.36.refs_13_
  4.6 0.8 copy.37.refs_17_
  5.4 127.9 %shard_map.314 = (f32[16,512]{1,0:T(8,128)}, f32[16,512]{1,0:T(8,128)}, f32[1,512]{1,0:T(1,128)}, f32[1,512]{1,0:T(1,128)}, f32[1,512]{1,0:T(1,128)}, /*index=5*...) custom-call(f32[16,512]{1,0:T(8,128)} %refs_0_.1, ...), custom_call_target="tpu_custom_call" | custom-call | tf_op jit(solution)/shard_map/pallas_call | solution.py:974
  133.3 1.4 copy.38
  134.7 1.7 %copy.39 = f32[512,8]{0,1:T(8,128)} copy(f32[512,8]{1,0:T(8,128)} %get-tuple-element.66) | data formatting | bytes 32768
  136.3 0.6 copy.55
  136.9 0.2 copy-done.7
  137.1 0.6 copy.56
  137.8 0.6 copy.57
  138.4 0.6 copy.58
  139.1 0.6 copy.59
  139.7 0.6 copy.60
  140.3 0.6 copy.61
  140.9 0.7 copy.62
  141.6 0.3 copy-done.5
  141.9 0.7 copy.63
  142.6 0.3 copy-done.4
  143.0 0.7 copy.64
  143.7 0.7 copy.65
  144.4 0.8 copy.66
  145.2 0.4 copy-done.1
  145.6 0.8 copy.67
  146.4 0.4 copy-done
  146.9 0.8 copy.68
  147.7 0.5 copy.69
  (34 shorter events, 0.3 us)
Async XLA Ops:
  0.7 0.7 copy-start.15
  1.3 0.7 copy-start.16
  2.0 0.7 copy-start.17
  2.0 1.3 copy-start.18
  2.0 1.8 %copy-start.19 = (bf16[32,2]{0,1:T(2,128)(2,1)S(1)}, bf16[32,2]{0,1:T(2,128)(2,1)}, u32[]{:S(2)}) copy-start(bf16[32,2]{0,1:T(2,128)(2,1)} %param.32) | copy-start | bytes 388
  2.7 1.9 %copy-start.10 = (bf16[512,8]{0,1:T(8,128)(2,1)S(1)}, bf16[512,8]{0,1:T(8,128)(2,1)}, u32[]{:S(2)}) copy-start(bf16[512,8]{0,1:T(8,128)(2,1)} %param.36) | copy-start | bytes 24580
  133.3 7.6 %copy-start.6 = (f32[512,128]{1,0:T(8,128)S(1)}, f32[512,128]{1,0:T(8,128)}, u32[]{:S(2)}) copy-start(f32[512,128]{1,0:T(8,128)} %get-tuple-element.92) | copy-start | bytes 786436
  134.7 1.7 %copy-start.8 = (f32[16,512]{1,0:T(8,128)S(1)}, f32[16,512]{1,0:T(8,128)}, u32[]{:S(2)}) copy-start(f32[16,512]{1,0:T(8,128)} %get-tuple-element.85) | copy-start | bytes 98308
  136.3 0.8 copy-start.7
  137.1 0.7 copy-start.14
  137.1 2.5 %copy-start.9 = (f32[8,512]{1,0:T(8,128)S(1)}, f32[8,512]{1,0:T(8,128)}, u32[]{:S(2)}) copy-start(f32[8,512]{1,0:T(8,128)} %get-tuple-element.90) | copy-start | bytes 49156
  137.8 0.7 copy-start.13
  138.4 0.6 copy-start.12
  139.6 0.7 copy-start.11
  140.9 1.0 copy-start.5
  141.9 1.0 copy-start.4
  141.9 1.7 %copy-start.3 = (f32[128,512]{1,0:T(8,128)S(1)}, f32[128,512]{1,0:T(8,128)}, u32[]{:S(2)}) copy-start(f32[128,512]{1,0:T(8,128)} %get-tuple-element.95) | copy-start | bytes 786436
  143.0 1.4 copy-start.2
  144.4 1.2 copy-start.1
  145.6 1.2 copy-start
  146.9 0.8 copy-start.20

commit v3 on v2

--- a/solution.py
+++ b/solution.py
@@ -73,6 +73,7 @@
 class Layer:
     def __init__(self, **refs):
         self.__dict__.update(refs)
+        self.rows = {}
 
     def prepare(self, head_index):
         rows, steps = self.series.shape
@@ -118,10 +119,14 @@
         fold = (iota(self.fold.shape, 1) % patch == iota(self.fold.shape, 0)).astype(BF16)
         self.fold[...] = fold
         pw = self.patch_w[...].astype(F32)
+        for name, source in zip(("g1", "g2", "g3", "pb"), self.vectors):
+            self.rows[name] = jnp.concatenate(
+                [source[i : i + 1, :].astype(F32) for i in range(source.shape[0])], axis=1
+            )
         self.ptile[...] = jnp.broadcast_to(
             pw[None], (self.ptile.shape[0] // patch, patch, pw.shape[1])
         ).reshape(self.ptile.shape).astype(BF16)
-        self.htile[...] = nn(self.head_w[...], fold[:patch]).astype(BF16)
+        self.htile[...] = tn(self.head_w[...], fold[:patch]).astype(BF16)
         hb = jnp.broadcast_to(self.head_b[...], (16, patch))
         self.hbias = nn(hb, fold[:patch])[0:1]
 
@@ -147,11 +152,11 @@
         at = pl.ds(pl.multiple_of(tile * TILE, TILE), TILE)
         spread = self.spread_rows(self.normed_low, tile)
         self.p8t[:, at] = nt(self.fold[...], spread).astype(BF16)
-        embedded = nn(spread, self.ptile[...]) + self.patch_b[...].astype(F32)
+        embedded = nn(spread, self.ptile[...]) + self.rows["pb"]
         self.embedded[at, :] = embedded
         scale = row_scale(embedded)
         self.s_attn[at, :] = scale
-        self.attn_in[at, :] = (embedded * scale * self.gain_attn[...].astype(F32)).astype(BF16)
+        self.attn_in[at, :] = (embedded * scale * self.rows["g1"]).astype(BF16)
 
     def buckets(self):
         length = self.pm.shape[0]
@@ -169,9 +174,9 @@
         return ids, used
 
     def own_table(self):
-        table = self.table[...].astype(F32)
-        lane = iota((table.shape[0], 128), 1)
-        self.tab[0] = jnp.where(lane < 64, table[:, 0:1], table[:, 1:2])
+        table = self.table[...].astype(BF16)
+        pick = (iota((2, 128), 1) // 64 == iota((2, 128), 0)).astype(BF16)
+        self.tab[0] = tn(table, pick)
 
     def offsets(self, slot):
         ids, used = self.buckets()
@@ -184,69 +189,81 @@
         lane = iota((1, 128), 1)
         return (lane < 64).astype(BF16), (lane >= 64).astype(BF16)
 
-    def attend(self, slot, tile):
+    def attend(self, tile):
         at = pl.ds(pl.multiple_of(tile * TILE, TILE), TILE)
-        wide = pl.ds(pl.multiple_of(slot * 384, 128), 384)
         length = self.pm.shape[0]
+        rows_tile = TILE // length
         even, odd = self.head_masks()
-        projected = nn(self.attn_in[at, :], self.wq[:, wide]).astype(BF16)
-        self.qkv[at, wide] = projected
-        bias = self.bias[slot]
-        block = (
-            iota(bias.shape, 0) // (length // 2) != (iota(bias.shape, 1) % length) // (length // 2)
-        ).astype(F32) * -1e30
-        contexts = []
-        for r in range(TILE // length):
-            rows = slice(r * length, (r + 1) * length)
-            query, key, value = (projected[rows, i * 128 : (i + 1) * 128] for i in range(3))
+        half = length // 2
+        shape = (length, 2 * length)
+        block = (iota(shape, 0) // half != (iota(shape, 1) % length) // half).astype(F32) * -1e30
+        splits = [self.splitb[pl.ds(tile * rows_tile + r, 1), :] * block for r in range(rows_tile)]
+        width = self.ctx.shape[1]
+        projected = []
+        for i in range(3):
+            part = nn(self.attn_in[at, :], self.wq[:, i * width : (i + 1) * width]).astype(BF16)
+            self.qkv[at, i * width : (i + 1) * width] = part
+            projected.append(part)
+        items = [(s, r) for s in range(self.slots) for r in range(rows_tile)]
+
+        def piece(s, r, i):
+            return projected[i][r * length : (r + 1) * length, s * 128 : (s + 1) * 128]
+
+        scores = []
+        for s, r in items:
+            query = piece(s, r, 0)
             both = jnp.concatenate([query * even, query * odd], axis=0)
-            split = self.splitb[pl.ds(tile * (TILE // length) + r, 1), :]
-            scores = nt(key, both) + (bias + split * block)
-            top = jnp.max(scores, axis=0, keepdims=True)
-            raised = jnp.exp(scores - top)
+            scores.append(nt(piece(s, r, 1), both))
+        turned = []
+        for (s, r), score in zip(items, scores):
+            score = score + (self.bias[s] + splits[r])
+            top = jnp.max(score, axis=0, keepdims=True)
+            raised = jnp.exp(score - top)
             probs = raised * (1.0 / jnp.sum(raised, axis=0, keepdims=True))
-            self.probs[slot, pl.ds(pl.multiple_of(tile * TILE + r * length, length), length), :] = (
-                probs
+            self.probs[
+                s, pl.ds(pl.multiple_of(tile * TILE + r * length, length), length), :
+            ] = probs.astype(self.probs.dtype)
+            turned.append(probs.astype(BF16))
+        turned = [probs.T for probs in turned]
+        mixed = [nn(probs, piece(s, r, 2)) for probs, (s, r) in zip(turned, items)]
+        low_lanes = iota((1, 128), 1) < 64
+        for s in range(self.slots):
+            self.ctx[at, s * 128 : (s + 1) * 128] = jnp.concatenate(
+                [
+                    jnp.where(low_lanes, m[:length], m[length:]).astype(BF16)
+                    for m in mixed[s * rows_tile : (s + 1) * rows_tile]
+                ],
+                axis=0,
             )
-            mixed = tn(probs.astype(BF16), value)
-            contexts.append(
-                jnp.where(iota((1, 128), 1) < 64, mixed[:length], mixed[length:]).astype(BF16)
-            )
-        self.ctx[at, pl.ds(pl.multiple_of(slot * 128, 128), 128)] = jnp.concatenate(
-            contexts, axis=0
-        )
-
-    def middle(self, tile):
+
+    def middle_gate(self, tile):
         at = pl.ds(pl.multiple_of(tile * TILE, TILE), TILE)
         hidden_mid = self.embedded[at, :] + nt(self.ctx[at, :], self.wo[...])
-        ff_scale = row_scale(hidden_mid)
-        ff_unit = hidden_mid * ff_scale
-        gain_ff = self.gain_ff[...].astype(F32)
-        ff_in = (ff_unit * gain_ff).astype(BF16)
+        self.hidden_mid[at, :] = hidden_mid
+        ff_in = (hidden_mid * row_scale(hidden_mid) * self.rows["g2"]).astype(BF16)
         self.ff_in[at, :] = ff_in
-        slots = self.slots
-        ff_out = None
-        keep = []
-        for s in range(slots):
-            w = self.wg.shape[1] // slots
-            gu = nn(ff_in, self.wg[:, s * w : (s + 1) * w])
-            gate, up = gu[:, : w // 2], gu[:, w // 2 :]
-            c = math.sqrt(2.0 / math.pi)
+        total = self.inner.shape[1]
+        block = 256
+        c = math.sqrt(2.0 / math.pi)
+        for first in range(0, total, block):
+            cols = slice(first, first + block)
+            gate = nn(ff_in, self.wg[:, first : first + block])
+            up = nn(ff_in, self.wg[:, total + first : total + first + block])
             square = gate * gate
             t = jnp.tanh(gate * (c + (c * 0.044715) * square))
             plus = 0.5 * (1.0 + t)
             act = gate * plus
             slope = plus + (0.5 * gate) * (1.0 - t * t) * (c + (3.0 * c * 0.044715) * square)
-            inner = (act * up).astype(BF16)
-            cols = slice(s * (w // 2), (s + 1) * (w // 2))
-            self.inner[at, cols] = inner
-            self.act[:, cols] = act.astype(BF16)
-            self.slope[:, cols] = (up * slope).astype(BF16)
-        ff_out = nt(self.inner[at, :], self.wd[...])
-        hidden_end = hidden_mid + ff_out
+            self.inner[at, cols] = (act * up).astype(BF16)
+            self.act[at, cols] = act.astype(BF16)
+            self.slope[at, cols] = (up * slope).astype(BF16)
+
+    def middle_down(self, tile):
+        at = pl.ds(pl.multiple_of(tile * TILE, TILE), TILE)
+        hidden_end = self.hidden_mid[at, :] + nt(self.inner[at, :], self.wd[...])
         final_scale = row_scale(hidden_end)
         final_unit = hidden_end * final_scale
-        gain_final = self.gain_final[...].astype(F32)
+        gain_final = self.rows["g3"]
         final_in = (final_unit * gain_final).astype(BF16)
         self.final_in[at, :] = final_in
         self.gather_rows(self.output, tile, nn(final_in, self.htile[...]), self.hbias)
@@ -255,61 +272,82 @@
         d_final = nt(d_spread, self.htile[...])
         d_end, gain_part = norm_back(d_final, final_unit, final_scale, gain_final)
         self.g_final[...] += gain_part
-        d_low = d_end.astype(BF16)
-        self.d_end_low[at, :] = d_low
-        d_in = None
-        for s in range(slots):
-            w = self.wg.shape[1] // slots
-            cols = slice(s * (w // 2), (s + 1) * (w // 2))
+        self.d_end_low[at, :] = d_end.astype(BF16)
+        self.d_mid[at, :] = d_end
+
+    def middle_back(self, tile):
+        at = pl.ds(pl.multiple_of(tile * TILE, TILE), TILE)
+        d_low = self.d_end_low[at, :]
+        total = self.inner.shape[1]
+        block = 256
+        for first in range(0, total, block):
+            cols = slice(first, first + block)
             d_inner = nn(d_low, self.wd[:, cols])
-            d_gate = (d_inner * self.slope[:, cols].astype(F32)).astype(BF16)
-            d_up = (d_inner * self.act[:, cols].astype(F32)).astype(BF16)
-            self.dgu[at, s * w : s * w + w // 2] = d_gate
-            self.dgu[at, s * w + w // 2 : (s + 1) * w] = d_up
+            d_gate = (d_inner * self.slope[at, cols].astype(F32)).astype(BF16)
+            d_up = (d_inner * self.act[at, cols].astype(F32)).astype(BF16)
+            self.dgu[at, cols] = d_gate
+            self.dgu[at, total + first : total + first + block] = d_up
         d_in = nt(self.dgu[at, :], self.wg[...])
-        d_norm, gain_part = norm_back(d_in, ff_unit, ff_scale, gain_ff)
+        hidden_mid = self.hidden_mid[at, :]
+        ff_scale = row_scale(hidden_mid)
+        d_norm, gain_part = norm_back(d_in, hidden_mid * ff_scale, ff_scale, self.rows["g2"])
         self.g_ff[...] += gain_part
-        d_mid = d_end + d_norm
+        d_mid = self.d_mid[at, :] + d_norm
         self.d_mid[at, :] = d_mid
         d_mid_low = d_mid.astype(BF16)
         self.d_mid_low[at, :] = d_mid_low
         self.d_ctx[at, :] = nn(d_mid_low, self.wo[...]).astype(BF16)
 
-    def attend_back(self, slot, tile):
+    def attend_back(self, tile):
+        width = self.ctx.shape[1]
         length = self.pm.shape[0]
+        rows_tile = TILE // length
         even, odd = self.head_masks()
-        total = jnp.zeros((length, 128), F32)
-        for r in range(TILE // length):
-            rows = pl.ds(pl.multiple_of(tile * TILE + r * length, length), length)
-
-            def part(i):
-                return self.qkv[rows, pl.ds(pl.multiple_of(slot * 384 + i * 128, 128), 128)]
-
-            query, key, value = part(0), part(1), part(2)
-            d_ctx = self.d_ctx[rows, pl.ds(pl.multiple_of(slot * 128, 128), 128)]
-            query_both = jnp.concatenate([query * even, query * odd], axis=0)
-            d_both = jnp.concatenate([d_ctx * even, d_ctx * odd], axis=0)
-            probs = self.probs[slot, rows, :]
-            d_probs = nt(value, d_both)
-            d_value = nn(probs.astype(BF16), d_both)
-            dots = jnp.sum(probs * d_probs, axis=0, keepdims=True)
-            d_scores = (probs * (d_probs - dots)).astype(BF16)
-            total = total + d_scores.astype(F32)
-            d_key = nn(d_scores, query_both)
-            mixed = tn(d_scores, key)
-            d_query = jnp.where(iota((1, 128), 1) < 64, mixed[:length], mixed[length:])
-            for i, grad in enumerate((d_query, d_key, d_value)):
-                self.dqkv[rows, pl.ds(pl.multiple_of(slot * 384 + i * 128, 128), 128)] = (
-                    grad.astype(BF16)
-                )
-        self.dsum[slot] += total
+        items = [(s, r) for s in range(self.slots) for r in range(rows_tile)]
+        rows = [
+            pl.ds(pl.multiple_of(tile * TILE + r * length, length), length)
+            for r in range(rows_tile)
+        ]
+
+        def piece(s, r, i):
+            return self.qkv[rows[r], i * width + s * 128 : i * width + (s + 1) * 128]
+
+        d_both = []
+        for s, r in items:
+            d_ctx = self.d_ctx[rows[r], s * 128 : (s + 1) * 128]
+            d_both.append(jnp.concatenate([d_ctx * even, d_ctx * odd], axis=0))
+        d_probs = [nt(piece(s, r, 2), both) for (s, r), both in zip(items, d_both)]
+        probs = [self.probs[s, rows[r], :] for s, r in items]
+        d_value = [nn(p.astype(BF16), both) for p, both in zip(probs, d_both)]
+        d_scores = []
+        for p, dp in zip(probs, d_probs):
+            p = p.astype(F32)
+            dots = jnp.sum(p * dp, axis=0, keepdims=True)
+            d_scores.append((p * (dp - dots)).astype(BF16))
+        turned = [d.T for d in d_scores]
+        d_key = []
+        for (s, r), d in zip(items, d_scores):
+            query = piece(s, r, 0)
+            d_key.append(nn(d, jnp.concatenate([query * even, query * odd], axis=0)))
+        mixed = [nn(d, piece(s, r, 1)) for (s, r), d in zip(items, turned)]
+        low_lanes = iota((1, 128), 1) < 64
+        for n, (s, r) in enumerate(items):
+            d_query = jnp.where(low_lanes, mixed[n][:length], mixed[n][length:])
+            for i, grad in enumerate((d_query, d_key[n], d_value[n])):
+                cols = slice(i * width + s * 128, i * width + (s + 1) * 128)
+                self.dqkv[rows[r], cols] = grad.astype(BF16)
+        for s in range(self.slots):
+            total = self.dsum[s]
+            for d in d_scores[s * rows_tile : (s + 1) * rows_tile]:
+                total = total + d.astype(F32)
+            self.dsum[s] = total
 
     def embed_back(self, tile):
         at = pl.ds(pl.multiple_of(tile * TILE, TILE), TILE)
         d_in = nt(self.dqkv[at, :], self.wq[...])
         scale = self.s_attn[at, :]
         d_norm, gain_part = norm_back(
-            d_in, self.embedded[at, :] * scale, scale, self.gain_attn[...].astype(F32)
+            d_in, self.embedded[at, :] * scale, scale, self.rows["g1"]
         )
         self.g_attn[...] += gain_part
         d_embedded = (self.d_mid[at, :] + d_norm).astype(BF16)
@@ -339,6 +377,9 @@
         mean_weight = self.combine([g / n for g, n in zip(mean_grad, self.counts)])
         self.series_grad[...] = d_centred + obs * self.spread(mean_weight)
 
+    def head_grad(self):
+        self.small[16:24, :] = nn(self.d8t[...], self.final_in[...])[0:8]
+
     def small_grads(self, head_index):
         small = self.small
         heads = self.slots
@@ -349,7 +390,6 @@
             axis=0,
         )
         small[8:16, :] = nn(self.p8t[...], self.d_emb[...])[0:8]
-        small[16:24, :] = nn(self.d8t[...], self.final_in[...])[0:8]
         lane = iota((8, 128), 1)
         groups = self.tab.shape[1] // 8
         pieces = [jnp.zeros((8, 128), F32) for _ in range(groups)]
@@ -375,35 +415,6 @@
                     pieces[g] = pieces[g] + jnp.where(lane == 2 * owner + which, column, 0.0)
         small[24:32, :] = jnp.concatenate(pieces, axis=1)
 
-    def small_out(self, head_index):
-        small = self.small
-        for row, out in enumerate((self.o_attn, self.o_ff, self.o_final, self.o_pb)):
-            out[...] = small[row : row + 1, :]
-        self.o_pw[...] = small[8:16, :]
-        patch = self.o_pw.shape[0]
-        block = jnp.concatenate(
-            [small[16:24, :], jnp.zeros((120, small.shape[1]), F32)], axis=0
-        )
-        self.o_hw[...] = block.T[:, :patch]
-        lane = iota((8, 128), 1)
-        column = jnp.sum(
-            jnp.where(lane == 2 * self.slots, small[24:32, 0:128], 0.0), axis=1, keepdims=True
-        )
-        self.o_hb[...] = jnp.sum(jnp.where(lane == iota((8, 128), 0), column, 0.0), axis=0, keepdims=True)[
-            :, :patch
-        ]
-        for g in range(self.tab.shape[1] // 8):
-            piece = small[24:32, g * 128 : (g + 1) * 128]
-            columns = [
-                jnp.sum(
-                    jnp.where(lane == 2 * head_index + which, piece, 0.0), axis=1, keepdims=True
-                )
-                for which in range(2)
-            ]
-            self.o_table[8 * g : 8 * g + 8, :] = jnp.where(
-                iota((8, 2), 1) == 0, columns[0], columns[1]
-            )
-
     def clear(self):
         for ref in (self.g_attn, self.g_ff, self.g_final, self.g_bias):
             ref[...] = jnp.zeros(ref.shape, F32)
@@ -482,12 +493,16 @@
 class Gather:
     ORDERS = ((1, 2, 0), (2, 1, 0))
 
-    def __init__(self, net, ref):
-        self.net, self.ref = net, ref
+    def __init__(self, net, ref, parts):
+        self.net, self.ref, self.parts = net, ref, parts
         self.heads = net.heads
-        self.width = ref.shape[1] // self.heads
         self.unit = ref.shape[0] // 16
-        self.ids = [[net.claim() for _ in range(net.heads - 1 + 3)] for _ in range(2)]
+        self.ids = {}
+
+    def id(self, *key):
+        if key not in self.ids:
+            self.ids[key] = self.net.claim()
+        return self.ids[key]
 
     def block(self, half):
         bits = [self.net.bit(b) for b in self.ORDERS[half]]
@@ -501,54 +516,63 @@
         return rows_at((half * 8 + first * size) * self.unit, size * self.unit, self.unit)
 
     def start(self):
-        net, width = self.net, self.width
+        net = self.net
         for half in range(2):
             rows = self.span(half, 0)
             for t in range(1, self.heads):
                 slot = self.heads - t
-                net.send(
-                    self.ids[half][t - 1],
-                    self.ref.at[rows, 0:width],
-                    self.ref.at[rows, slot * width : (slot + 1) * width],
-                    net.beside(t),
-                )
-
-    def step(self, level):
-        net, width = self.net, self.width
-        others = pl.ds(width, (self.heads - 1) * width)
-        for half in range(2):
-            if level == 0:
-                for t in range(1, self.heads):
-                    slot = self.heads - t
-                    net.arrived(
-                        self.ids[half][t - 1],
-                        self.ref.at[self.span(half, 0), slot * width : (slot + 1) * width],
+                for first, width in self.parts:
+                    net.send(
+                        self.id(half, "z", t, first),
+                        self.ref.at[rows, first : first + width],
+                        self.ref.at[rows, first + slot * width : first + (slot + 1) * width],
                         net.beside(t),
                     )
-            else:
-                net.arrived(
-                    self.ids[half][self.heads - 2 + level],
-                    self.ref.at[self.span(half, level - 1, mine=False), others],
-                    net.across(self.ORDERS[half][level - 1]),
-                )
+
+    def others(self, first, width):
+        return slice(first + width, first + self.heads * width)
+
+    def step(self, level):
+        net = self.net
+        for half in range(2):
+            for first, width in self.parts:
+                if level == 0:
+                    for t in range(1, self.heads):
+                        slot = self.heads - t
+                        net.arrived(
+                            self.id(half, "z", t, first),
+                            self.ref.at[
+                                self.span(half, 0), first + slot * width : first + (slot + 1) * width
+                            ],
+                            net.beside(t),
+                        )
+                else:
+                    net.arrived(
+                        self.id(half, "s", level - 1, first),
+                        self.ref.at[self.span(half, level - 1, mine=False), self.others(first, width)],
+                        net.across(self.ORDERS[half][level - 1]),
+                    )
             if level < 3:
                 rows = self.span(half, level)
-                net.send(
-                    self.ids[half][self.heads - 1 + level],
-                    self.ref.at[rows, others],
-                    self.ref.at[rows, others],
-                    net.across(self.ORDERS[half][level]),
-                )
+                for first, width in self.parts:
+                    place = self.ref.at[rows, self.others(first, width)]
+                    net.send(
+                        self.id(half, "s", level, first),
+                        place,
+                        place,
+                        net.across(self.ORDERS[half][level]),
+                    )
 
 
 class Reduce:
     ORDERS = ((1, 2), (2, 1))
 
-    def __init__(self, net, refs, columns, width):
+    def __init__(self, net, refs, parts):
         self.net = net
         self.heads = net.heads
-        self.width = width
-        self.columns = columns
+        self.parts = parts
+        last, width = parts[-1]
+        self.columns = slice(parts[0][0], last + self.heads * width)
         (
             self.own, self.snd0, self.rcv0, self.snd1, self.rcv1,
             self.snd2, self.rcv2, self.sndz, self.rcvz, self.fin,
@@ -560,14 +584,17 @@
             self.ids[name] = self.net.claim()
         return self.ids[name]
 
-    def slots(self, s):
-        first = self.columns.start + s * self.width
-        return slice(first, first + self.width)
+    def slots(self, part, s):
+        first, width = part
+        return slice(first + s * width, first + (s + 1) * width)
+
+    def fin_part(self, part):
+        first, width = part
+        return slice(first // self.heads, first // self.heads + width)
 
     @property
     def fin_columns(self):
-        first = self.columns.start // self.heads
-        return slice(first, first + self.width)
+        return slice(self.columns.start // self.heads, self.columns.stop // self.heads)
 
     def produce(self, left_t, right, block=512):
         net = self.net
@@ -586,7 +613,7 @@
             cols = slice(self.columns.start + c, self.columns.start + c + block)
             self.own[:, cols] = nn(
                 left_t[rows_at(core * count, count, count), :], right[:, c : c + block]
-            )
+            ).astype(self.own.dtype)
 
     def halving(self, level):
         net, cols = self.net, self.columns
@@ -609,7 +636,7 @@
                 send, target = ((self.snd1, self.rcv1), (self.snd2, self.rcv2))[level]
                 place = slice(half * (count // 2), (half + 1) * (count // 2))
                 send[place, cols] = (
-                    self.own[rows_at(at + away, count // 2, 32), cols]
+                    self.own[rows_at(at + away, count // 2, 32), cols].astype(F32)
                     + source[rows_at(first + away, count // 2, 32), cols].astype(F32)
                 ).astype(BF16)
                 net.send(
@@ -625,13 +652,16 @@
                 bit = net.bit(self.ORDERS[half][level])
                 stay = bit * (count // 2)
                 rows = rows_at(at + stay, count // 2, 32)
-                self.own[rows, cols] = self.own[rows, cols] + source[
-                    rows_at(first + stay, count // 2, 32), cols
-                ].astype(F32)
+                self.own[rows, cols] = (
+                    self.own[rows, cols].astype(F32)
+                    + source[rows_at(first + stay, count // 2, 32), cols].astype(F32)
+                ).astype(self.own.dtype)
             else:
                 rows = rows_at(at, count, 32)
-                total = self.own[rows, cols] + source[first : first + count, cols].astype(F32)
-                self.own[rows, cols] = total
+                total = self.own[rows, cols].astype(F32) + source[
+                    first : first + count, cols
+                ].astype(F32)
+                self.own[rows, cols] = total.astype(self.own.dtype)
                 if net.bits <= 3:
                     self.sndz[first : first + count, cols] = total.astype(BF16)
 
@@ -662,9 +692,9 @@
             for half in range(2):
                 rows = rows_at(self.kept(half, 2), count, 32)
                 place = slice(half * count, (half + 1) * count)
-                self.own[rows, cols] = self.sndz[place, cols].astype(F32) + inbox[
-                    place, cols
-                ].astype(F32)
+                self.own[rows, cols] = (
+                    self.sndz[place, cols].astype(F32) + inbox[place, cols].astype(F32)
+                ).astype(self.own.dtype)
         if net.bits > 3:
             for half in range(2):
                 rows = rows_at(self.kept(half, 2), count, 32)
@@ -675,12 +705,13 @@
     def owners(self):
         net = self.net
         for s in range(1, self.heads):
-            net.send(
-                self.id(f"z{s}"),
-                self.sndz.at[:, self.slots(s)],
-                self.rcvz.at[s - 1, :, self.fin_columns],
-                net.beside(s),
-            )
+            for part in self.parts:
+                net.send(
+                    self.id(f"z{s}{part[0]}"),
+                    self.sndz.at[:, self.slots(part, s)],
+                    self.rcvz.at[s - 1, :, self.fin_part(part)],
+                    net.beside(s),
+                )
 
     def place(self, half, level, mine=True):
         net = self.net
@@ -700,14 +731,23 @@
         fin = self.fin_columns
         count = self.sndz.shape[0] // 2
         for s in range(1, self.heads):
-            net.arrived(self.id(f"z{s}"), self.rcvz.at[s - 1, :, fin], net.beside(s))
+            for part in self.parts:
+                net.arrived(
+                    self.id(f"z{s}{part[0]}"),
+                    self.rcvz.at[s - 1, :, self.fin_part(part)],
+                    net.beside(s),
+                )
         for half in range(2):
-            part = slice(half * count, (half + 1) * count)
-            total = self.own[rows_at(self.kept(half, 2), count, 32), self.slots(0)]
-            for s in range(1, self.heads):
-                total = total + self.rcvz[s - 1, part, fin].astype(F32)
             rows = self.place(half, 0)
-            self.fin[rows, fin] = total.astype(BF16)
+            for part in self.parts:
+                total = self.own[
+                    rows_at(self.kept(half, 2), count, 32), self.slots(part, 0)
+                ].astype(F32)
+                for s in range(1, self.heads):
+                    total = total + self.rcvz[
+                        s - 1, half * count : (half + 1) * count, self.fin_part(part)
+                    ].astype(F32)
+                self.fin[rows, self.fin_part(part)] = total.astype(BF16)
             net.send(
                 self.id(f"f0{half}"),
                 self.fin.at[rows, fin],
@@ -783,144 +823,185 @@
 
 
 INPUTS = (
-    "series", "observed", "split", "cot", "gain_attn", "gain_ff", "gain_final", "patch_w", "patch_b", "wq_in", "wk_in", "wv_in", "wo_in", "table", "wg_in", "wu_in", "wd_in", "head_w", "head_b",
+    "series", "observed", "split", "cot", "gain_attn", "gain_ff", "gain_final", "patch_w", "patch_b",
+    "wq_in", "wk_in", "wv_in", "wo_in", "table", "wg_in", "wu_in", "wd_in", "head_w", "head_b",
 )
-OUTPUTS = (
-    "rebuilt", "series_grad", "o_attn", "o_ff", "o_final", "o_pw", "o_pb", "o_q", "o_k", "o_v", "o_o", "o_table", "o_g", "o_u", "o_d", "o_hw", "o_hb",
-)
-SHARED = (
-    "own", "snd0", "rcv0", "snd1", "rcv1", "snd2", "rcv2", "sndz", "rcvz", "fin",
-)
+OUTPUTS = ("rebuilt", "series_grad", "sums", "fin_out")
+SHARED = ("own", "snd0", "rcv0", "snd1", "rcv1", "snd2", "rcv2", "sndz", "rcvz", "fin")
 
 
 def layer_kernel(groups, heads, names, *refs):
     named = dict(zip(names, refs))
-    dgu = named["dgu"]
-    wq, wo, wg, wd = (named[k] for k in ("wq", "wo", "wg", "wd"))
-    named["dqkv"] = dgu.at[:, 0 : wq.shape[1]]
+    dgu, weights = named["dgu"], named["weights"]
+    starts = {}
+    first = 0
+    for key, width in zip("qkvogud", [named["wq_in"].shape[1]] * 4 + [named["wg_in"].shape[1]] * 3):
+        starts[key] = (first, width)
+        first += heads * width
+    parts = {keys: [starts[key] for key in keys] for keys in ("qkv", "o", "gu", "g", "u", "d")}
+    named["wq"] = weights.at[:, 0 : starts["o"][0]]
+    named["wo"] = weights.at[:, starts["o"][0] : starts["g"][0]]
+    named["wg"] = weights.at[:, starts["g"][0] : starts["d"][0]]
+    named["wd"] = weights.at[:, starts["d"][0] : first]
+    named["dqkv"] = dgu.at[:, 0 : starts["o"][0]]
     named["d_emb"] = named["ff_in"]
-    named["fin"] = wg.at[:, 0 : named["rcvz"].shape[2]]
+    named["d_mid_low"] = named["final_in"]
+    named["small"] = named["slabs"].at[0]
     layer = Layer(slots=heads, **named)
+    layer.vectors = (layer.gain_attn, layer.gain_ff, layer.gain_final, layer.patch_b)
     tiles = layer.embedded.shape[0] // TILE
     net = Net(groups, heads, named["send_sems"], named["recv_sems"])
+
+    def own(key, ref, turn=False):
+        first, width = starts[key]
+        weights[:, first : first + width] = ref[...].T if turn else ref[...]
+
     net.greet_start()
-    part = layer.wq_in.shape[1]
-    for i, ref in enumerate((layer.wq_in, layer.wk_in, layer.wv_in)):
-        wq[:, i * part : (i + 1) * part] = ref[...]
-    wo[:, 0 : layer.wo_in.shape[0]] = layer.wo_in[...].T
-    part = layer.wg_in.shape[1]
-    for i, ref in enumerate((layer.wg_in, layer.wu_in)):
-        wg[:, i * part : (i + 1) * part] = ref[...]
-    wd[:, 0 : layer.wd_in.shape[0]] = layer.wd_in[...].T
+    own("q", layer.wq_in)
+    own("k", layer.wk_in)
+    own("v", layer.wv_in)
     layer.own_table()
     net.greet_end()
-    gather_q, gather_o, gather_g, gather_d = (Gather(net, ref) for ref in (wq, wo, wg, wd))
+    gather = {keys: Gather(net, weights, parts[keys]) for keys in ("qkv", "o", "gu", "d")}
+    gather["qkv"].start()
     table_ids = [net.claim() for _ in range(heads - 1)]
-    gather_q.start()
     for t in range(1, heads):
         net.send(table_ids[t - 1], layer.tab.at[0], layer.tab.at[heads - t], net.beside(t))
-    gather_o.start()
-    gather_g.start()
-    gather_d.start()
+    own("o", layer.wo_in, turn=True)
+    own("g", layer.wg_in)
+    own("u", layer.wu_in)
+    own("d", layer.wd_in, turn=True)
     layer.clear()
     layer.prepare(net.head)
     loop(tiles, layer.embed)
-    layer.offsets(0)
-    gather_q.step(0)
-    loop(tiles // 2, lambda t: layer.attend(0, t))
-    gather_o.step(0)
-    gather_q.step(1)
-    loop(tiles // 2, lambda t: layer.attend(0, t + tiles // 2))
-    gather_g.step(0)
-    gather_o.step(1)
-    gather_q.step(2)
+    gather["qkv"].step(0)
+    gather["o"].start()
+    gather["gu"].start()
     for t in range(1, heads):
         net.arrived(table_ids[t - 1], layer.tab.at[heads - t], net.beside(t))
-    loop(heads - 1, lambda s: layer.offsets(s + 1))
-    gather_d.step(0)
-    gather_g.step(1)
-    gather_q.step(3)
-    loop(tiles, lambda t: layer.attend(1, t))
-    gather_o.step(2)
-    gather_d.step(1)
-    gather_g.step(2)
-    loop(tiles, lambda t: layer.attend(2, t))
-    gather_o.step(3)
-    gather_d.step(2)
-    gather_g.step(3)
-    loop(tiles, lambda t: layer.attend(3, t))
-    gather_d.step(3)
+    loop(heads, layer.offsets)
+    gather["qkv"].step(1)
+    gather["o"].step(0)
+    gather["qkv"].step(2)
+    gather["gu"].step(0)
+    gather["d"].start()
+    gather["o"].step(1)
+    gather["qkv"].step(3)
+    loop(tiles // 2, layer.attend)
+    gather["gu"].step(1)
+    gather["o"].step(2)
+    gather["d"].step(0)
+    loop(tiles // 2, lambda t: layer.attend(t + tiles // 2))
+    gather["gu"].step(2)
+    gather["o"].step(3)
+    gather["d"].step(1)
+    gather["gu"].step(3)
+    loop(tiles // 2, layer.middle_gate)
+    gather["d"].step(2)
+    loop(tiles // 2, lambda t: layer.middle_gate(t + tiles // 2))
+    gather["d"].step(3)
     net.drain()
-    loop(tiles, layer.middle)
+    loop(tiles, layer.middle_down)
+    layer.head_grad()
+
     shared = [named[k] for k in SHARED]
-    bounds = {}
-    first = 0
-    for key, ref in zip("qogd", (wq, wo, wg, wd)):
-        bounds[key] = slice(first, first + ref.shape[1])
-        first += ref.shape[1]
-    reduce = {
-        key: Reduce(net, shared, bounds[key], ref.shape[1] // heads)
-        for key, ref in zip("qogd", (wq, wo, wg, wd))
-    }
+    reduce = {keys: Reduce(net, shared, parts[keys]) for keys in ("qkv", "o", "gu", "d")}
     for one in reduce.values():
         one.extra = named.get("extra")
+    steps = {keys: one.steps() for keys, one in reduce.items()}
     left, right = layer.left_t, layer.right_t
-    left[...] = layer.ff_in[...].T
-    reduce["g"].produce(left, dgu)
     right[...] = layer.d_end_low[...].T
     reduce["d"].produce(right, layer.inner)
-    left[...] = layer.d_mid_low[...].T
-    reduce["o"].produce(left, layer.ctx)
-    right[...] = layer.attn_in[...].T
-    pending = []
-    steps = {key: reduce[key].steps() for key in "god"}
-    for level in range(7):
-        pending += [steps[key][level] for key in "gdo"]
-
-    def advance(count):
-        for _ in range(min(count, len(pending))):
-            pending.pop(0)()
-
-    for s in range(heads):
-        advance(2)
-        loop(tiles // 2, lambda t: layer.attend_back(s, t))
-        advance(3)
-        loop(tiles // 2, lambda t: layer.attend_back(s, t + tiles // 2))
-    reduce["q"].produce(right, named["dqkv"])
-    advance(1)
-    loop(tiles, layer.embed_back)
-    last = reduce["q"].steps()
-    last[0]()
-    layer.small = named["slabs"].at[0]
+    for t in range(tiles):
+        layer.middle_back(t)
+        steps["d"][t]()
+    left[...] = layer.ff_in[...].T
+    reduce["gu"].produce(left, dgu)
+    steps["d"][4]()
+    right[...] = layer.d_mid_low[...].T
+    reduce["o"].produce(right, layer.ctx)
+    steps["gu"][0]()
+    steps["d"][5]()
+    left[...] = layer.attn_in[...].T
+    layer.attend_back(0)
+    steps["o"][0]()
+    layer.attend_back(1)
+    steps["gu"][1]()
+    steps["d"][6]()
+    layer.attend_back(2)
+    steps["o"][1]()
+    layer.attend_back(3)
+    reduce["qkv"].produce(left, named["dqkv"])
+    steps["gu"][2]()
+    steps["o"][2]()
+    steps["qkv"][0]()
+    loop(tiles // 2, layer.embed_back)
+    steps["gu"][3]()
+    steps["qkv"][1]()
+    loop(tiles // 2, lambda t: layer.embed_back(t + tiles // 2))
     layer.small_grads(net.head)
     total = Total(net, named["slabs"], named["inbox"])
+    levels = len(total.partners)
     total.start(0)
-    last[1]()
+    steps["o"][3]()
+    steps["gu"][4]()
+    total.step(0)
+    steps["qkv"][2]()
+    steps["o"][4]()
     layer.finish()
-    total.step(0)
-    last[2]()
-    advance(len(pending))
-    levels = len(total.partners)
+    steps["gu"][5]()
     total.step(1)
-    last[3]()
+    steps["qkv"][3]()
+    steps["o"][5]()
     total.step(2)
-    last[4]()
+    steps["gu"][6]()
+    steps["qkv"][4]()
+    steps["o"][6]()
     total.step(3)
-    last[5]()
-    fin = named["fin"]
-    ff = layer.o_g.shape[1]
-    layer.o_o[...] = fin[:, 3 * 128 : 4 * 128].astype(F32).T
-    layer.o_g[...] = fin[:, 512 : 512 + ff].astype(F32)
-    layer.o_u[...] = fin[:, 512 + ff : 512 + 2 * ff].astype(F32)
-    layer.o_d[...] = fin[:, 512 + 2 * ff :].astype(F32).T
+    steps["qkv"][5]()
     for level in range(4, levels):
         total.step(level)
-    layer.small = named["slabs"].at[levels]
-    layer.small_out(net.head)
-    last[6]()
-    for i, out in enumerate((layer.o_q, layer.o_k, layer.o_v)):
-        out[...] = fin[:, i * 128 : (i + 1) * 128].astype(F32)
+    layer.sums[...] = named["slabs"][levels]
+    steps["qkv"][6]()
+    layer.fin_out[...] = named["fin"][...]
     net.drain()
+
+
+def finish_kernel(
+    heads, rebuilt, series_grad, sums, fin, o_rebuilt, o_series, o_attn, o_ff, o_final, o_pw, o_pb, o_q, o_k, o_v, o_o, o_table, o_g, o_u, o_d, o_hw, o_hb,
+):
+    o_rebuilt[...] = rebuilt[...]
+    o_series[...] = series_grad[...]
+    for row, out in enumerate((o_attn, o_ff, o_final, o_pb)):
+        out[...] = sums[row : row + 1, :]
+    patch = o_pw.shape[0]
+    o_pw[...] = sums[8:16, :]
+    o_hw[...] = sums[16:24, :]
+    lane = iota((8, 128), 1)
+    column = jnp.sum(
+        jnp.where(lane == 2 * heads, sums[24:32, 0:128], 0.0), axis=1, keepdims=True
+    )
+    o_hb[...] = jnp.sum(jnp.where(lane == iota((8, 128), 0), column, 0.0), axis=0, keepdims=True)[
+        :, :patch
+    ]
+    head_index = lax.axis_index("head")
+    for which in range(2):
+        row = jnp.zeros((1, 128), F32)
+        for g in range(o_table.shape[1] // 8):
+            piece = sums[24:32, g * 128 : (g + 1) * 128]
+            column = jnp.sum(
+                jnp.where(lane == 2 * head_index + which, piece, 0.0), axis=1, keepdims=True
+            )
+            row = row + jnp.sum(
+                jnp.where(lane == 8 * g + iota((8, 128), 0), column, 0.0), axis=0, keepdims=True
+            )
+        o_table[which : which + 1, :] = row[:, : o_table.shape[1]]
+    first = 0
+    for out, turn in ((o_q, False), (o_k, False), (o_v, False), (o_o, True), (o_g, False), (o_u, False), (o_d, True)):
+        width = out.shape[0] if turn else out.shape[1]
+        block = fin[:, first : first + width].astype(F32)
+        out[...] = block.T if turn else block
+        first += width
 
 
 def layer_call(groups, heads, args):
@@ -931,7 +1012,7 @@
     tokens = rows * length
     part = args[9].shape[1]
     ff = args[14].shape[1]
-    table_rows, table_heads = args[13].shape
+    table_heads, table_rows = args[13].shape
     total = heads * (4 * part + 3 * ff)
     bits = groups.bit_length() - 1
     levels = bits + heads.bit_length() - 1
@@ -943,45 +1024,53 @@
         embedded=((tokens, width), F32), s_attn=((tokens, 1), F32), attn_in=((tokens, width), BF16),
         qkv=((tokens, heads * 3 * part), BF16), tab=((heads, table_rows, 128), F32),
         bias=((heads, length, 128), F32), probs=((heads, tokens, 128), F32),
-        ctx=((tokens, heads * part), BF16), ff_in=((tokens, width), BF16),
-        inner=((tokens, heads * ff), BF16), act=((TILE, heads * ff), BF16),
-        slope=((TILE, heads * ff), BF16), final_in=((tokens, width), BF16),
-        d_end_low=((tokens, width), BF16), dgu=((tokens, heads * 2 * ff), BF16),
-        d_mid=((tokens, width), F32), d_mid_low=((tokens, width), BF16),
+        ctx=((tokens, heads * part), BF16), hidden_mid=((tokens, width), F32),
+        ff_in=((tokens, width), BF16), inner=((tokens, heads * ff), BF16),
+        act=((tokens, heads * ff), BF16), slope=((tokens, heads * ff), BF16),
+        final_in=((tokens, width), BF16), d_end_low=((tokens, width), BF16),
+        dgu=((tokens, heads * 2 * ff), BF16), d_mid=((tokens, width), F32),
         d_ctx=((tokens, heads * part), BF16), dsum=((heads, length, 128), F32),
-        g_attn=((8, width), F32), g_ff=((8, width), F32),
-        g_final=((8, width), F32), g_bias=((8, width), F32), tgr=((table_rows, 128), F32),
+        g_attn=((8, width), F32), g_ff=((8, width), F32), g_final=((8, width), F32),
+        g_bias=((8, width), F32), tgr=((table_rows, 128), F32),
         left_t=((width, tokens), BF16), right_t=((width, tokens), BF16),
-        wq=((width, heads * 3 * part), BF16), wo=((width, heads * part), BF16),
-        wg=((width, heads * 2 * ff), BF16), wd=((width, heads * ff), BF16),
-        own=((width // 2, total), F32), snd0=((width // 2, total), BF16),
-        rcv0=((width // 2, total), BF16), snd1=((width // 4, total), BF16),
-        rcv1=((width // 4, total), BF16), snd2=((width // 8, total), BF16),
-        rcv2=((width // 8, total), BF16), sndz=((width // 8, total), BF16),
-        rcvz=((heads - 1, width // 8, total // heads), BF16),
+        weights=((width, total), BF16), own=((width // 2, total), BF16),
+        snd0=((width // 2, total), BF16), rcv0=((width // 2, total), BF16),
+        snd1=((width // 4, total), BF16), rcv1=((width // 4, total), BF16),
+        snd2=((width // 8, total), BF16), rcv2=((width // 8, total), BF16),
+        sndz=((width // 8, total), BF16), rcvz=((heads - 1, width // 8, total // heads), BF16),
+        fin=((width, total // heads), BF16),
         slabs=((levels + 1, 32, width), F32), inbox=((levels, 32, width), F32),
     )
     if bits > 3:
         scratch["extra"] = ((bits - 3, width // 8, total), BF16)
-    copies = 4 * 2 * (heads - 1 + 3) + heads - 1 + 4 * (10 + heads - 1 + 2 * (bits - 3)) + levels
-    outs = [
-        (rows, steps), (rows, steps), (1, width), (1, width), (1, width), (patch, width), (1, width),
-        (width, part), (width, part), (width, part), (part, width), (table_rows, table_heads),
-        (width, ff), (width, ff), (ff, width), (width, patch), (1, patch),
-    ]
+    copies = 7 * 2 * (heads - 1 + 3) + heads - 1 + 7 * (10 + heads - 1 + bits - 3) + levels
+    outs = [((rows, steps), F32), ((rows, steps), F32), ((32, width), F32), ((width, total // heads), BF16)]
     names = list(INPUTS + OUTPUTS) + list(scratch) + ["send_sems", "recv_sems"]
     vmem = pl.BlockSpec(memory_space=pltpu.VMEM)
-    return pl.pallas_call(
+    parts = pl.pallas_call(
         functools.partial(layer_kernel, groups, heads, names),
-        out_shape=[jax.ShapeDtypeStruct(shape, F32) for shape in outs],
+        out_shape=[jax.ShapeDtypeStruct(*out) for out in outs],
         in_specs=[vmem] * len(INPUTS),
         out_specs=[vmem] * len(OUTPUTS),
         scratch_shapes=[pltpu.VMEM(*v) for v in scratch.values()]
         + [pltpu.SemaphoreType.DMA((copies,)), pltpu.SemaphoreType.DMA((copies,))],
         compiler_params=pltpu.CompilerParams(
-            collective_id=0, has_side_effects=True, vmem_limit_bytes=61 * 1024 * 1024
+            collective_id=0, has_side_effects=True, vmem_limit_bytes=63 * 1024 * 1024
         ),
     )(*args)
+    shapes = [
+        (rows, steps), (rows, steps), (1, width), (1, width), (1, width), (patch, width), (1, width), (width, part), (width, part),
+        (width, part), (part, width), (table_heads, table_rows), (width, ff), (width, ff), (ff, width),
+        (patch, width), (1, patch),
+    ]
+    return list(
+        pl.pallas_call(
+            functools.partial(finish_kernel, heads),
+            out_shape=[jax.ShapeDtypeStruct(shape, F32) for shape in shapes],
+            in_specs=[vmem] * len(parts),
+            out_specs=[vmem] * len(shapes),
+        )(*parts)
+    )
 
 
 def solution(mesh):
@@ -989,11 +1078,16 @@
 
     def local(*args):
         args = list(args)
-        for i in (2, 4, 5, 6, 8, 18):
+        for i in (2, 18):
             args[i] = args[i].reshape(1, -1)
-        outs = list(layer_call(groups, heads, args))
+        for i in (4, 5, 6, 8):
+            args[i] = args[i].reshape(-1, 128)
+        for i in (13, 17):
+            args[i] = args[i].T
+        outs = layer_call(groups, heads, args)
         for i in (2, 3, 4, 6, 16):
             outs[i] = outs[i].reshape(-1)
+        outs[11], outs[15] = outs[11].T, outs[15].T
         return tuple(outs)
 
     both = P(("dp", "head"), None)

time: 149 us -> 114 us (0.77)
  local copies, waits for them, and re-layouts: 19.6 us -> 0 us
  Pallas kernels: 128 us -> 113 us
    pallas_call x1, Pallas kernels: 128 us -> 109 us  [layer_call(): pl.pallas_call(functools.partial(layer_kernel, groups, heads, names), out...]
    unnamed x61 -> x0, local copies, waits for them, and re-layouts: 17.2 us -> none
    pallas_call x0 -> x1, Pallas kernels: none -> 3.1 us  [layer_call(): pl.pallas_call(functools.partial(finish_kernel, heads), out_shape=[jax.Sh...]
    reshape x4 -> x0, local copies, waits for them, and re-layouts: 2.32 us -> none  [local(): args[i] = args[i].reshape(1, -1)]
where the time goes in v3:
time: 114 us; the launch traced here: 113 us
  Pallas kernels  113 us (99%)
    pallas_call x1, Pallas kernels, layer_call(): pl.pallas_call(functools.partial(layer_kernel, groups, heads, names), out...  109 us
    pallas_call x1, Pallas kernels, layer_call(): pl.pallas_call(functools.partial(finish_kernel, heads), out_shape=[jax.Sh...  3.1 us

profile of v3, /device:TPU:0, one launch (start us, length us, event | category | flops | bytes accessed | tf_op | source)
XLA Modules:
  0.0 113.3 jit_solution(14549270549439210374)
XLA Ops:
  0.7 109.4 %shard_map.314 = (f32[16,512]{1,0:T(8,128)}, f32[16,512]{1,0:T(8,128)}, f32[32,512]{1,0:T(8,128)}, bf16[512,1280]{1,0:T(8,128)(2,1)}) custom-call(f32[16,512]{1,0:T(8,128)} %refs_0_.1, s32[16,512]{1,0:T(8,128)} %refs_1_.1, s32[1,64]{1,0:T(1,128)} %bitcast.20, f32[16,512]{1,0:T(8,128)} %refs_3_.1, bf16[4,128]{1,0:T(4,128)(2,1)} %bitcast.16, ...), custom_call_target="tpu_custom_call" | custom-call | tf_op jit(solution)/shard_map/pallas_call | solution.py:1050
  110.1 3.1 %shard_map.315 = (f32[16,512]{1,0:T(8,128)}, f32[16,512]{1,0:T(8,128)}, f32[1,512]{1,0:T(1,128)}, f32[1,512]{1,0:T(1,128)}, f32[1,512]{1,0:T(1,128)}, /*index=5*...) custom-call(f32[16,512]{1,0:T(8,128)} %get-tuple-element.38.rebuilt,, ...), custom_call_target="tpu_custom_call" | custom-call | tf_op jit(solution)/shard_map/pallas_call | solution.py:1067

commit v4 on v3

v4 whole, which is shorter than its diff:
```python
import functools
import math

import jax
import jax.numpy as jnp
from jax import lax
from jax.experimental import pallas as pl
from jax.experimental.pallas import tpu as pltpu
from jax.sharding import PartitionSpec as P

F32 = jnp.float32
BF16 = jnp.bfloat16
EPS = 1e-06
TILE = 256
MAX_DIST = 128


def bucket_cuts(buckets, length):
    half_count = buckets // 2
    exact_count = half_count // 2
    ids = []
    for distance in range(length):
        if distance < exact_count:
            ids.append(distance)
        else:
            ids.append(
                min(
                    half_count - 1,
                    exact_count
                    + int(
                        math.log(distance / exact_count)
                        / math.log(MAX_DIST / exact_count)
                        * (half_count - exact_count)
                    ),
                )
            )
    cuts = []
    for distance in range(1, length):
        cuts += [distance] * (ids[distance] - ids[distance - 1])
    return cuts, ids[-1]


def nt(left, right):
    return lax.dot_general(left, right, (((1,), (1,)), ((), ())), preferred_element_type=F32)


def nn(left, right):
    return jnp.dot(left, right, preferred_element_type=F32)


def tn(left, right):
    return lax.dot_general(left, right, (((0,), (0,)), ((), ())), preferred_element_type=F32)


def iota(shape, dim):
    return lax.broadcasted_iota(jnp.int32, shape, dim)


def fold8(values):
    return jnp.sum(values.reshape(values.shape[0] // 8, 8, values.shape[1]), axis=0)


def row_scale(values):
    return lax.rsqrt(jnp.mean(values * values, axis=-1, keepdims=True) + EPS)


def norm_back(grad_out, unit_rows, scale, gain_row):
    d_unit = grad_out * gain_row
    spread = jnp.mean(d_unit * unit_rows, axis=-1, keepdims=True)
    return scale * (d_unit - unit_rows * spread), fold8(grad_out * unit_rows)


class Layer:
    more = None

    def __init__(self, **refs):
        self.__dict__.update(refs)

    def prepare(self, head_index):
        rows, steps = self.series.shape
        half = steps // 2
        length = self.pm.shape[0]
        patch = steps // length
        split_row = self.split[...].astype(F32)
        pick = iota((rows, split_row.shape[1]), 1) == (
            iota((rows, split_row.shape[1]), 0) + head_index * rows
        )
        split_col = jnp.sum(jnp.where(pick, split_row, 0.0), axis=1, keepdims=True)
        self.splitb[...] = jnp.broadcast_to(split_col, self.splitb.shape)
        obs = self.observed[...].astype(F32)
        series = self.series[...]
        low_half = iota((rows, steps), 1) < half

        def halves(values):
            return [
                jnp.sum(values[:, :half], axis=1, keepdims=True),
                jnp.sum(values[:, half:], axis=1, keepdims=True),
            ]

        def combine(sums):
            both = sums[0] + sums[1]
            return [split_col * one + (1.0 - split_col) * both for one in sums]

        def spread(pair):
            return jnp.where(low_half, pair[0], pair[1])

        self.halves, self.combine, self.spread = halves, combine, spread
        self.counts = combine(halves(obs))
        item_mean = [a / b for a, b in zip(combine(halves(obs * series)), self.counts)]
        centred = series - spread(item_mean)
        item_var = [a / b for a, b in zip(combine(halves(obs * centred * centred)), self.counts)]
        self.std = [jnp.sqrt(v + 1e-05) for v in item_var]
        std_full = spread(self.std)
        self.std_full, self.mean_full = std_full, spread(item_mean)
        normed = obs * centred / std_full
        self.normed[...] = normed
        self.normed_low[...] = normed.astype(BF16).astype(F32)
        self.dout_low[...] = (self.cot[...] * std_full).astype(BF16).astype(F32)
        self.pm[...] = (iota(self.pm.shape, 1) // patch == iota(self.pm.shape, 0)).astype(F32)
        fold = (iota(self.fold.shape, 1) % patch == iota(self.fold.shape, 0)).astype(BF16)
        self.fold[...] = fold
        pw = self.patch_w[...].astype(F32)
        self.row_attn, self.row_ff, self.row_final, self.row_bias = (
            jnp.concatenate(
                [source[i : i + 1, :].astype(F32) for i in range(source.shape[0])], axis=1
            )
            for source in (self.gain_attn, self.gain_ff, self.gain_final, self.patch_b)
        )
        self.ptile[...] = jnp.broadcast_to(
            pw[None], (self.ptile.shape[0] // patch, patch, pw.shape[1])
        ).reshape(self.ptile.shape).astype(BF16)
        self.htile[...] = tn(self.head_w[...], fold[:patch]).astype(BF16)
        hb = jnp.broadcast_to(self.head_b[...], (16, patch))
        self.hbias = nn(hb, fold[:patch])[0:1]

    def spread_rows(self, source, tile):
        rows_tile = TILE // self.pm.shape[0]
        mask = self.pm[...]
        pieces = [
            (source[pl.ds(tile * rows_tile + r, 1), :] * mask).astype(BF16)
            for r in range(rows_tile)
        ]
        return jnp.concatenate(pieces, axis=0)

    def gather_rows(self, target, tile, values, extra=None):
        length = self.pm.shape[0]
        mask = self.pm[...]
        for r in range(TILE // length):
            part = jnp.sum(values[r * length : (r + 1) * length] * mask, axis=0, keepdims=True)
            if extra is not None:
                part = part + extra
            target[pl.ds(tile * (TILE // length) + r, 1), :] = part

    def embed(self, tile):
        at = pl.ds(pl.multiple_of(tile * TILE, TILE), TILE)
        spread = self.spread_rows(self.normed_low, tile)
        self.p8t[:, at] = nt(self.fold[...], spread).astype(BF16)
        embedded = nn(spread, self.ptile[...]) + self.row_bias
        self.embedded[at, :] = embedded
        scale = row_scale(embedded)
        self.s_attn[at, :] = scale
        self.attn_in[at, :] = (embedded * scale * self.row_attn).astype(BF16)

    def buckets(self):
        length = self.pm.shape[0]
        lanes = 2 * length
        key = iota((length, lanes), 0)
        query = iota((length, lanes), 1) % length
        offset = key - query
        distance = jnp.abs(offset)
        table = self.tab.shape[1]
        cuts, top = bucket_cuts(table, length)
        ids = jnp.where(offset > 0, table // 2, 0)
        for cut in cuts:
            ids = ids + (distance >= cut).astype(jnp.int32)
        used = list(range(top + 1)) + list(range(table // 2, table // 2 + top + 1))
        return ids, used

    def own_table(self):
        table = self.table[...].astype(BF16)
        pick = (iota((2, 128), 1) // 64 == iota((2, 128), 0)).astype(BF16)
        self.tab[0] = tn(table, pick)

    def offsets(self, slot):
        ids, used = self.buckets()
        total = jnp.zeros(ids.shape, F32)
        for b in used:
            total = jnp.where(ids == b, self.tab[slot, b : b + 1, :], total)
        self.bias[slot] = total

    def head_masks(self):
        lane = iota((1, 128), 1)
        return (lane < 64).astype(BF16), (lane >= 64).astype(BF16)

    def attend(self, tile):
        at = pl.ds(pl.multiple_of(tile * TILE, TILE), TILE)
        length = self.pm.shape[0]
        rows_tile = TILE // length
        even, odd = self.head_masks()
        half = length // 2
        shape = (length, 2 * length)
        block = (iota(shape, 0) // half != (iota(shape, 1) % length) // half).astype(F32) * -1e30
        splits = [self.splitb[pl.ds(tile * rows_tile + r, 1), :] * block for r in range(rows_tile)]
        width = self.ctx.shape[1]
        projected = []
        for i in range(3):
            part = nn(self.attn_in[at, :], self.wq[:, i * width : (i + 1) * width]).astype(BF16)
            self.qkv[at, i * width : (i + 1) * width] = part
            projected.append(part)
        items = [(s, r) for s in range(self.slots) for r in range(rows_tile)]

        def piece(s, r, i):
            return projected[i][r * length : (r + 1) * length, s * 128 : (s + 1) * 128]

        scores = []
        for s, r in items:
            query = piece(s, r, 0)
            both = jnp.concatenate([query * even, query * odd], axis=0)
            scores.append(nt(piece(s, r, 1), both))
        turned = []
        for (s, r), score in zip(items, scores):
            score = score + (self.bias[s] + splits[r])
            top = jnp.max(score, axis=0, keepdims=True)
            raised = jnp.exp(score - top)
            probs = raised * (1.0 / jnp.sum(raised, axis=0, keepdims=True))
            self.probs[
                s, pl.ds(pl.multiple_of(tile * TILE + r * length, length), length), :
            ] = probs.astype(self.probs.dtype)
            turned.append(probs.astype(BF16))
        turned = [probs.T for probs in turned]
        mixed = [nn(probs, piece(s, r, 2)) for probs, (s, r) in zip(turned, items)]
        low_lanes = iota((1, 128), 1) < 64
        for s in range(self.slots):
            self.ctx[at, s * 128 : (s + 1) * 128] = jnp.concatenate(
                [
                    jnp.where(low_lanes, m[:length], m[length:]).astype(BF16)
                    for m in mixed[s * rows_tile : (s + 1) * rows_tile]
                ],
                axis=0,
            )

    def middle_gate(self, tile):
        at = pl.ds(pl.multiple_of(tile * TILE, TILE), TILE)
        hidden_mid = self.embedded[at, :] + nt(self.ctx[at, :], self.wo[...])
        self.hidden_mid[at, :] = hidden_mid
        ff_in = (hidden_mid * row_scale(hidden_mid) * self.row_ff).astype(BF16)
        self.ff_in[at, :] = ff_in
        total = self.inner.shape[1]
        block = 256
        c = math.sqrt(2.0 / math.pi)
        for first in range(0, total, block):
            cols = slice(first, first + block)
            gate = nn(ff_in, self.wg[:, first : first + block])
            up = nn(ff_in, self.wg[:, total + first : total + first + block])
            square = gate * gate
            t = jnp.tanh(gate * (c + (c * 0.044715) * square))
            plus = 0.5 * (1.0 + t)
            act = gate * plus
            slope = plus + (0.5 * gate) * (1.0 - t * t) * (c + (3.0 * c * 0.044715) * square)
            self.inner[at, cols] = (act * up).astype(BF16)
            self.act[at, cols] = act.astype(BF16)
            self.slope[at, cols] = (up * slope).astype(BF16)

    def cotangent(self, tile):
        at = pl.ds(pl.multiple_of(tile * TILE, TILE), TILE)
        d_spread = self.spread_rows(self.dout_low, tile)
        self.d8t[:, at] = nt(self.fold[...], d_spread).astype(BF16)
        self.d_mid[at, :] = nt(d_spread, self.htile[...])

    def outputs(self, tile):
        at = pl.ds(pl.multiple_of(tile * TILE, TILE), TILE)
        self.gather_rows(
            self.output, tile, nn(self.final_in[at, :], self.htile[...]), self.hbias
        )

    def middle_down(self, tile):
        at = pl.ds(pl.multiple_of(tile * TILE, TILE), TILE)
        hidden_end = self.hidden_mid[at, :] + nt(self.inner[at, :], self.wd[...])
        final_scale = row_scale(hidden_end)
        final_unit = hidden_end * final_scale
        gain_final = self.row_final
        final_in = (final_unit * gain_final).astype(BF16)
        self.final_in[at, :] = final_in
        d_end, gain_part = norm_back(self.d_mid[at, :], final_unit, final_scale, gain_final)
        self.g_final[...] += gain_part
        self.d_end_low[at, :] = d_end.astype(BF16)
        self.d_mid[at, :] = d_end

    def inner_back(self, tile):
        at = pl.ds(pl.multiple_of(tile * TILE, TILE), TILE)
        d_low = self.d_end_low[at, :]
        total = self.inner.shape[1]
        block = 256
        for first in range(0, total, block):
            cols = slice(first, first + block)
            d_inner = nn(d_low, self.wd[:, cols])
            d_gate = (d_inner * self.slope[at, cols].astype(F32)).astype(BF16)
            d_up = (d_inner * self.act[at, cols].astype(F32)).astype(BF16)
            self.dgu[at, cols] = d_gate
            self.dgu[at, total + first : total + first + block] = d_up

    def middle_back(self, tile):
        at = pl.ds(pl.multiple_of(tile * TILE, TILE), TILE)
        d_in = nt(self.dgu[at, :], self.wg[...])
        hidden_mid = self.hidden_mid[at, :]
        ff_scale = row_scale(hidden_mid)
        d_norm, gain_part = norm_back(d_in, hidden_mid * ff_scale, ff_scale, self.row_ff)
        self.g_ff[...] += gain_part
        d_mid = self.d_mid[at, :] + d_norm
        self.d_mid[at, :] = d_mid
        d_mid_low = d_mid.astype(BF16)
        self.d_mid_low[at, :] = d_mid_low
        self.d_ctx[at, :] = nn(d_mid_low, self.wo[...]).astype(BF16)

    def attend_back(self, tile):
        width = self.ctx.shape[1]
        length = self.pm.shape[0]
        rows_tile = TILE // length
        even, odd = self.head_masks()
        items = [(s, r) for s in range(self.slots) for r in range(rows_tile)]
        rows = [
            pl.ds(pl.multiple_of(tile * TILE + r * length, length), length)
            for r in range(rows_tile)
        ]

        def piece(s, r, i):
            return self.qkv[rows[r], i * width + s * 128 : i * width + (s + 1) * 128]

        d_both = []
        for s, r in items:
            d_ctx = self.d_ctx[rows[r], s * 128 : (s + 1) * 128]
            d_both.append(jnp.concatenate([d_ctx * even, d_ctx * odd], axis=0))
        d_probs = [nt(piece(s, r, 2), both) for (s, r), both in zip(items, d_both)]
        probs = [self.probs[s, rows[r], :] for s, r in items]
        d_value = [nn(p.astype(BF16), both) for p, both in zip(probs, d_both)]
        d_scores = []
        for p, dp in zip(probs, d_probs):
            p = p.astype(F32)
            dots = jnp.sum(p * dp, axis=0, keepdims=True)
            d_scores.append((p * (dp - dots)).astype(BF16))
        turned = [d.T for d in d_scores]
        d_key = []
        for (s, r), d in zip(items, d_scores):
            query = piece(s, r, 0)
            d_key.append(nn(d, jnp.concatenate([query * even, query * odd], axis=0)))
        mixed = [nn(d, piece(s, r, 1)) for (s, r), d in zip(items, turned)]
        low_lanes = iota((1, 128), 1) < 64
        for n, (s, r) in enumerate(items):
            d_query = jnp.where(low_lanes, mixed[n][:length], mixed[n][length:])
            for i, grad in enumerate((d_query, d_key[n], d_value[n])):
                cols = slice(i * width + s * 128, i * width + (s + 1) * 128)
                self.dqkv[rows[r], cols] = grad.astype(BF16)
        for s in range(self.slots):
            total = self.dsum[s]
            for d in d_scores[s * rows_tile : (s + 1) * rows_tile]:
                total = total + d.astype(F32)
            self.dsum[s] = total

    def embed_back(self, tile):
        at = pl.ds(pl.multiple_of(tile * TILE, TILE), TILE)
        d_in = nt(self.dqkv[at, :], self.wq[...])
        scale = self.s_attn[at, :]
        d_norm, gain_part = norm_back(
            d_in, self.embedded[at, :] * scale, scale, self.row_attn
        )
        self.g_attn[...] += gain_part
        d_embedded = (self.d_mid[at, :] + d_norm).astype(BF16)
        self.d_emb[at, :] = d_embedded
        self.g_bias[...] += fold8(d_embedded.astype(F32))
        self.gather_rows(self.d_normed, tile, nt(d_embedded, self.ptile[...]))

    def finish(self):
        obs = self.observed[...].astype(F32)
        cot = self.cot[...]
        output = self.output[...]
        std_full, mean_full = self.std_full, self.mean_full
        self.rebuilt[...] = output * std_full + mean_full
        d_normed = self.d_normed[...]
        std_grad = [
            a - b / c
            for a, b, c in zip(
                self.halves(cot * output), self.halves(d_normed * self.normed[...]), self.std
            )
        ]
        var_weight = self.combine(
            [g / (2.0 * s) / n for g, s, n in zip(std_grad, self.std, self.counts)]
        )
        centred = self.series[...] - mean_full
        d_centred = d_normed * obs / std_full + 2.0 * obs * centred * self.spread(var_weight)
        mean_grad = [a - b for a, b in zip(self.halves(cot), self.halves(d_centred))]
        mean_weight = self.combine([g / n for g, n in zip(mean_grad, self.counts)])
        self.series_grad[...] = d_centred + obs * self.spread(mean_weight)

    def head_grad(self):
        self.small[16:24, :] = nn(self.d8t[...], self.final_in[...])[0:8]

    def small_grads(self, head_index):
        small = self.small
        heads = self.slots
        self.head_grad()
        zero = jnp.zeros((4, self.embedded.shape[1]), F32)
        small[0:8, :] = jnp.concatenate(
            [jnp.sum(r[...], axis=0, keepdims=True) for r in (self.g_attn, self.g_ff, self.g_final, self.g_bias)]
            + [zero],
            axis=0,
        )
        small[8:16, :] = nn(self.p8t[...], self.d_emb[...])[0:8]
        lane = iota((8, 128), 1)
        groups = self.tab.shape[1] // 8
        pieces = [jnp.zeros((8, 128), F32) for _ in range(groups)]
        pieces[0] = jnp.where(
            lane == 2 * heads, jnp.sum(self.d8t[0:8, :].astype(F32), axis=1, keepdims=True), 0.0
        )
        ids, used = self.buckets()
        for s in range(self.slots):
            dsum = self.dsum[s]
            owner = lax.rem(head_index + s, heads)
            for b in range(self.tab.shape[1]):
                if b in used:
                    self.tgr[b : b + 1, :] = jnp.sum(
                        jnp.where(ids == b, dsum, 0.0), axis=0, keepdims=True
                    )
                else:
                    self.tgr[b : b + 1, :] = jnp.zeros((1, 128), F32)
            for g in range(groups):
                rows = self.tgr[8 * g : 8 * g + 8, :]
                for which in range(2):
                    inside = (lane < 64) if which == 0 else (lane >= 64)
                    column = jnp.sum(jnp.where(inside, rows, 0.0), axis=1, keepdims=True)
                    pieces[g] = pieces[g] + jnp.where(lane == 2 * owner + which, column, 0.0)
        small[24:32, :] = jnp.concatenate(pieces, axis=1)

    def clear(self):
        for ref in (self.g_attn, self.g_ff, self.g_final, self.g_bias):
            ref[...] = jnp.zeros(ref.shape, F32)
        self.dsum[...] = jnp.zeros(self.dsum.shape, F32)


MESH = pl.DeviceIdType.MESH


TABLE, WEIGHTS, HALVES, QUARTERS, EIGHTHS, OWNERS, FIN, SMALL, PLANE, HEADS = range(-11, -1)


class Net:
    def __init__(self, groups, heads, send_sems, recv_sems):
        self.dp, self.head = lax.axis_index("dp"), lax.axis_index("head")
        self.bits = groups.bit_length() - 1
        self.heads = heads
        self.send_sems, self.recv_sems = send_sems, recv_sems
        self.recv_ids, self.send_ids = {}, {}

    def bit(self, which):
        return (self.dp // (1 << which)) % 2

    def across(self, *which):
        place = self.dp
        for one in which:
            place = place + (1 - 2 * self.bit(one)) * (1 << one)
        return (place, self.head)

    def beside(self, hops):
        return (self.dp, (self.head + hops) % self.heads)

    def plane(self):
        return [self.across(1), self.across(2), self.across(1, 2)]

    def partners(self):
        found = [self.across(b) for b in range(self.bits)] + [self.across(1, 2)]
        return found + [self.beside(t) for t in range(1, self.heads)]

    def greet_start(self):
        barrier = pltpu.get_barrier_semaphore()
        for partner in self.partners():
            pl.semaphore_signal(barrier, inc=1, device_id=partner, device_id_type=MESH)

    def greet_end(self):
        pl.semaphore_wait(pltpu.get_barrier_semaphore(), len(self.partners()))

    def copy(self, key, group, src, dst, device):
        recv = self.recv_ids.setdefault(key, len(self.recv_ids))
        send = self.send_ids.setdefault(group, len(self.send_ids))
        return pltpu.make_async_remote_copy(
            src_ref=src,
            dst_ref=dst,
            send_sem=self.send_sems.at[send],
            recv_sem=self.recv_sems.at[recv],
            device_id=device,
            device_id_type=MESH,
        )

    def send(self, key, group, src, dst, device):
        self.copy(key, group, src, dst, device).start()

    def arrived(self, key, group, bulk):
        self.copy(key, group, bulk, bulk, self.across(0)).wait_recv()

    def sent(self, group, bulk):
        self.copy(-1, group, bulk, bulk, self.across(0)).wait_send()


def rows_at(start, count, unit):
    return pl.ds(pl.multiple_of(start, unit), count)


class Gather:
    ORDERS = ((1, 2, 0), (2, 1, 0))

    def __init__(self, net, ref, name, first, width):
        self.net, self.ref, self.name = net, ref, name
        self.first, self.width = first, width
        self.heads = net.heads
        self.unit = ref.shape[0] // 16
        self.others = slice(first + width, first + self.heads * width)

    def block(self, half):
        bits = [self.net.bit(b) for b in self.ORDERS[half]]
        return bits[0] + 2 * bits[1] + 4 * bits[2]

    def span(self, half, level):
        size = 1 << level
        first = self.block(half) // size
        return rows_at((half * 8 + first * size) * self.unit, size * self.unit, self.unit)

    def start(self):
        net, first, width = self.net, self.first, self.width
        for half in range(2):
            rows = self.span(half, 0)
            for t in range(1, self.heads):
                slot = self.heads - t
                net.send(
                    (self.name, 0),
                    WEIGHTS,
                    self.ref.at[rows, first : first + width],
                    self.ref.at[rows, first + slot * width : first + (slot + 1) * width],
                    net.beside(t),
                )

    def step(self, level):
        net = self.net
        count = 2 * self.unit << max(level - 1, 0)
        net.arrived((self.name, level), WEIGHTS, self.ref.at[0:count, self.others])
        if level < 3:
            for half in range(2):
                place = self.ref.at[self.span(half, level), self.others]
                net.send(
                    (self.name, level + 1),
                    WEIGHTS,
                    place,
                    place,
                    net.across(self.ORDERS[half][level]),
                )


class Reduce:
    ORDERS = ((1, 2), (2, 1))

    def __init__(self, net, refs, name, first, width):
        self.__dict__.update(refs)
        self.net, self.name = net, name
        self.heads = net.heads
        self.width = width
        self.columns = slice(first, first + self.heads * width)
        self.fin_columns = slice(first // self.heads, first // self.heads + width)

    def slots(self, s):
        first = self.columns.start + s * self.width
        return slice(first, first + self.width)

    def partner(self, left_t, right):
        net, cols = self.net, self.columns
        count = self.own.shape[0]
        rows = rows_at((1 - net.bit(0)) * count, count, count)
        self.snd0[:, cols] = nn(left_t[rows, :], right[...]).astype(BF16)
        net.send(
            (self.name, 4), HALVES, self.snd0.at[:, cols], self.rcv0.at[:, cols], net.across(0)
        )

    def mine(self, left_t, right):
        count = self.own.shape[0]
        rows = rows_at(self.net.bit(0) * count, count, count)
        self.own[:, self.columns] = nn(left_t[rows, :], right[...]).astype(self.own.dtype)

    def kept(self, half, level):
        count = self.own.shape[0] // 2
        start = half * count
        for step in range(level):
            count = count // 2
            start = start + self.net.bit(self.ORDERS[half][step]) * count
        return start

    def halving(self, level):
        net, cols = self.net, self.columns
        source = (self.rcv0, self.rcv1, self.rcv2)[level]
        count = self.own.shape[0] // 2 >> level
        net.arrived((self.name, 4 + level), HALVES, source.at[:, cols])
        if level < 2:
            group = (QUARTERS, EIGHTHS)[level]
            send, target = ((self.snd1, self.rcv1), (self.snd2, self.rcv2))[level]
            part = count // 2
            for half in range(2):
                away = (1 - net.bit(self.ORDERS[half][level])) * part
                place = slice(half * part, (half + 1) * part)
                send[place, cols] = (
                    self.own[rows_at(self.kept(half, level) + away, part, 32), cols].astype(F32)
                    + source[rows_at(half * count + away, part, 32), cols].astype(F32)
                ).astype(BF16)
                net.send(
                    (self.name, 5 + level),
                    group,
                    send.at[place, cols],
                    target.at[place, cols],
                    net.across(self.ORDERS[half][level]),
                )
            for half in range(2):
                stay = net.bit(self.ORDERS[half][level]) * part
                rows = rows_at(self.kept(half, level) + stay, part, 32)
                self.own[rows, cols] = (
                    self.own[rows, cols].astype(F32)
                    + source[rows_at(half * count + stay, part, 32), cols].astype(F32)
                ).astype(self.own.dtype)
        else:
            for half in range(2):
                part = slice(half * count, (half + 1) * count)
                self.sndz[part, cols] = (
                    self.own[rows_at(self.kept(half, 2), count, 32), cols].astype(F32)
                    + source[part, cols].astype(F32)
                ).astype(BF16)

    def groups(self):
        net, cols = self.net, self.columns
        for bit in range(3, net.bits):
            inbox = self.extra.at[bit - 3]
            copy = net.copy(
                (self.name, 8 + bit),
                (self.name, bit),
                self.sndz.at[:, cols],
                inbox.at[:, cols],
                net.across(bit),
            )
            copy.start()
            copy.wait()
            self.sndz[:, cols] = (
                self.sndz[:, cols].astype(F32) + inbox[:, cols].astype(F32)
            ).astype(BF16)

    def owners(self):
        net = self.net
        for s in range(1, self.heads):
            net.send(
                (self.name, 7),
                OWNERS,
                self.sndz.at[:, self.slots(s)],
                self.rcvz.at[s - 1, :, self.fin_columns],
                net.beside(s),
            )

    def place(self, half, level):
        net = self.net
        quarter = self.fin.shape[0] // 4
        count = quarter // 4
        start = net.bit(0) * 2 * quarter + half * quarter
        order = self.ORDERS[half]
        start = start + net.bit(order[0]) * 2 * count
        if level == 0:
            return rows_at(start + net.bit(order[1]) * count, count, count)
        return rows_at(start, 2 * count, count)

    def owned(self):
        net, fin = self.net, self.fin_columns
        count = self.sndz.shape[0] // 2
        net.arrived((self.name, 7), OWNERS, self.rcvz.at[:, :, fin])
        for half in range(2):
            part = slice(half * count, (half + 1) * count)
            total = self.sndz[part, self.slots(0)].astype(F32)
            for s in range(1, self.heads):
                total = total + self.rcvz[s - 1, part, fin].astype(F32)
            rows = self.place(half, 0)
            self.fin[rows, fin] = total.astype(BF16)
            place = self.fin.at[rows, fin]
            net.send((self.name, 8), FIN, place, place, net.across(self.ORDERS[half][1]))

    def spread(self, level):
        net, fin = self.net, self.fin_columns
        rows = self.fin.shape[0]
        count = (rows // 8, rows // 4, rows // 2)[level]
        net.arrived((self.name, 8 + level), FIN, self.fin.at[0:count, fin])
        if level == 0:
            for half in range(2):
                place = self.fin.at[self.place(half, 1), fin]
                net.send((self.name, 9), FIN, place, place, net.across(self.ORDERS[half][0]))
        if level == 1:
            place = self.fin.at[rows_at(net.bit(0) * (rows // 2), rows // 2, rows // 2), fin]
            net.send((self.name, 10), FIN, place, place, net.across(0))
        if level == 2:
            pltpu.make_async_copy(
                self.fin.at[:, fin], self.fin_out.at[:, fin], self.out_sem
            ).start()

    def steps(self):
        return [
            lambda: self.halving(0),
            lambda: self.halving(1),
            lambda: (self.halving(2), self.groups(), self.owners()),
            self.owned,
            lambda: self.spread(0),
            lambda: self.spread(1),
            lambda: self.spread(2),
        ]


class Total:
    def __init__(self, net, small, core_in, plane, more, across):
        self.net, self.small, self.core_in = net, small, core_in
        self.plane, self.more, self.heads = plane, more, across

    def start(self):
        net = self.net
        net.send(SMALL, SMALL, self.small, self.core_in, net.across(0))

    def cores(self):
        net = self.net
        net.arrived(SMALL, SMALL, self.core_in)
        here = net.bit(1) + 2 * net.bit(2)
        self.plane[here] = (self.small[...] + self.core_in[...]).astype(BF16)
        for partner in net.plane():
            net.send(PLANE, PLANE, self.plane.at[here], self.plane.at[here], partner)

    def chips(self):
        net = self.net
        net.arrived(PLANE, PLANE, self.plane.at[0:3])
        total = self.summed(self.plane, 4)
        for bit in range(3, net.bits):
            mine, theirs = self.more.at[2 * (bit - 3)], self.more.at[2 * (bit - 3) + 1]
            mine[...] = total.astype(BF16)
            copy = net.copy((SMALL, bit), (SMALL, bit), mine, theirs, net.across(bit))
            copy.start()
            copy.wait()
            total = mine[...].astype(F32) + theirs[...].astype(F32)
        self.heads[net.head] = total.astype(BF16)
        for t in range(1, net.heads):
            place = self.heads.at[net.head]
            net.send(HEADS, HEADS, place, place, net.beside(t))

    def done(self):
        net = self.net
        net.arrived(HEADS, HEADS, self.heads.at[1 : net.heads])
        return self.summed(self.heads, net.heads)

    def summed(self, ref, count):
        total = ref[0].astype(F32)
        for i in range(1, count):
            total = total + ref[i].astype(F32)
        return total


def loop(count, body):
    def once(i, carry):
        body(i)
        return carry

    lax.fori_loop(0, count, once, 0)


CHUNKS = 10
Q, K, V, O, G1, G2, U1, U2, D1, D2 = range(CHUNKS)
ORDER = (
    0, 46, 60, 74, 88, 1, 2, 3, 4, 5, 6, 7, 47, 102, 61, 130, 75, 116, 48, 89, 144, 62, 103, 158,
    76, 49, 131, 172, 90, 50, 117, 63, 104, 64, 145, 77, 132, 159, 78, 8, 91, 118, 173, 9, 92, 105,
    146, 10, 106, 133, 11, 160, 134, 119, 174, 120, 147, 148, 12, 161, 13, 162, 175, 14, 176, 15,
    16, 17, 18, 19, 38, 163, 177, 164, 178, 39, 20, 165, 179, 21, 22, 23, 107, 121, 135, 149, 108,
    122, 136, 150, 24, 109, 166, 123, 137, 151, 25, 180, 26, 27, 40, 110, 93, 94, 41, 167, 28, 95,
    124, 29, 30, 138, 31, 51, 65, 79, 52, 152, 66, 80, 32, 168, 181, 111, 53, 67, 81, 33, 96, 34,
    125, 139, 35, 169, 153, 42, 182, 54, 36, 43, 112, 37, 68, 126, 82, 97, 170, 183, 140, 55, 171,
    154, 113, 44, 69, 127, 83, 98, 184, 141, 155, 114, 185, 56, 128, 115, 99, 129, 142, 156, 57,
    143, 157, 45, 100, 70, 101, 58, 84, 59, 71, 85, 72, 73, 86, 87,
)


def inputs(
    series, observed, split, cot, gain_attn, gain_ff, gain_final, patch_w, patch_b, wq_in, wk_in,
    wv_in, wo_in, table, wg_in, wu_in, wd_in, head_w, head_b, rebuilt, series_grad, sums, fin_out,
):
    return locals()


def layer_kernel(groups, heads, names, *refs):
    count = len(refs) - len(names) - 3
    named = inputs(*refs[:count])
    named.update(zip(names, refs[count:]))
    send_sems, recv_sems, out_sem = refs[-3:]
    layer = Layer(slots=heads, **named)
    weights, dgu, fin = layer.weights, layer.dgu, layer.fin
    width = layer.wq_in.shape[1]
    block = heads * width
    layer.wq = weights.at[:, Q * block : O * block]
    layer.wo = weights.at[:, O * block : G1 * block]
    layer.wg = weights.at[:, G1 * block : D1 * block]
    layer.wd = weights.at[:, D1 * block :]
    layer.dqkv = dgu.at[:, 0 : O * block]
    layer.d_emb = layer.ff_in
    tiles = layer.embedded.shape[0] // TILE
    net = Net(groups, heads, send_sems, recv_sems)
    left, right = layer.left_t, layer.right_t

    def own():
        for chunk, ref in ((Q, layer.wq_in), (K, layer.wk_in), (V, layer.wv_in)):
            weights[:, chunk * block : chunk * block + width] = ref[...]
        weights[:, O * block : O * block + width] = layer.wo_in[...].T
        for i in range(layer.wg_in.shape[1] // width):
            cols = slice(i * width, (i + 1) * width)
            for chunk, part in (
                (G1 + i, layer.wg_in[:, cols]),
                (U1 + i, layer.wu_in[:, cols]),
                (D1 + i, layer.wd_in[cols, :].T),
            ):
                weights[:, chunk * block : chunk * block + width] = part
        layer.own_table()

    def greet():
        net.greet_end()
        for t in range(1, heads):
            net.send(TABLE, TABLE, layer.tab.at[0], layer.tab.at[heads - t], net.beside(t))

    def offsets():
        net.arrived(TABLE, TABLE, layer.tab.at[1:heads])
        loop(heads, layer.offsets)

    def turn(target, source):
        target[...] = source[...].T

    def sums():
        layer.sums[...] = total.done()

    total = Total(net, layer.small, layer.core_in, layer.plane, layer.more, layer.heads_in)
    tasks = [
        greet,
        lambda: (layer.clear(), layer.prepare(net.head)),
        lambda: loop(tiles, layer.embed),
        offsets,
    ]
    for body in (
        layer.cotangent,
        layer.attend,
        layer.middle_gate,
        layer.middle_down,
        layer.inner_back,
        layer.middle_back,
        layer.attend_back,
        layer.embed_back,
    ):
        tasks += [functools.partial(body, t) for t in range(tiles)]
    tasks += [
        lambda: loop(tiles, layer.outputs),
        layer.finish,
        lambda: turn(right, layer.d_end_low),
        lambda: turn(left, layer.ff_in),
        lambda: turn(right, layer.d_mid_low),
        lambda: turn(left, layer.attn_in),
        lambda: (layer.small_grads(net.head), total.start()),
        total.cores,
        total.chips,
        sums,
    ]
    sources = [(left, layer.dqkv, i) for i in range(3)] + [(right, layer.ctx, 0)]
    sources += [(left, dgu, i) for i in range(4)] + [(right, layer.inner, i) for i in range(2)]
    named.update(out_sem=out_sem)
    for chunk, (turned, source, i) in enumerate(sources):
        gather = Gather(net, weights, chunk, chunk * block, width)
        reduce = Reduce(net, named, chunk, chunk * block, width)
        source = source.at[:, i * block : (i + 1) * block]
        tasks += [gather.start] + [functools.partial(gather.step, level) for level in range(4)]
        tasks += [
            functools.partial(reduce.partner, turned, source),
            functools.partial(reduce.mine, turned, source),
        ]
        tasks += reduce.steps()

    net.greet_start()
    own()
    for place in ORDER:
        tasks[place]()
    slots = heads - 1
    pltpu.make_async_copy(fin, layer.fin_out, out_sem).wait()
    net.sent(TABLE, layer.tab.at[1:heads])
    net.sent(WEIGHTS, weights.at[:, 0 : slots * fin.shape[1]])
    net.sent(HALVES, layer.snd0)
    net.sent(QUARTERS, layer.snd1)
    net.sent(EIGHTHS, layer.snd2)
    net.sent(OWNERS, layer.sndz.at[:, 0 : slots * fin.shape[1]])
    net.sent(FIN, fin.at[0 : fin.shape[0] * 7 // 8])
    net.sent(SMALL, layer.small)
    net.sent(PLANE, layer.plane.at[0:3])
    net.sent(HEADS, layer.heads_in.at[1:heads])


def finish_kernel(
    heads, rebuilt, series_grad, sums, fin, o_rebuilt, o_series, o_attn, o_ff, o_final, o_pw, o_pb, o_q, o_k, o_v, o_o, o_table, o_g, o_u, o_d, o_hw, o_hb,
):
    o_rebuilt[...] = rebuilt[...]
    o_series[...] = series_grad[...]
    for row, out in enumerate((o_attn, o_ff, o_final, o_pb)):
        out[...] = sums[row : row + 1, :]
    patch = o_pw.shape[0]
    o_pw[...] = sums[8:16, :]
    o_hw[...] = sums[16:24, :]
    lane = iota((8, 128), 1)
    column = jnp.sum(
        jnp.where(lane == 2 * heads, sums[24:32, 0:128], 0.0), axis=1, keepdims=True
    )
    o_hb[...] = jnp.sum(jnp.where(lane == iota((8, 128), 0), column, 0.0), axis=0, keepdims=True)[
        :, :patch
    ]
    head_index = lax.axis_index("head")
    for which in range(2):
        row = jnp.zeros((1, 128), F32)
        for g in range(o_table.shape[1] // 8):
            piece = sums[24:32, g * 128 : (g + 1) * 128]
            column = jnp.sum(
                jnp.where(lane == 2 * head_index + which, piece, 0.0), axis=1, keepdims=True
            )
            row = row + jnp.sum(
                jnp.where(lane == 8 * g + iota((8, 128), 0), column, 0.0), axis=0, keepdims=True
            )
        o_table[which : which + 1, :] = row[:, : o_table.shape[1]]
    first = 0
    for out, turn in ((o_q, False), (o_k, False), (o_v, False), (o_o, True), (o_g, False), (o_u, False), (o_d, True)):
        width = out.shape[0] if turn else out.shape[1]
        block = fin[:, first : first + width].astype(F32)
        out[...] = block.T if turn else block
        first += width


def layer_call(groups, heads, args):
    series = args[0]
    rows, steps = series.shape
    patch, width = args[7].shape
    length = steps // patch
    tokens = rows * length
    part = args[9].shape[1]
    ff = args[14].shape[1]
    table_heads, table_rows = args[13].shape
    total = heads * (4 * part + 3 * ff)
    bits = groups.bit_length() - 1
    scratch = dict(
        pm=((length, steps), F32), fold=((16, steps), BF16), ptile=((steps, width), BF16),
        htile=((width, steps), BF16), splitb=((rows, 128), F32), normed=((rows, steps), F32),
        normed_low=((rows, steps), F32), dout_low=((rows, steps), F32), output=((rows, steps), F32),
        d_normed=((rows, steps), F32), p8t=((16, tokens), BF16), d8t=((16, tokens), BF16),
        embedded=((tokens, width), F32), s_attn=((tokens, 1), F32), attn_in=((tokens, width), BF16),
        qkv=((tokens, heads * 3 * part), BF16), tab=((heads, table_rows, 128), F32),
        bias=((heads, length, 128), F32), probs=((heads, tokens, 128), F32),
        ctx=((tokens, heads * part), BF16), hidden_mid=((tokens, width), F32),
        ff_in=((tokens, width), BF16), inner=((tokens, heads * ff), BF16),
        act=((tokens, heads * ff), BF16), slope=((tokens, heads * ff), BF16),
        final_in=((tokens, width), BF16), d_end_low=((tokens, width), BF16),
        dgu=((tokens, heads * 2 * ff), BF16), d_mid=((tokens, width), F32),
        d_ctx=((tokens, heads * part), BF16), dsum=((heads, length, 128), F32),
        g_attn=((8, width), F32), g_ff=((8, width), F32), g_final=((8, width), F32),
        g_bias=((8, width), F32), tgr=((table_rows, 128), F32),
        left_t=((width, tokens), BF16), right_t=((width, tokens), BF16),
        weights=((width, total), BF16), own=((width // 2, total), BF16),
        snd0=((width // 2, total), BF16), rcv0=((width // 2, total), BF16),
        snd1=((width // 4, total), BF16), rcv1=((width // 4, total), BF16),
        snd2=((width // 8, total), BF16), rcv2=((width // 8, total), BF16),
        sndz=((width // 8, total), BF16), rcvz=((heads - 1, width // 8, total // heads), BF16),
        fin=((width, total // heads), BF16), small=((32, width), F32), core_in=((32, width), F32),
        plane=((4, 32, width), BF16), heads_in=((heads, 32, width), BF16),
        d_mid_low=((tokens, width), BF16),
    )
    extra = bits - 3
    if extra > 0:
        scratch.update(
            extra=((extra, width // 8, total), BF16), more=((2 * extra, 32, width), BF16)
        )
    copies = CHUNKS * (4 + 7 + extra) + 4 + extra + 1
    sends = 10 + (CHUNKS + 1) * extra
    outs = [((rows, steps), F32), ((rows, steps), F32), ((32, width), F32), ((width, total // heads), BF16)]
    vmem = pl.BlockSpec(memory_space=pltpu.VMEM)
    parts = pl.pallas_call(
        functools.partial(layer_kernel, groups, heads, list(scratch)),
        out_shape=[jax.ShapeDtypeStruct(*out) for out in outs],
        in_specs=[vmem] * len(args),
        out_specs=[vmem] * 3 + [pl.BlockSpec(memory_space=pl.ANY)],
        scratch_shapes=[pltpu.VMEM(*v) for v in scratch.values()]
        + [
            pltpu.SemaphoreType.DMA((sends,)),
            pltpu.SemaphoreType.DMA((copies,)),
            pltpu.SemaphoreType.DMA,
        ],
        compiler_params=pltpu.CompilerParams(
            collective_id=0, has_side_effects=True, vmem_limit_bytes=63 * 1024 * 1024
        ),
    )(*args)
    shapes = [
        (rows, steps), (rows, steps), (1, width), (1, width), (1, width), (patch, width), (1, width), (width, part), (width, part),
        (width, part), (part, width), (table_heads, table_rows), (width, ff), (width, ff), (ff, width),
        (patch, width), (1, patch),
    ]
    return list(
        pl.pallas_call(
            functools.partial(finish_kernel, heads),
            out_shape=[jax.ShapeDtypeStruct(shape, F32) for shape in shapes],
            in_specs=[vmem] * len(parts),
            out_specs=[vmem] * len(shapes),
        )(*parts)
    )


def solution(mesh):
    groups, heads = mesh.shape["dp"], mesh.shape["head"]

    def local(*args):
        args = list(args)
        for i in (2, 18):
            args[i] = args[i].reshape(1, -1)
        for i in (4, 5, 6, 8):
            args[i] = args[i].reshape(-1, 128)
        for i in (13, 17):
            args[i] = args[i].T
        outs = layer_call(groups, heads, args)
        for i in (2, 3, 4, 6, 16):
            outs[i] = outs[i].reshape(-1)
        outs[11], outs[15] = outs[11].T, outs[15].T
        return tuple(outs)

    both = P(("dp", "head"), None)
    by_column, by_row = P(None, "head"), P("head", None)
    return jax.shard_map(
        local,
        mesh=mesh,
        in_specs=(both, both, P("dp"), both) + (P(),) * 5 + (by_column,) * 3
        + (by_row, by_column, by_column, by_column, by_row, P(), P()),
        out_specs=(both, both) + (P(),) * 5 + (by_column,) * 3
        + (by_row, by_column, by_column, by_column, by_row, P(), P()),
        check_vma=False,
    )
```

time: 114 us -> 90.2 us (0.79)
  Pallas kernels: 113 us -> 89.2 us
    pallas_call x1, Pallas kernels: 109 us -> 86.1 us  [layer_call(): pl.pallas_call(functools.partial(layer_kernel, groups, heads, list(scratc...]
where the time goes in v4:
time: 90.2 us; the launch traced here: 90 us
  Pallas kernels  89.2 us (99%)
    pallas_call x1, Pallas kernels, layer_call(): pl.pallas_call(functools.partial(layer_kernel, groups, heads, list(scratc...  86.1 us
    pallas_call x1, Pallas kernels, layer_call(): pl.pallas_call(functools.partial(finish_kernel, heads), out_shape=[jax.Sh...  3.1 us

profile of v4, /device:TPU:0, one launch (start us, length us, event | category | flops | bytes accessed | tf_op | source)
XLA Modules:
  0.0 90.0 jit_solution(8730557066606077530)
XLA Ops:
  0.7 86.1 %shard_map.314 = (f32[16,512]{1,0:T(8,128)}, f32[16,512]{1,0:T(8,128)}, f32[32,512]{1,0:T(8,128)}, bf16[512,1280]{1,0:T(8,128)(2,1)}) custom-call(f32[16,512]{1,0:T(8,128)} %refs_0_.1, s32[16,512]{1,0:T(8,128)} %refs_1_.1, s32[1,64]{1,0:T(1,128)} %bitcast.20, f32[16,512]{1,0:T(8,128)} %refs_3_.1, bf16[4,128]{1,0:T(4,128)(2,1)} %bitcast.16, ...), custom_call_target="tpu_custom_call" | custom-call | tf_op jit(solution)/shard_map/pallas_call | solution.py:980
  86.8 3.1 %shard_map.315 = (f32[16,512]{1,0:T(8,128)}, f32[16,512]{1,0:T(8,128)}, f32[1,512]{1,0:T(1,128)}, f32[1,512]{1,0:T(1,128)}, f32[1,512]{1,0:T(1,128)}, /*index=5*...) custom-call(f32[16,512]{1,0:T(8,128)} %get-tuple-element.38.rebuilt,, ...), custom_call_target="tpu_custom_call" | custom-call | tf_op jit(solution)/shard_map/pallas_call | solution.py:1001

commit v5 on v4

--- a/solution.py
+++ b/solution.py
@@ -245,6 +245,7 @@
         self.hidden_mid[at, :] = hidden_mid
         ff_in = (hidden_mid * row_scale(hidden_mid) * self.row_ff).astype(BF16)
         self.ff_in[at, :] = ff_in
+        self.left_t[:, at] = ff_in.T
         total = self.inner.shape[1]
         block = 256
         c = math.sqrt(2.0 / math.pi)
@@ -283,7 +284,9 @@
         self.final_in[at, :] = final_in
         d_end, gain_part = norm_back(self.d_mid[at, :], final_unit, final_scale, gain_final)
         self.g_final[...] += gain_part
-        self.d_end_low[at, :] = d_end.astype(BF16)
+        d_low = d_end.astype(BF16)
+        self.d_end_low[at, :] = d_low
+        self.right_t[:, at] = d_low.T
         self.d_mid[at, :] = d_end
 
     def inner_back(self, tile):
@@ -309,10 +312,12 @@
         d_mid = self.d_mid[at, :] + d_norm
         self.d_mid[at, :] = d_mid
         d_mid_low = d_mid.astype(BF16)
-        self.d_mid_low[at, :] = d_mid_low
+        self.right_t[:, at] = d_mid_low.T
         self.d_ctx[at, :] = nn(d_mid_low, self.wo[...]).astype(BF16)
 
     def attend_back(self, tile):
+        at = pl.ds(pl.multiple_of(tile * TILE, TILE), TILE)
+        self.left_t[:, at] = self.attn_in[at, :].T
         width = self.ctx.shape[1]
         length = self.pm.shape[0]
         rows_tile = TILE // length
@@ -439,7 +444,7 @@
 MESH = pl.DeviceIdType.MESH
 
 
-TABLE, WEIGHTS, HALVES, QUARTERS, EIGHTHS, OWNERS, FIN, SMALL, PLANE, HEADS = range(-11, -1)
+TABLE, WEIGHTS, HALVES, FIRST, QUARTERS, EIGHTHS, OWNERS, FIN, SMALL, PLANE, HEADS = range(-12, -1)
 
 
 class Net:
@@ -466,8 +471,8 @@
         return [self.across(1), self.across(2), self.across(1, 2)]
 
     def partners(self):
-        found = [self.across(b) for b in range(self.bits)] + [self.across(1, 2)]
-        return found + [self.beside(t) for t in range(1, self.heads)]
+        found = [self.beside(t) for t in range(1, self.heads)] + [self.across(1, 2)]
+        return found + [self.across(b) for b in reversed(range(self.bits))]
 
     def greet_start(self):
         barrier = pltpu.get_barrier_semaphore()
@@ -522,8 +527,9 @@
         first = self.block(half) // size
         return rows_at((half * 8 + first * size) * self.unit, size * self.unit, self.unit)
 
-    def start(self):
+    def start(self, ready):
         net, first, width = self.net, self.first, self.width
+        ready()
         for half in range(2):
             rows = self.span(half, 0)
             for t in range(1, self.heads):
@@ -561,6 +567,7 @@
         self.heads = net.heads
         self.width = width
         self.columns = slice(first, first + self.heads * width)
+        self.summed = self.columns
         self.fin_columns = slice(first // self.heads, first // self.heads + width)
 
     def slots(self, s):
@@ -590,7 +597,7 @@
         return start
 
     def halving(self, level):
-        net, cols = self.net, self.columns
+        net, cols = self.net, self.summed
         source = (self.rcv0, self.rcv1, self.rcv2)[level]
         count = self.own.shape[0] // 2 >> level
         net.arrived((self.name, 4 + level), HALVES, source.at[:, cols])
@@ -628,7 +635,7 @@
                 ).astype(BF16)
 
     def groups(self):
-        net, cols = self.net, self.columns
+        net, cols = self.net, self.summed
         for bit in range(3, net.bits):
             inbox = self.extra.at[bit - 3]
             copy = net.copy(
@@ -666,14 +673,15 @@
             return rows_at(start + net.bit(order[1]) * count, count, count)
         return rows_at(start, 2 * count, count)
 
-    def owned(self):
+    def owned(self, apart=True):
         net, fin = self.net, self.fin_columns
         count = self.sndz.shape[0] // 2
-        net.arrived((self.name, 7), OWNERS, self.rcvz.at[:, :, fin])
+        if apart:
+            net.arrived((self.name, 7), OWNERS, self.rcvz.at[:, :, fin])
         for half in range(2):
             part = slice(half * count, (half + 1) * count)
             total = self.sndz[part, self.slots(0)].astype(F32)
-            for s in range(1, self.heads):
+            for s in range(1, self.heads if apart else 1):
                 total = total + self.rcvz[s - 1, part, fin].astype(F32)
             rows = self.place(half, 0)
             self.fin[rows, fin] = total.astype(BF16)
@@ -709,6 +717,64 @@
         ]
 
 
+class ReduceFirst(Reduce):
+    def __init__(self, net, refs, name, first, width, place):
+        super().__init__(net, refs, name, first, width)
+        self.summed = self.slots(0)
+        self.inbox = slice(place * width, (place + 1) * width)
+
+    def scatter(self):
+        net = self.net
+        net.arrived((self.name, 4), HALVES, self.rcv0.at[:, self.columns])
+        for s in range(1, self.heads):
+            cols = self.slots(s)
+            self.sndf[s - 1, :, self.inbox] = (
+                self.own[:, cols].astype(F32) + self.rcv0[:, cols].astype(F32)
+            ).astype(BF16)
+            net.send(
+                (self.name, 7),
+                FIRST,
+                self.sndf.at[s - 1, :, self.inbox],
+                self.rcvf.at[s - 1, :, self.inbox],
+                net.beside(s),
+            )
+
+    def gathered(self):
+        net, cols = self.net, self.summed
+        net.arrived((self.name, 7), FIRST, self.rcvf.at[:, :, self.inbox])
+        part = self.own.shape[0] // 4
+        for stays in (False, True):
+            for half in range(2):
+                bit = net.bit(self.ORDERS[half][0])
+                rows = rows_at((2 * half + (bit if stays else 1 - bit)) * part, part, 32)
+                total = self.own[rows, cols].astype(F32) + self.rcv0[rows, cols].astype(F32)
+                for s in range(1, self.heads):
+                    total = total + self.rcvf[s - 1, rows, self.inbox].astype(F32)
+                if stays:
+                    self.own[rows, cols] = total.astype(BF16)
+                else:
+                    place = slice(half * part, (half + 1) * part)
+                    self.snd1[place, cols] = total.astype(BF16)
+                    net.send(
+                        (self.name, 5),
+                        QUARTERS,
+                        self.snd1.at[place, cols],
+                        self.rcv1.at[place, cols],
+                        net.across(self.ORDERS[half][0]),
+                    )
+
+    def steps(self):
+        return [
+            self.scatter,
+            self.gathered,
+            lambda: self.halving(1),
+            lambda: (self.halving(2), self.groups(), self.owned(False)),
+            lambda: self.spread(0),
+            lambda: self.spread(1),
+            lambda: self.spread(2),
+        ]
+
+
 class Total:
     def __init__(self, net, small, core_in, plane, more, across):
         self.net, self.small, self.core_in = net, small, core_in
@@ -729,7 +795,7 @@
     def chips(self):
         net = self.net
         net.arrived(PLANE, PLANE, self.plane.at[0:3])
-        total = self.summed(self.plane, 4)
+        total = self.added(self.plane, 4)
         for bit in range(3, net.bits):
             mine, theirs = self.more.at[2 * (bit - 3)], self.more.at[2 * (bit - 3) + 1]
             mine[...] = total.astype(BF16)
@@ -745,9 +811,9 @@
     def done(self):
         net = self.net
         net.arrived(HEADS, HEADS, self.heads.at[1 : net.heads])
-        return self.summed(self.heads, net.heads)
-
-    def summed(self, ref, count):
+        return self.added(self.heads, net.heads)
+
+    def added(self, ref, count):
         total = ref[0].astype(F32)
         for i in range(1, count):
             total = total + ref[i].astype(F32)
@@ -764,16 +830,17 @@
 
 CHUNKS = 10
 Q, K, V, O, G1, G2, U1, U2, D1, D2 = range(CHUNKS)
+EARLY = (D1, D2)
 ORDER = (
-    0, 46, 60, 74, 88, 1, 2, 3, 4, 5, 6, 7, 47, 102, 61, 130, 75, 116, 48, 89, 144, 62, 103, 158,
-    76, 49, 131, 172, 90, 50, 117, 63, 104, 64, 145, 77, 132, 159, 78, 8, 91, 118, 173, 9, 92, 105,
-    146, 10, 106, 133, 11, 160, 134, 119, 174, 120, 147, 148, 12, 161, 13, 162, 175, 14, 176, 15,
-    16, 17, 18, 19, 38, 163, 177, 164, 178, 39, 20, 165, 179, 21, 22, 23, 107, 121, 135, 149, 108,
-    122, 136, 150, 24, 109, 166, 123, 137, 151, 25, 180, 26, 27, 40, 110, 93, 94, 41, 167, 28, 95,
-    124, 29, 30, 138, 31, 51, 65, 79, 52, 152, 66, 80, 32, 168, 181, 111, 53, 67, 81, 33, 96, 34,
-    125, 139, 35, 169, 153, 42, 182, 54, 36, 43, 112, 37, 68, 126, 82, 97, 170, 183, 140, 55, 171,
-    154, 113, 44, 69, 127, 83, 98, 184, 141, 155, 114, 185, 56, 128, 115, 99, 129, 142, 156, 57,
-    143, 157, 45, 100, 70, 101, 58, 84, 59, 71, 85, 72, 73, 86, 87,
+    1, 2, 4, 5, 6, 7, 0, 42, 56, 70, 84, 3, 43, 98, 57, 126, 71, 112, 44, 85, 140, 58, 99, 154, 72,
+    45, 127, 168, 86, 46, 113, 59, 100, 60, 141, 73, 128, 155, 74, 8, 87, 169, 114, 9, 101, 88,
+    142, 10, 102, 129, 156, 11, 170, 130, 115, 143, 116, 157, 144, 12, 13, 14, 171, 158, 15, 172,
+    16, 17, 18, 19, 159, 173, 160, 174, 20, 21, 161, 22, 23, 103, 117, 175, 131, 145, 104, 118,
+    132, 105, 146, 119, 24, 133, 25, 147, 26, 27, 106, 89, 90, 28, 120, 29, 91, 134, 30, 31, 47,
+    148, 61, 75, 107, 48, 62, 76, 121, 49, 32, 77, 92, 63, 33, 135, 34, 50, 176, 108, 162, 149, 35,
+    78, 122, 38, 93, 36, 64, 136, 39, 37, 51, 177, 109, 150, 163, 79, 123, 65, 137, 94, 178, 40,
+    110, 151, 52, 164, 124, 138, 95, 111, 80, 125, 139, 179, 66, 152, 53, 165, 153, 81, 96, 180,
+    97, 67, 54, 181, 166, 41, 55, 82, 167, 83, 68, 69,
 )
 
 
@@ -785,10 +852,10 @@
 
 
 def layer_kernel(groups, heads, names, *refs):
-    count = len(refs) - len(names) - 3
+    count = len(refs) - len(names) - 4
     named = inputs(*refs[:count])
     named.update(zip(names, refs[count:]))
-    send_sems, recv_sems, out_sem = refs[-3:]
+    send_sems, recv_sems, local_sems, out_sem = refs[-4:]
     layer = Layer(slots=heads, **named)
     weights, dgu, fin = layer.weights, layer.dgu, layer.fin
     width = layer.wq_in.shape[1]
@@ -803,21 +870,36 @@
     net = Net(groups, heads, send_sems, recv_sems)
     left, right = layer.left_t, layer.right_t
 
-    def own():
-        for chunk, ref in ((Q, layer.wq_in), (K, layer.wk_in), (V, layer.wv_in)):
-            weights[:, chunk * block : chunk * block + width] = ref[...]
-        weights[:, O * block : O * block + width] = layer.wo_in[...].T
-        for i in range(layer.wg_in.shape[1] // width):
-            cols = slice(i * width, (i + 1) * width)
-            for chunk, part in (
-                (G1 + i, layer.wg_in[:, cols]),
-                (U1 + i, layer.wu_in[:, cols]),
-                (D1 + i, layer.wd_in[cols, :].T),
-            ):
-                weights[:, chunk * block : chunk * block + width] = part
+    def place(chunk):
+        return weights.at[:, chunk * block : chunk * block + width]
+
+    def fetch(index, source, target):
+        return pltpu.make_async_copy(source, target, local_sems.at[index])
+
+    fetches = [
+        fetch(0, layer.wq_in, place(Q)),
+        fetch(1, layer.wk_in, place(K)),
+        fetch(2, layer.wv_in, place(V)),
+        fetch(3, layer.wo_in, layer.wo_raw),
+    ]
+    for i, (source, chunk) in enumerate(
+        ((layer.wg_in, G1), (layer.wg_in, G2), (layer.wu_in, U1), (layer.wu_in, U2))
+    ):
+        cols = slice(i % 2 * width, (i % 2 + 1) * width)
+        fetches.append(fetch(4 + i, source.at[:, cols], place(chunk)))
+    fetches.append(fetch(8, layer.wd_in, layer.wd_raw))
+
+    def ready(chunk):
+        if chunk != D2:
+            fetches[chunk].wait()
+        if chunk == O:
+            place(O)[...] = layer.wo_raw[...].T
+        if chunk >= D1:
+            first = (chunk - D1) * width
+            place(chunk)[...] = layer.wd_raw[first : first + width, :].T
+
+    def greet():
         layer.own_table()
-
-    def greet():
         net.greet_end()
         for t in range(1, heads):
             net.send(TABLE, TABLE, layer.tab.at[0], layer.tab.at[heads - t], net.beside(t))
@@ -825,9 +907,6 @@
     def offsets():
         net.arrived(TABLE, TABLE, layer.tab.at[1:heads])
         loop(heads, layer.offsets)
-
-    def turn(target, source):
-        target[...] = source[...].T
 
     def sums():
         layer.sums[...] = total.done()
@@ -853,10 +932,6 @@
     tasks += [
         lambda: loop(tiles, layer.outputs),
         layer.finish,
-        lambda: turn(right, layer.d_end_low),
-        lambda: turn(left, layer.ff_in),
-        lambda: turn(right, layer.d_mid_low),
-        lambda: turn(left, layer.attn_in),
         lambda: (layer.small_grads(net.head), total.start()),
         total.cores,
         total.chips,
@@ -867,9 +942,12 @@
     named.update(out_sem=out_sem)
     for chunk, (turned, source, i) in enumerate(sources):
         gather = Gather(net, weights, chunk, chunk * block, width)
-        reduce = Reduce(net, named, chunk, chunk * block, width)
+        if chunk in EARLY:
+            reduce = ReduceFirst(net, named, chunk, chunk * block, width, EARLY.index(chunk))
+        else:
+            reduce = Reduce(net, named, chunk, chunk * block, width)
         source = source.at[:, i * block : (i + 1) * block]
-        tasks += [gather.start] + [functools.partial(gather.step, level) for level in range(4)]
+        tasks += [functools.partial(gather.start, functools.partial(ready, chunk))] + [functools.partial(gather.step, level) for level in range(4)]
         tasks += [
             functools.partial(reduce.partner, turned, source),
             functools.partial(reduce.mine, turned, source),
@@ -877,17 +955,21 @@
         tasks += reduce.steps()
 
     net.greet_start()
-    own()
-    for place in ORDER:
-        tasks[place]()
+    for one in fetches:
+        one.start()
+    for step in ORDER:
+        tasks[step]()
     slots = heads - 1
     pltpu.make_async_copy(fin, layer.fin_out, out_sem).wait()
     net.sent(TABLE, layer.tab.at[1:heads])
     net.sent(WEIGHTS, weights.at[:, 0 : slots * fin.shape[1]])
     net.sent(HALVES, layer.snd0)
-    net.sent(QUARTERS, layer.snd1)
-    net.sent(EIGHTHS, layer.snd2)
-    net.sent(OWNERS, layer.sndz.at[:, 0 : slots * fin.shape[1]])
+    net.sent(FIRST, layer.sndf)
+    late = CHUNKS - len(EARLY)
+    count = (late * heads + len(EARLY)) * width
+    net.sent(QUARTERS, layer.snd1.at[:, 0:count])
+    net.sent(EIGHTHS, layer.snd2.at[:, 0:count])
+    net.sent(OWNERS, layer.sndz.at[:, 0 : slots * late * width])
     net.sent(FIN, fin.at[0 : fin.shape[0] * 7 // 8])
     net.sent(SMALL, layer.small)
     net.sent(PLANE, layer.plane.at[0:3])
@@ -966,7 +1048,9 @@
         sndz=((width // 8, total), BF16), rcvz=((heads - 1, width // 8, total // heads), BF16),
         fin=((width, total // heads), BF16), small=((32, width), F32), core_in=((32, width), F32),
         plane=((4, 32, width), BF16), heads_in=((heads, 32, width), BF16),
-        d_mid_low=((tokens, width), BF16),
+        sndf=((heads - 1, width // 2, len(EARLY) * part), BF16),
+        wo_raw=((part, width), BF16), wd_raw=((ff, width), BF16),
+        rcvf=((heads - 1, width // 2, len(EARLY) * part), BF16),
     )
     extra = bits - 3
     if extra > 0:
@@ -974,18 +1058,20 @@
             extra=((extra, width // 8, total), BF16), more=((2 * extra, 32, width), BF16)
         )
     copies = CHUNKS * (4 + 7 + extra) + 4 + extra + 1
-    sends = 10 + (CHUNKS + 1) * extra
+    sends = 11 + (CHUNKS + 1) * extra
     outs = [((rows, steps), F32), ((rows, steps), F32), ((32, width), F32), ((width, total // heads), BF16)]
     vmem = pl.BlockSpec(memory_space=pltpu.VMEM)
+    any_space = pl.BlockSpec(memory_space=pl.ANY)
     parts = pl.pallas_call(
         functools.partial(layer_kernel, groups, heads, list(scratch)),
         out_shape=[jax.ShapeDtypeStruct(*out) for out in outs],
-        in_specs=[vmem] * len(args),
-        out_specs=[vmem] * 3 + [pl.BlockSpec(memory_space=pl.ANY)],
+        in_specs=[any_space if i in (9, 10, 11, 12, 14, 15, 16) else vmem for i in range(len(args))],
+        out_specs=[vmem] * 3 + [any_space],
         scratch_shapes=[pltpu.VMEM(*v) for v in scratch.values()]
         + [
             pltpu.SemaphoreType.DMA((sends,)),
             pltpu.SemaphoreType.DMA((copies,)),
+            pltpu.SemaphoreType.DMA((9,)),
             pltpu.SemaphoreType.DMA,
         ],
         compiler_params=pltpu.CompilerParams(

time: 90.2 us -> 85.8 us (0.951)
  Pallas kernels: 89.2 us -> 84.6 us
    pallas_call x1, Pallas kernels: 86.1 us -> 81.5 us  [layer_call(): pl.pallas_call(functools.partial(layer_kernel, groups, heads, list(scratc...]
where the time goes in v5:
time: 85.8 us; the launch traced here: 85.4 us
  Pallas kernels  84.6 us (99%)
    pallas_call x1, Pallas kernels, layer_call(): pl.pallas_call(functools.partial(layer_kernel, groups, heads, list(scratc...  81.5 us
    pallas_call x1, Pallas kernels, layer_call(): pl.pallas_call(functools.partial(finish_kernel, heads), out_shape=[jax.Sh...  3.1 us

profile of v5, /device:TPU:0, one launch (start us, length us, event | category | flops | bytes accessed | tf_op | source)
XLA Modules:
  0.0 85.4 jit_solution(849904426526093107)
XLA Ops:
  0.7 81.5 %shard_map.314 = (f32[16,512]{1,0:T(8,128)}, f32[16,512]{1,0:T(8,128)}, f32[32,512]{1,0:T(8,128)}, bf16[512,1280]{1,0:T(8,128)(2,1)}) custom-call(f32[16,512]{1,0:T(8,128)} %refs_0_.1, s32[16,512]{1,0:T(8,128)} %refs_1_.1, s32[1,64]{1,0:T(1,128)} %bitcast.20, f32[16,512]{1,0:T(8,128)} %refs_3_.1, bf16[4,128]{1,0:T(4,128)(2,1)} %bitcast.16, ...), custom_call_target="tpu_custom_call" | custom-call | tf_op jit(solution)/shard_map/pallas_call | solution.py:1065
  82.2 3.1 %shard_map.315 = (f32[16,512]{1,0:T(8,128)}, f32[16,512]{1,0:T(8,128)}, f32[1,512]{1,0:T(1,128)}, f32[1,512]{1,0:T(1,128)}, f32[1,512]{1,0:T(1,128)}, /*index=5*...) custom-call(f32[16,512]{1,0:T(8,128)} %get-tuple-element.38.rebuilt,, ...), custom_call_target="tpu_custom_call" | custom-call | tf_op jit(solution)/shard_map/pallas_call | solution.py:1087

commit v6 on v5

--- a/solution.py
+++ b/solution.py
@@ -192,7 +192,13 @@
         lane = iota((1, 128), 1)
         return (lane < 64).astype(BF16), (lane >= 64).astype(BF16)
 
-    def attend(self, tile):
+    def project(self, at, i):
+        width = self.ctx.shape[1]
+        part = nn(self.attn_in[at, :], self.wq[:, i * width : (i + 1) * width]).astype(BF16)
+        self.qkv[at, i * width : (i + 1) * width] = part
+        return part
+
+    def weigh(self, tile):
         at = pl.ds(pl.multiple_of(tile * TILE, TILE), TILE)
         length = self.pm.shape[0]
         rows_tile = TILE // length
@@ -201,12 +207,7 @@
         shape = (length, 2 * length)
         block = (iota(shape, 0) // half != (iota(shape, 1) % length) // half).astype(F32) * -1e30
         splits = [self.splitb[pl.ds(tile * rows_tile + r, 1), :] * block for r in range(rows_tile)]
-        width = self.ctx.shape[1]
-        projected = []
-        for i in range(3):
-            part = nn(self.attn_in[at, :], self.wq[:, i * width : (i + 1) * width]).astype(BF16)
-            self.qkv[at, i * width : (i + 1) * width] = part
-            projected.append(part)
+        projected = [self.project(at, i) for i in range(2)]
         items = [(s, r) for s in range(self.slots) for r in range(rows_tile)]
 
         def piece(s, r, i):
@@ -217,7 +218,6 @@
             query = piece(s, r, 0)
             both = jnp.concatenate([query * even, query * odd], axis=0)
             scores.append(nt(piece(s, r, 1), both))
-        turned = []
         for (s, r), score in zip(items, scores):
             score = score + (self.bias[s] + splits[r])
             top = jnp.max(score, axis=0, keepdims=True)
@@ -226,9 +226,21 @@
             self.probs[
                 s, pl.ds(pl.multiple_of(tile * TILE + r * length, length), length), :
             ] = probs.astype(self.probs.dtype)
-            turned.append(probs.astype(BF16))
-        turned = [probs.T for probs in turned]
-        mixed = [nn(probs, piece(s, r, 2)) for probs, (s, r) in zip(turned, items)]
+
+    def mix(self, tile):
+        at = pl.ds(pl.multiple_of(tile * TILE, TILE), TILE)
+        length = self.pm.shape[0]
+        rows_tile = TILE // length
+        value = self.project(at, 2)
+        items = [(s, r) for s in range(self.slots) for r in range(rows_tile)]
+        turned = []
+        for s, r in items:
+            rows = pl.ds(pl.multiple_of(tile * TILE + r * length, length), length)
+            turned.append(self.probs[s, rows, :].astype(BF16).T)
+        mixed = [
+            nn(probs, value[r * length : (r + 1) * length, s * 128 : (s + 1) * 128])
+            for probs, (s, r) in zip(turned, items)
+        ]
         low_lanes = iota((1, 128), 1) < 64
         for s in range(self.slots):
             self.ctx[at, s * 128 : (s + 1) * 128] = jnp.concatenate(
@@ -239,17 +251,21 @@
                 axis=0,
             )
 
-    def middle_gate(self, tile):
+    def middle_in(self, tile):
         at = pl.ds(pl.multiple_of(tile * TILE, TILE), TILE)
         hidden_mid = self.embedded[at, :] + nt(self.ctx[at, :], self.wo[...])
         self.hidden_mid[at, :] = hidden_mid
         ff_in = (hidden_mid * row_scale(hidden_mid) * self.row_ff).astype(BF16)
         self.ff_in[at, :] = ff_in
         self.left_t[:, at] = ff_in.T
+
+    def middle_gate(self, which, tile):
+        at = pl.ds(pl.multiple_of(tile * TILE, TILE), TILE)
+        ff_in = self.ff_in[at, :]
         total = self.inner.shape[1]
         block = 256
         c = math.sqrt(2.0 / math.pi)
-        for first in range(0, total, block):
+        for first in range(which * total // 2, (which + 1) * total // 2, block):
             cols = slice(first, first + block)
             gate = nn(ff_in, self.wg[:, first : first + block])
             up = nn(ff_in, self.wg[:, total + first : total + first + block])
@@ -662,16 +678,15 @@
                 net.beside(s),
             )
 
-    def place(self, half, level):
+    def place(self, half):
         net = self.net
         quarter = self.fin.shape[0] // 4
         count = quarter // 4
         start = net.bit(0) * 2 * quarter + half * quarter
         order = self.ORDERS[half]
-        start = start + net.bit(order[0]) * 2 * count
-        if level == 0:
-            return rows_at(start + net.bit(order[1]) * count, count, count)
-        return rows_at(start, 2 * count, count)
+        return rows_at(
+            start + net.bit(order[0]) * 2 * count + net.bit(order[1]) * count, count, count
+        )
 
     def owned(self, apart=True):
         net, fin = self.net, self.fin_columns
@@ -683,24 +698,21 @@
             total = self.sndz[part, self.slots(0)].astype(F32)
             for s in range(1, self.heads if apart else 1):
                 total = total + self.rcvz[s - 1, part, fin].astype(F32)
-            rows = self.place(half, 0)
+            rows = self.place(half)
             self.fin[rows, fin] = total.astype(BF16)
             place = self.fin.at[rows, fin]
-            net.send((self.name, 8), FIN, place, place, net.across(self.ORDERS[half][1]))
+            for partner in net.plane():
+                net.send((self.name, 8), FIN, place, place, partner)
 
     def spread(self, level):
         net, fin = self.net, self.fin_columns
         rows = self.fin.shape[0]
-        count = (rows // 8, rows // 4, rows // 2)[level]
-        net.arrived((self.name, 8 + level), FIN, self.fin.at[0:count, fin])
         if level == 0:
-            for half in range(2):
-                place = self.fin.at[self.place(half, 1), fin]
-                net.send((self.name, 9), FIN, place, place, net.across(self.ORDERS[half][0]))
-        if level == 1:
+            net.arrived((self.name, 8), FIN, self.fin.at[0 : rows * 3 // 8, fin])
             place = self.fin.at[rows_at(net.bit(0) * (rows // 2), rows // 2, rows // 2), fin]
-            net.send((self.name, 10), FIN, place, place, net.across(0))
-        if level == 2:
+            net.send((self.name, 9), FIN, place, place, net.across(0))
+        else:
+            net.arrived((self.name, 9), FIN, self.fin.at[0 : rows // 2, fin])
             pltpu.make_async_copy(
                 self.fin.at[:, fin], self.fin_out.at[:, fin], self.out_sem
             ).start()
@@ -713,7 +725,6 @@
             self.owned,
             lambda: self.spread(0),
             lambda: self.spread(1),
-            lambda: self.spread(2),
         ]
 
 
@@ -771,7 +782,6 @@
             lambda: (self.halving(2), self.groups(), self.owned(False)),
             lambda: self.spread(0),
             lambda: self.spread(1),
-            lambda: self.spread(2),
         ]
 
 
@@ -832,15 +842,15 @@
 Q, K, V, O, G1, G2, U1, U2, D1, D2 = range(CHUNKS)
 EARLY = (D1, D2)
 ORDER = (
-    1, 2, 4, 5, 6, 7, 0, 42, 56, 70, 84, 3, 43, 98, 57, 126, 71, 112, 44, 85, 140, 58, 99, 154, 72,
-    45, 127, 168, 86, 46, 113, 59, 100, 60, 141, 73, 128, 155, 74, 8, 87, 169, 114, 9, 101, 88,
-    142, 10, 102, 129, 156, 11, 170, 130, 115, 143, 116, 157, 144, 12, 13, 14, 171, 158, 15, 172,
-    16, 17, 18, 19, 159, 173, 160, 174, 20, 21, 161, 22, 23, 103, 117, 175, 131, 145, 104, 118,
-    132, 105, 146, 119, 24, 133, 25, 147, 26, 27, 106, 89, 90, 28, 120, 29, 91, 134, 30, 31, 47,
-    148, 61, 75, 107, 48, 62, 76, 121, 49, 32, 77, 92, 63, 33, 135, 34, 50, 176, 108, 162, 149, 35,
-    78, 122, 38, 93, 36, 64, 136, 39, 37, 51, 177, 109, 150, 163, 79, 123, 65, 137, 94, 178, 40,
-    110, 151, 52, 164, 124, 138, 95, 111, 80, 125, 139, 179, 66, 152, 53, 165, 153, 81, 96, 180,
-    97, 67, 54, 181, 166, 41, 55, 82, 167, 83, 68, 69,
+    1, 2, 4, 5, 6, 7, 0, 54, 67, 3, 80, 93, 106, 132, 119, 145, 158, 171, 55, 68, 81, 56, 94, 69,
+    107, 82, 57, 133, 95, 58, 70, 120, 108, 71, 8, 146, 134, 83, 9, 96, 159, 10, 84, 121, 172, 97,
+    11, 147, 12, 13, 135, 14, 160, 109, 15, 136, 16, 17, 110, 173, 122, 18, 19, 20, 21, 148, 22,
+    161, 123, 23, 149, 24, 162, 174, 25, 26, 27, 175, 28, 29, 30, 31, 163, 176, 164, 177, 32, 165,
+    33, 34, 35, 111, 124, 137, 150, 112, 125, 138, 113, 151, 126, 36, 152, 37, 38, 114, 139, 39,
+    127, 98, 166, 99, 178, 40, 100, 41, 115, 153, 42, 43, 59, 72, 128, 140, 85, 167, 60, 73, 86,
+    101, 61, 44, 74, 154, 87, 45, 141, 102, 46, 62, 168, 179, 47, 75, 116, 50, 88, 48, 63, 51, 155,
+    49, 180, 169, 142, 129, 76, 170, 103, 117, 89, 118, 64, 52, 181, 156, 77, 143, 157, 130, 90,
+    144, 104, 131, 65, 105, 182, 66, 78, 183, 91, 79, 53, 92,
 )
 
 
@@ -920,8 +930,11 @@
     ]
     for body in (
         layer.cotangent,
-        layer.attend,
-        layer.middle_gate,
+        layer.weigh,
+        layer.mix,
+        layer.middle_in,
+        functools.partial(layer.middle_gate, 0),
+        functools.partial(layer.middle_gate, 1),
         layer.middle_down,
         layer.inner_back,
         layer.middle_back,
@@ -1057,7 +1070,7 @@
         scratch.update(
             extra=((extra, width // 8, total), BF16), more=((2 * extra, 32, width), BF16)
         )
-    copies = CHUNKS * (4 + 7 + extra) + 4 + extra + 1
+    copies = CHUNKS * (4 + 6 + extra) + 4 + extra + 1
     sends = 11 + (CHUNKS + 1) * extra
     outs = [((rows, steps), F32), ((rows, steps), F32), ((32, width), F32), ((width, total // heads), BF16)]
     vmem = pl.BlockSpec(memory_space=pltpu.VMEM)

time: 85.8 us -> 83 us (0.967)
  Pallas kernels: 84.6 us -> 81.5 us
    pallas_call x1, Pallas kernels: 81.5 us -> 78.4 us  [layer_call(): pl.pallas_call(functools.partial(layer_kernel, groups, heads, list(scratc...]
where the time goes in v6:
time: 83 us; the launch traced here: 82.3 us
  Pallas kernels  81.5 us (98%)
    pallas_call x1, Pallas kernels, layer_call(): pl.pallas_call(functools.partial(layer_kernel, groups, heads, list(scratc...  78.4 us
    pallas_call x1, Pallas kernels, layer_call(): pl.pallas_call(functools.partial(finish_kernel, heads), out_shape=[jax.Sh...  3.1 us

profile of v6, /device:TPU:0, one launch (start us, length us, event | category | flops | bytes accessed | tf_op | source)
XLA Modules:
  0.0 82.3 jit_solution(16010181311983550322)
XLA Ops:
  0.7 78.4 %shard_map.314 = (f32[16,512]{1,0:T(8,128)}, f32[16,512]{1,0:T(8,128)}, f32[32,512]{1,0:T(8,128)}, bf16[512,1280]{1,0:T(8,128)(2,1)}) custom-call(f32[16,512]{1,0:T(8,128)} %refs_0_.1, s32[16,512]{1,0:T(8,128)} %refs_1_.1, s32[1,64]{1,0:T(1,128)} %bitcast.20, f32[16,512]{1,0:T(8,128)} %refs_3_.1, bf16[4,128]{1,0:T(4,128)(2,1)} %bitcast.16, ...), custom_call_target="tpu_custom_call" | custom-call | tf_op jit(solution)/shard_map/pallas_call | solution.py:1078
  79.1 3.1 %shard_map.315 = (f32[16,512]{1,0:T(8,128)}, f32[16,512]{1,0:T(8,128)}, f32[1,512]{1,0:T(1,128)}, f32[1,512]{1,0:T(1,128)}, f32[1,512]{1,0:T(1,128)}, /*index=5*...) custom-call(f32[16,512]{1,0:T(8,128)} %get-tuple-element.38.rebuilt,, ...), custom_call_target="tpu_custom_call" | custom-call | tf_op jit(solution)/shard_map/pallas_call | solution.py:1100

commit v7 on v6

--- a/solution.py
+++ b/solution.py
@@ -524,6 +524,10 @@
     return pl.ds(pl.multiple_of(start, unit), count)
 
 
+def far_first(heads):
+    return sorted(range(1, heads), key=lambda t: -min(t, heads - t))
+
+
 class Gather:
     ORDERS = ((1, 2, 0), (2, 1, 0))
 
@@ -548,7 +552,7 @@
         ready()
         for half in range(2):
             rows = self.span(half, 0)
-            for t in range(1, self.heads):
+            for t in far_first(self.heads):
                 slot = self.heads - t
                 net.send(
                     (self.name, 0),
@@ -669,7 +673,7 @@
 
     def owners(self):
         net = self.net
-        for s in range(1, self.heads):
+        for s in far_first(self.heads):
             net.send(
                 (self.name, 7),
                 OWNERS,

time: 83 us -> 82.9 us (level)
  no operation moved by 1% of the time
where the time goes in v7:
time: 82.9 us; the launch traced here: 82.3 us
  Pallas kernels  81.5 us (98%)
    pallas_call x1, Pallas kernels, layer_call(): pl.pallas_call(functools.partial(layer_kernel, groups, heads, list(scratc...  78.4 us
    pallas_call x1, Pallas kernels, layer_call(): pl.pallas_call(functools.partial(finish_kernel, heads), out_shape=[jax.Sh...  3.1 us

profile of v7, /device:TPU:0, one launch (start us, length us, event | category | flops | bytes accessed | tf_op | source)
XLA Modules:
  0.0 82.3 jit_solution(5525094209567488589)
XLA Ops:
  0.7 78.4 %shard_map.314 = (f32[16,512]{1,0:T(8,128)}, f32[16,512]{1,0:T(8,128)}, f32[32,512]{1,0:T(8,128)}, bf16[512,1280]{1,0:T(8,128)(2,1)}) custom-call(f32[16,512]{1,0:T(8,128)} %refs_0_.1, s32[16,512]{1,0:T(8,128)} %refs_1_.1, s32[1,64]{1,0:T(1,128)} %bitcast.20, f32[16,512]{1,0:T(8,128)} %refs_3_.1, bf16[4,128]{1,0:T(4,128)(2,1)} %bitcast.16, ...), custom_call_target="tpu_custom_call" | custom-call | tf_op jit(solution)/shard_map/pallas_call | solution.py:1082
  79.1 3.1 %shard_map.315 = (f32[16,512]{1,0:T(8,128)}, f32[16,512]{1,0:T(8,128)}, f32[1,512]{1,0:T(1,128)}, f32[1,512]{1,0:T(1,128)}, f32[1,512]{1,0:T(1,128)}, /*index=5*...) custom-call(f32[16,512]{1,0:T(8,128)} %get-tuple-element.38.rebuilt,, ...), custom_call_target="tpu_custom_call" | custom-call | tf_op jit(solution)/shard_map/pallas_call | solution.py:1104
